TPU v7x, 32 devices: a whole 2x2x4 slice. The times are simulated.
32 devices in a mesh: chan: 4 (over y, x), uv: 8 (over z, core).
Axes of the slice: x: 2, y: 2, z: 4, core: 2. Of those that a mesh axis runs over, the one named last changes fastest.
Arguments:
- visibilities: bfloat16 [16384, 2, 512], P('uv', None, 'chan'), may hold values from -3 to 3
- pair_patch_number: int32 [16384, 1], P('uv'), may hold values from 0 to 7; in each aligned block of 2048 rows (0 to 2047, 2048 to 4095, ...) at most 512 rows name the same one
- baseline_kernel_taps: bfloat16 [16384, 16], P('uv'), may hold values from 0.099609375 to 1
- kernel_start_cells: int32 [16384, 2], P('uv'), may hold values from 0 to 24
Outputs:
- spectra: float32 [8, 1024, 2, 512], P('uv', 'chan')
Inputs may be any that keep to these rules, and one draw needn't show every extreme that they name: `pair_patch_number`: in each aligned block of 2048 baselines (the baselines of one index of uv) no subgrid is named more than 512 times, a bound that some block reaches.
All inputs are finite; a program needn't handle non-finite values.
Results may differ from a plain program's by a relative error of at most 0.004.
Values may be sent and summed in bfloat16 or wider, within the bound.
No kernel may reach another device: no remote copies, remote signals or barrier semaphores. Data moves between devices by JAX's collectives and lax.ppermute only.
A program may use at most 64 MiB of HBM per device.

v0:
```python
import math

import jax
import jax.numpy as jnp
from jax import lax
from jax.sharding import PartitionSpec as P

SUBGRID_SIDE = 32
KERNEL_TAPS = 8


def kernel_rows(taps_float, offsets_float, cells_side):
    cell_index = jnp.arange(cells_side, dtype=jnp.float32)
    tap_index = jnp.arange(KERNEL_TAPS, dtype=jnp.float32)

    def one_axis(tap_values, opening_pixel):
        matches = (
            cell_index[None, None, :] == opening_pixel[:, None, None] + tap_index[None, :, None]
        ).astype(jnp.float32)
        return jnp.sum(tap_values[:, :, None] * matches, axis=1)

    return (
        one_axis(taps_float[:, :KERNEL_TAPS], offsets_float[:, 0]),
        one_axis(taps_float[:, KERNEL_TAPS : 2 * KERNEL_TAPS], offsets_float[:, 1]),
    )


def angle_table(row_count, col_count, period):
    row_ids = jnp.arange(row_count, dtype=jnp.int32)[:, None]
    col_ids = jnp.arange(col_count, dtype=jnp.int32)[None, :]
    angles = (row_ids * col_ids % period).astype(jnp.float32) * (2.0 * math.pi / period)
    return (jnp.cos(angles), jnp.sin(angles))


def delay_transform(pencil_data):
    leading, cell_count, parts_count, length = pencil_data.shape
    inner_len = 128
    outer_len = length // inner_len
    fine = lax.Precision.HIGH
    wide = jnp.float32
    values = pencil_data.reshape(leading * cell_count, parts_count, outer_len, inner_len)
    real_part = values[:, 0]
    imag_part = values[:, 1]
    cos_outer, sin_outer = angle_table(outer_len, outer_len, outer_len)
    first_real = jnp.einsum(
        "kn,mnj->mkj", cos_outer, real_part, precision=fine, preferred_element_type=wide
    ) + jnp.einsum("kn,mnj->mkj", sin_outer, imag_part, precision=fine, preferred_element_type=wide)
    first_imag = jnp.einsum(
        "kn,mnj->mkj", cos_outer, imag_part, precision=fine, preferred_element_type=wide
    ) - jnp.einsum("kn,mnj->mkj", sin_outer, real_part, precision=fine, preferred_element_type=wide)
    cos_twist, sin_twist = angle_table(outer_len, inner_len, length)
    twisted_real = first_real * cos_twist + first_imag * sin_twist
    twisted_imag = first_imag * cos_twist - first_real * sin_twist
    cos_inner, sin_inner = angle_table(inner_len, inner_len, inner_len)
    final_real = jnp.einsum("mkn,nq->mqk", twisted_real, cos_inner, precision=fine) + jnp.einsum(
        "mkn,nq->mqk", twisted_imag, sin_inner, precision=fine
    )
    final_imag = jnp.einsum("mkn,nq->mqk", twisted_imag, cos_inner, precision=fine) - jnp.einsum(
        "mkn,nq->mqk", twisted_real, sin_inner, precision=fine
    )
    scaling = 1.0 / math.sqrt(length)
    stacked = (
        jnp.stack([final_real.reshape(-1, length), final_imag.reshape(-1, length)], axis=1)
        * scaling
    )
    return stacked.reshape(leading, cell_count, parts_count, length)


def on_device(visibilities, pair_patch_number, baseline_kernel_taps, kernel_start_cells):
    rows_here, parts_count, frequency_bins = visibilities.shape
    uv_devices = lax.axis_size("uv")
    capacity = 2 * rows_here // uv_devices
    slot_count = uv_devices * capacity
    flat_layout = visibilities.reshape(rows_here, parts_count * frequency_bins)
    subgrid_list = pair_patch_number[:, 0]
    member = (subgrid_list[:, None] == jnp.arange(uv_devices, dtype=jnp.int32)[None, :]).astype(
        jnp.int32
    )
    preceding = jnp.sum((jnp.cumsum(member, axis=0) - member) * member, axis=1)
    target = subgrid_list * capacity + preceding
    vis_buffer = (
        jnp.zeros((slot_count, parts_count * frequency_bins), jnp.bfloat16)
        .at[target]
        .set(flat_layout)
    )
    vis_buffer = vis_buffer.reshape(uv_devices, capacity, parts_count * frequency_bins)
    u_rows, v_rows = kernel_rows(
        baseline_kernel_taps.astype(jnp.float32),
        kernel_start_cells.astype(jnp.float32),
        SUBGRID_SIDE,
    )
    payload = jnp.concatenate([u_rows, v_rows], axis=1).astype(jnp.bfloat16)
    payload_buffer = jnp.zeros((slot_count, 2 * SUBGRID_SIDE), jnp.bfloat16).at[target].set(payload)
    got_vis, got_payload = (
        lax.all_to_all(vis_buffer, "uv", split_axis=0, concat_axis=0, tiled=True),
        lax.all_to_all(
            payload_buffer.reshape(uv_devices, capacity, 2 * SUBGRID_SIDE),
            "uv",
            split_axis=0,
            concat_axis=0,
            tiled=True,
        ),
    )

    def kernels(payload_block):
        widened = payload_block.astype(jnp.float32)
        return (widened[:, :SUBGRID_SIDE], widened[:, SUBGRID_SIDE:])

    got_vis = got_vis.reshape(slot_count, parts_count * frequency_bins)
    got_payload = got_payload.reshape(slot_count, -1)
    stride = math.gcd(slot_count, 256)
    turn_count = slot_count // stride

    def accumulate(counter, accumulated):
        starting = counter * stride
        vis_block = lax.dynamic_slice_in_dim(got_vis, starting, stride, 0)
        payload_block = lax.dynamic_slice_in_dim(got_payload, starting, stride, 0)
        u_block, v_block = kernels(payload_block)
        weights = (
            (v_block[:, :, None] * u_block[:, None, :])
            .reshape(stride, SUBGRID_SIDE * SUBGRID_SIDE)
            .astype(jnp.bfloat16)
        )
        return accumulated + lax.dot_general(
            weights, vis_block, (((0,), (0,)), ((), ())), preferred_element_type=jnp.float32
        )

    gridded = lax.fori_loop(
        0,
        turn_count,
        accumulate,
        jnp.zeros((SUBGRID_SIDE * SUBGRID_SIDE, parts_count * frequency_bins), jnp.float32),
    )
    gridded = gridded.astype(jnp.bfloat16)
    chan_devices = lax.axis_size("chan")
    pieces = gridded.reshape(
        chan_devices, SUBGRID_SIDE * SUBGRID_SIDE // chan_devices, parts_count, frequency_bins
    )
    return delay_transform(lax.all_to_all(pieces, "chan", split_axis=0, concat_axis=3, tiled=True))


def solution(mesh):
    in_specs = (P("uv", None, "chan"), P("uv", None), P("uv", None), P("uv", None))
    out_specs = P("uv", "chan", None, None)
    return jax.shard_map(
        on_device, mesh=mesh, in_specs=in_specs, out_specs=out_specs, check_vma=False
    )
```

profile of v0, /device:TPU:0, one launch (start us, length us, event | category | flops | bytes accessed | tf_op | source)
XLA Modules:
  0.0 132.5 jit_solution(1215554758848807889)
XLA Ops:
  0.0 0.8 fusion.91
  0.8 0.7 convert_element_type.73
  1.6 0.4 select_reduce_fusion
  2.0 0.3 copy.57
  2.4 2.3 %reduce-window.6 = s32[8,16,128]{2,1,0:T(8,128)S(1)} reduce-window(s32[8,16,128]{2,1,0:T(8,128)S(1)} %fusion.33, s32[]{:T(128)} %constant.82.clone.1), window={size=1x1x128 pad=0_0x0_0x127_0}, to_apply=%region_0.0 | reduce-window | flops 2080768 | bytes 131076 | tf_op jit(solution)/shard_map/reduce-window
  4.6 0.3 slice_reduce_fusion
  4.9 0.2 reduce-window.9
  5.3 6.1 %scatter_custom_fusion = bf16[4096,64]{1,0:T(8,128)(2,1)S(1)} fusion(s32[2048]{0:T(1024)S(1)} %bitcast.106, bf16[2048,64]{1,0:T(8,128)(2,1)S(1)} %copy.57, bf16[]{:T(256)} %constant.87.clone.1), kind=kCustom, calls=%fused_computation.27 | custom fusion | bytes 524290 | tf_op jit(solution)/shard_map/scatter | solution.py:93
  11.4 1.1 copy.58
  12.5 6.3 %all-to-all-start = ((bf16[8,512,64]{1,2,0:T(8,128)(2,1)}), bf16[8,512,64]{1,2,0:T(8,128)(2,1)S(1)}, u32[]{:S(2)}, u32[]{:S(2)}) async-start(bf16[8,512,64]{1,2,0:T(8,128)(2,1)} %copy.58), calls=%async_computation | async-start | bytes 1048576 | tf_op jit(solution)/shard_map/all_to_all | solution.py:96
  18.8 11.2 %scatter_custom_fusion.1 = bf16[4096,256]{1,0:T(8,128)(2,1)} fusion(s32[2048]{0:T(1024)S(1)} %bitcast.107, bf16[256,8,2,128]{3,2,1,0:T(2,128)(2,1)S(1)} %bitcast.98, bf16[]{:T(256)} %constant.87.clone.1), kind=kCustom, calls=%fused_computation.19 | custom fusion | bytes 3145730 | tf_op jit(solution)/shard_map/scatter | solution.py:84
  30.0 4.2 %all-to-all-done = bf16[8,512,64]{1,2,0:T(8,128)(2,1)S(1)} async-done(((bf16[8,512,64]{1,2,0:T(8,128)(2,1)}), bf16[8,512,64]{1,2,0:T(8,128)(2,1)S(1)}, u32[]{:S(2)}, u32[]{:S(2)}) %all-to-all-start) | async-done | bytes 524320 | tf_op jit(solution)/shard_map/all_to_all | solution.py:96
  34.2 4.3 %all-to-all-start.1 = ((bf16[8,512,256]{2,1,0:T(8,128)(2,1)}), bf16[8,512,256]{2,1,0:T(8,128)(2,1)}, u32[]{:S(2)}, u32[]{:S(2)}) async-start(bf16[8,512,256]{2,1,0:T(8,128)(2,1)} %bitcast.9), calls=%async_computation.1 | async-start | bytes 4194304 | tf_op jit(solution)/shard_map/all_to_all | solution.py:95
  38.6 49.0 %all-to-all-done.1 = bf16[8,512,256]{2,1,0:T(8,128)(2,1)} async-done(((bf16[8,512,256]{2,1,0:T(8,128)(2,1)}), bf16[8,512,256]{2,1,0:T(8,128)(2,1)}, u32[]{:S(2)}, u32[]{:S(2)}) %all-to-all-start.1) | async-done | bytes 2097184 | tf_op jit(solution)/shard_map/all_to_all | solution.py:95
  87.6 24.7 %while.14 = (s32[]{:T(128)}, f32[1024,256]{1,0:T(8,128)S(1)}, bf16[4096,64]{0,1:T(8,128)(2,1)S(1)}, bf16[4096,256]{1,0:T(8,128)(2,1)}, s32[]{:T(128)}, /*index=5*/s32[]{:T(128)}, s32[]{:T(128)}, s32[]{:T(128)}) while((s32[]{:T(128)}, f32[1024,256]{1,0:T(8,128)S(1)}, bf16[4096,64]{0,1:T(8,128)(2,1)S(1)}, ...), condition=%wide.region_8.9_spmd.clone, body=%wide.region_7.8_spmd.clone.sunk | while | flops 135282688 | bytes 3571861 | solution.py:128
  87.6 0.1 multiply_convert_fusion.2
  87.7 1.3 %convolution_add_fusion.4 = f32[1024,256]{1,0:T(8,128)S(1)} fusion(bf16[256,1024]{0,1:T(8,128)(2,1)S(1)} %bitcast.91, f32[1024,256]{1,0:T(8,128)S(1)} %get-tuple-element.158, pred[]{:T(512)S(6)} %compare.11, bf16[4096,256]{1,0:T(8,128)(2,1)} %get-tuple-element.168, s32[]{:T(128)S(6)} %select_n.117), kind=kOutput, calls=%fused_computation.2.clone.1 | convolution fusion | flops 134742016 | bytes 2752517 | tf_op jit(solution)/shard_map/while/body/eval_jaxpr/dot_general | solution.py:124
  89.1 0.1 multiply_convert_fusion.2
  89.3 1.3 %convolution_add_fusion.4 = f32[1024,256]{1,0:T(8,128)S(1)} fusion(bf16[256,1024]{0,1:T(8,128)(2,1)S(1)} %bitcast.91, f32[1024,256]{1,0:T(8,128)S(1)} %get-tuple-element.158, pred[]{:T(512)S(6)} %compare.11, bf16[4096,256]{1,0:T(8,128)(2,1)} %get-tuple-element.168, s32[]{:T(128)S(6)} %select_n.117), kind=kOutput, calls=%fused_computation.2.clone.1 | convolution fusion | flops 134742016 | bytes 2752517 | tf_op jit(solution)/shard_map/while/body/eval_jaxpr/dot_general | solution.py:124
  90.7 0.1 multiply_convert_fusion.2
  90.8 1.3 %convolution_add_fusion.4 = f32[1024,256]{1,0:T(8,128)S(1)} fusion(bf16[256,1024]{0,1:T(8,128)(2,1)S(1)} %bitcast.91, f32[1024,256]{1,0:T(8,128)S(1)} %get-tuple-element.158, pred[]{:T(512)S(6)} %compare.11, bf16[4096,256]{1,0:T(8,128)(2,1)} %get-tuple-element.168, s32[]{:T(128)S(6)} %select_n.117), kind=kOutput, calls=%fused_computation.2.clone.1 | convolution fusion | flops 134742016 | bytes 2752517 | tf_op jit(solution)/shard_map/while/body/eval_jaxpr/dot_general | solution.py:124
  92.2 0.1 multiply_convert_fusion.2
  92.4 1.3 %convolution_add_fusion.4 = f32[1024,256]{1,0:T(8,128)S(1)} fusion(bf16[256,1024]{0,1:T(8,128)(2,1)S(1)} %bitcast.91, f32[1024,256]{1,0:T(8,128)S(1)} %get-tuple-element.158, pred[]{:T(512)S(6)} %compare.11, bf16[4096,256]{1,0:T(8,128)(2,1)} %get-tuple-element.168, s32[]{:T(128)S(6)} %select_n.117), kind=kOutput, calls=%fused_computation.2.clone.1 | convolution fusion | flops 134742016 | bytes 2752517 | tf_op jit(solution)/shard_map/while/body/eval_jaxpr/dot_general | solution.py:124
  93.8 0.1 multiply_convert_fusion.2
  93.9 1.3 %convolution_add_fusion.4 = f32[1024,256]{1,0:T(8,128)S(1)} fusion(bf16[256,1024]{0,1:T(8,128)(2,1)S(1)} %bitcast.91, f32[1024,256]{1,0:T(8,128)S(1)} %get-tuple-element.158, pred[]{:T(512)S(6)} %compare.11, bf16[4096,256]{1,0:T(8,128)(2,1)} %get-tuple-element.168, s32[]{:T(128)S(6)} %select_n.117), kind=kOutput, calls=%fused_computation.2.clone.1 | convolution fusion | flops 134742016 | bytes 2752517 | tf_op jit(solution)/shard_map/while/body/eval_jaxpr/dot_general | solution.py:124
  95.3 0.1 multiply_convert_fusion.2
  95.5 1.3 %convolution_add_fusion.4 = f32[1024,256]{1,0:T(8,128)S(1)} fusion(bf16[256,1024]{0,1:T(8,128)(2,1)S(1)} %bitcast.91, f32[1024,256]{1,0:T(8,128)S(1)} %get-tuple-element.158, pred[]{:T(512)S(6)} %compare.11, bf16[4096,256]{1,0:T(8,128)(2,1)} %get-tuple-element.168, s32[]{:T(128)S(6)} %select_n.117), kind=kOutput, calls=%fused_computation.2.clone.1 | convolution fusion | flops 134742016 | bytes 2752517 | tf_op jit(solution)/shard_map/while/body/eval_jaxpr/dot_general | solution.py:124
  96.9 0.1 multiply_convert_fusion.2
  97.0 1.3 %convolution_add_fusion.4 = f32[1024,256]{1,0:T(8,128)S(1)} fusion(bf16[256,1024]{0,1:T(8,128)(2,1)S(1)} %bitcast.91, f32[1024,256]{1,0:T(8,128)S(1)} %get-tuple-element.158, pred[]{:T(512)S(6)} %compare.11, bf16[4096,256]{1,0:T(8,128)(2,1)} %get-tuple-element.168, s32[]{:T(128)S(6)} %select_n.117), kind=kOutput, calls=%fused_computation.2.clone.1 | convolution fusion | flops 134742016 | bytes 2752517 | tf_op jit(solution)/shard_map/while/body/eval_jaxpr/dot_general | solution.py:124
  98.4 0.1 multiply_convert_fusion.2
  98.5 1.3 %convolution_add_fusion.4 = f32[1024,256]{1,0:T(8,128)S(1)} fusion(bf16[256,1024]{0,1:T(8,128)(2,1)S(1)} %bitcast.91, f32[1024,256]{1,0:T(8,128)S(1)} %get-tuple-element.158, pred[]{:T(512)S(6)} %compare.11, bf16[4096,256]{1,0:T(8,128)(2,1)} %get-tuple-element.168, s32[]{:T(128)S(6)} %select_n.117), kind=kOutput, calls=%fused_computation.2.clone.1 | convolution fusion | flops 134742016 | bytes 2752517 | tf_op jit(solution)/shard_map/while/body/eval_jaxpr/dot_general | solution.py:124
  100.0 0.1 multiply_convert_fusion.2
  100.1 1.3 %convolution_add_fusion.4 = f32[1024,256]{1,0:T(8,128)S(1)} fusion(bf16[256,1024]{0,1:T(8,128)(2,1)S(1)} %bitcast.91, f32[1024,256]{1,0:T(8,128)S(1)} %get-tuple-element.158, pred[]{:T(512)S(6)} %compare.11, bf16[4096,256]{1,0:T(8,128)(2,1)} %get-tuple-element.168, s32[]{:T(128)S(6)} %select_n.117), kind=kOutput, calls=%fused_computation.2.clone.1 | convolution fusion | flops 134742016 | bytes 2752517 | tf_op jit(solution)/shard_map/while/body/eval_jaxpr/dot_general | solution.py:124
  101.5 0.1 multiply_convert_fusion.2
  101.6 1.3 %convolution_add_fusion.4 = f32[1024,256]{1,0:T(8,128)S(1)} fusion(bf16[256,1024]{0,1:T(8,128)(2,1)S(1)} %bitcast.91, f32[1024,256]{1,0:T(8,128)S(1)} %get-tuple-element.158, pred[]{:T(512)S(6)} %compare.11, bf16[4096,256]{1,0:T(8,128)(2,1)} %get-tuple-element.168, s32[]{:T(128)S(6)} %select_n.117), kind=kOutput, calls=%fused_computation.2.clone.1 | convolution fusion | flops 134742016 | bytes 2752517 | tf_op jit(solution)/shard_map/while/body/eval_jaxpr/dot_general | solution.py:124
  103.0 0.1 multiply_convert_fusion.2
  103.2 1.3 %convolution_add_fusion.4 = f32[1024,256]{1,0:T(8,128)S(1)} fusion(bf16[256,1024]{0,1:T(8,128)(2,1)S(1)} %bitcast.91, f32[1024,256]{1,0:T(8,128)S(1)} %get-tuple-element.158, pred[]{:T(512)S(6)} %compare.11, bf16[4096,256]{1,0:T(8,128)(2,1)} %get-tuple-element.168, s32[]{:T(128)S(6)} %select_n.117), kind=kOutput, calls=%fused_computation.2.clone.1 | convolution fusion | flops 134742016 | bytes 2752517 | tf_op jit(solution)/shard_map/while/body/eval_jaxpr/dot_general | solution.py:124
  104.6 0.1 multiply_convert_fusion.2
  104.7 1.3 %convolution_add_fusion.4 = f32[1024,256]{1,0:T(8,128)S(1)} fusion(bf16[256,1024]{0,1:T(8,128)(2,1)S(1)} %bitcast.91, f32[1024,256]{1,0:T(8,128)S(1)} %get-tuple-element.158, pred[]{:T(512)S(6)} %compare.11, bf16[4096,256]{1,0:T(8,128)(2,1)} %get-tuple-element.168, s32[]{:T(128)S(6)} %select_n.117), kind=kOutput, calls=%fused_computation.2.clone.1 | convolution fusion | flops 134742016 | bytes 2752517 | tf_op jit(solution)/shard_map/while/body/eval_jaxpr/dot_general | solution.py:124
  106.1 0.1 multiply_convert_fusion.2
  106.3 1.3 %convolution_add_fusion.4 = f32[1024,256]{1,0:T(8,128)S(1)} fusion(bf16[256,1024]{0,1:T(8,128)(2,1)S(1)} %bitcast.91, f32[1024,256]{1,0:T(8,128)S(1)} %get-tuple-element.158, pred[]{:T(512)S(6)} %compare.11, bf16[4096,256]{1,0:T(8,128)(2,1)} %get-tuple-element.168, s32[]{:T(128)S(6)} %select_n.117), kind=kOutput, calls=%fused_computation.2.clone.1 | convolution fusion | flops 134742016 | bytes 2752517 | tf_op jit(solution)/shard_map/while/body/eval_jaxpr/dot_general | solution.py:124
  107.7 0.1 multiply_convert_fusion.2
  107.8 1.3 %convolution_add_fusion.4 = f32[1024,256]{1,0:T(8,128)S(1)} fusion(bf16[256,1024]{0,1:T(8,128)(2,1)S(1)} %bitcast.91, f32[1024,256]{1,0:T(8,128)S(1)} %get-tuple-element.158, pred[]{:T(512)S(6)} %compare.11, bf16[4096,256]{1,0:T(8,128)(2,1)} %get-tuple-element.168, s32[]{:T(128)S(6)} %select_n.117), kind=kOutput, calls=%fused_computation.2.clone.1 | convolution fusion | flops 134742016 | bytes 2752517 | tf_op jit(solution)/shard_map/while/body/eval_jaxpr/dot_general | solution.py:124
  109.2 0.1 multiply_convert_fusion.2
  109.4 1.3 %convolution_add_fusion.4 = f32[1024,256]{1,0:T(8,128)S(1)} fusion(bf16[256,1024]{0,1:T(8,128)(2,1)S(1)} %bitcast.91, f32[1024,256]{1,0:T(8,128)S(1)} %get-tuple-element.158, pred[]{:T(512)S(6)} %compare.11, bf16[4096,256]{1,0:T(8,128)(2,1)} %get-tuple-element.168, s32[]{:T(128)S(6)} %select_n.117), kind=kOutput, calls=%fused_computation.2.clone.1 | convolution fusion | flops 134742016 | bytes 2752517 | tf_op jit(solution)/shard_map/while/body/eval_jaxpr/dot_general | solution.py:124
  110.8 0.1 multiply_convert_fusion.2
  110.9 1.3 %convolution_add_fusion.4 = f32[1024,256]{1,0:T(8,128)S(1)} fusion(bf16[256,1024]{0,1:T(8,128)(2,1)S(1)} %bitcast.91, f32[1024,256]{1,0:T(8,128)S(1)} %get-tuple-element.158, pred[]{:T(512)S(6)} %compare.11, bf16[4096,256]{1,0:T(8,128)(2,1)} %get-tuple-element.168, s32[]{:T(128)S(6)} %select_n.117), kind=kOutput, calls=%fused_computation.2.clone.1 | convolution fusion | flops 134742016 | bytes 2752517 | tf_op jit(solution)/shard_map/while/body/eval_jaxpr/dot_general | solution.py:124
  112.5 0.9 copy.60
  113.3 3.7 %all-to-all-start.2 = ((bf16[4,256,2,128]{3,1,2,0:T(8,128)(2,1)}), bf16[4,256,2,128]{3,1,2,0:T(8,128)(2,1)S(1)}, u32[]{:S(2)}, u32[]{:S(2)}) async-start(bf16[4,256,2,128]{3,1,2,0:T(8,128)(2,1)} %copy.60), calls=%async_computation.2 | async-start | bytes 1048576 | tf_op jit(solution)/shard_map/all_to_all | solution.py:139
  117.1 7.8 %all-to-all-done.2 = bf16[4,256,2,128]{3,1,2,0:T(8,128)(2,1)S(1)} async-done(((bf16[4,256,2,128]{3,1,2,0:T(8,128)(2,1)}), bf16[4,256,2,128]{3,1,2,0:T(8,128)(2,1)S(1)}, u32[]{:S(2)}, u32[]{:S(2)}) %all-to-all-start.2) | async-done | bytes 524320 | tf_op jit(solution)/shard_map/all_to_all | solution.py:139
  124.9 0.4 copy.86
  125.3 0.5 fusion.18
  125.8 0.5 fusion.19
  126.2 0.5 fusion.2
  126.7 0.7 multiply_add_fusion
  127.4 0.6 fusion.16
  128.1 0.6 fusion.12
  128.7 0.6 fusion.5
  129.3 0.3 copy.64
  129.7 0.2 stack.7
  129.9 0.6 fusion.4
  130.5 0.3 copy.67
  130.9 0.2 stack.8
  131.2 1.3 copy.68
  (50 shorter events, 0.9 us)
Async XLA Ops:
  0.0 2.3 %copy-start.1 = (s32[2048,1]{0,1:T(1,128)S(1)}, s32[2048,1]{0,1:T(1,128)}, u32[]{:S(2)}) copy-start(s32[2048,1]{0,1:T(1,128)} %param.7) | copy-start | bytes 24580
  2.3 16.5 %copy-start = (bf16[2048,2,128]{2,1,0:T(2,128)(2,1)S(1)}, bf16[2048,2,128]{2,1,0:T(2,128)(2,1)}, u32[]{:S(2)}) copy-start(bf16[2048,2,128]{2,1,0:T(2,128)(2,1)} %param.6) | copy-start | bytes 3145732
  12.5 21.7 %all-to-all-start = ((bf16[8,512,64]{1,2,0:T(8,128)(2,1)}), bf16[8,512,64]{1,2,0:T(8,128)(2,1)S(1)}, u32[]{:S(2)}, u32[]{:S(2)}) async-start(bf16[8,512,64]{1,2,0:T(8,128)(2,1)} %copy.58), calls=%async_computation | async-start | bytes 1048576 | tf_op jit(solution)/shard_map/all_to_all | solution.py:96
  34.2 53.4 %all-to-all-start.1 = ((bf16[8,512,256]{2,1,0:T(8,128)(2,1)}), bf16[8,512,256]{2,1,0:T(8,128)(2,1)}, u32[]{:S(2)}, u32[]{:S(2)}) async-start(bf16[8,512,256]{2,1,0:T(8,128)(2,1)} %bitcast.9), calls=%async_computation.1 | async-start | bytes 4194304 | tf_op jit(solution)/shard_map/all_to_all | solution.py:95
  113.3 11.5 %all-to-all-start.2 = ((bf16[4,256,2,128]{3,1,2,0:T(8,128)(2,1)}), bf16[4,256,2,128]{3,1,2,0:T(8,128)(2,1)S(1)}, u32[]{:S(2)}, u32[]{:S(2)}) async-start(bf16[4,256,2,128]{3,1,2,0:T(8,128)(2,1)} %copy.60), calls=%async_computation.2 | async-start | bytes 1048576 | tf_op jit(solution)/shard_map/all_to_all | solution.py:139
where the time goes:
time: 133 us; the launch traced here: 132 us
  waiting for transfers between devices  61 us (46%)
  matrix products  26.1 us (20%)
  local copies, waits for them, and re-layouts  23.6 us (18%)
  starting transfers between devices  14.4 us (11%)
  other arithmetic  6.19 us (5%)
    all_to_all x1, waiting for transfers between devices, on_device(): lax.all_to_all(vis_buffer, 'uv', split_axis=0, concat_axis=0, tiled=True)  49 us
    dot_general x16, matrix products, accumulate(): lax.dot_general(weights, vis_block, (((0,), (0,)), ((), ())), preferred_e...  21.5 us
    scatter x1, local copies, waits for them, and re-layouts, on_device(): vis_buffer = jnp.zeros((slot_count, parts_count * frequency_bins), jnp.bf...  11.2 us
    all_to_all x1, waiting for transfers between devices, on_device(): lax.all_to_all(pieces, 'chan', split_axis=0, concat_axis=3, tiled=True)  7.78 us
    all_to_all x1, starting transfers between devices, on_device(): lax.all_to_all(payload_buffer.reshape(uv_devices, capacity, 2 * SUBGRID_S...  6.33 us
    scatter x1, local copies, waits for them, and re-layouts, on_device(): jnp.zeros((slot_count, 2 * SUBGRID_SIDE), jnp.bfloat16).at[target]  6.07 us
    all_to_all x1, starting transfers between devices, on_device(): lax.all_to_all(vis_buffer, 'uv', split_axis=0, concat_axis=0, tiled=True)  4.34 us
    all_to_all x1, waiting for transfers between devices, on_device(): lax.all_to_all(payload_buffer.reshape(uv_devices, capacity, 2 * SUBGRID_S...  4.2 us
  transfers between devices with their start and end apart: 3, of which 3 were waited for; matrix products, arithmetic and copies ran while one was open for 8% of the time, Pallas kernels for 0%

commit v1 on v0

--- a/solution.py
+++ b/solution.py
@@ -1,12 +1,218 @@
+import functools
 import math
 
 import jax
 import jax.numpy as jnp
+import numpy as np
 from jax import lax
+from jax.experimental import pallas as pl
+from jax.experimental.pallas import tpu as pltpu
 from jax.sharding import PartitionSpec as P
 
 SUBGRID_SIDE = 32
 KERNEL_TAPS = 8
+CELLS = SUBGRID_SIDE * SUBGRID_SIDE
+HALF = 256
+META = 24
+VMEM_LIMIT = 56 << 20
+
+
+def sort_kernel(order_ref, patch_ref, meta_ref, vis_ref, out_ref, rank_ref):
+    patch = patch_ref[...]
+    groups, lanes = patch.shape
+    uv_devices = 8
+
+    @pl.when(pl.program_id(0) == 0)
+    def _():
+        members = jnp.concatenate(
+            [(patch == s).astype(jnp.float32) for s in range(uv_devices)], axis=0
+        ).astype(jnp.bfloat16)
+        row = lax.broadcasted_iota(jnp.int32, (lanes, lanes), 0)
+        col = lax.broadcasted_iota(jnp.int32, (lanes, lanes), 1)
+        before = (row < col).astype(jnp.float32).astype(jnp.bfloat16)
+        ahead = jnp.dot(members, before, preferred_element_type=jnp.float32)
+        totals = jnp.dot(members, jnp.ones((lanes, lanes), jnp.bfloat16), preferred_element_type=jnp.float32)
+        count = uv_devices * groups
+        r = lax.broadcasted_iota(jnp.int32, (count, count), 0)
+        c = lax.broadcasted_iota(jnp.int32, (count, count), 1)
+        earlier = ((c < r) & (c // groups == r // groups)).astype(jnp.float32).astype(jnp.bfloat16)
+        rank_all = ahead + jnp.dot(earlier, totals.astype(jnp.bfloat16), preferred_element_type=jnp.float32)
+        rank = jnp.zeros((groups, lanes), jnp.float32)
+        for s in range(uv_devices):
+            rank = jnp.where(patch == s, rank_all[s * groups : (s + 1) * groups], rank)
+        rank_ref[...] = rank
+
+    s = order_ref[pl.program_id(0)]
+    rank = rank_ref[...]
+    slot = lax.broadcasted_iota(jnp.int32, (HALF, lanes), 0).astype(jnp.float32).astype(jnp.bfloat16)
+    slot = slot.reshape(HALF // 16, 16, lanes)
+    one = jnp.ones((), jnp.bfloat16)
+    zero = jnp.zeros((), jnp.bfloat16)
+    meta_parts = []
+    for h in range(2):
+        key = jnp.where(patch == s, rank - h * HALF, -1.0)
+        key = jnp.where(key < HALF, key, -1.0)
+        pieces = []
+        for k in range(groups):
+            k16 = jnp.broadcast_to(key[k : k + 1, :], (16, lanes)).astype(jnp.bfloat16)
+            pieces.append(jnp.where(slot == k16[None], one, zero).reshape(HALF, lanes))
+        select = jnp.concatenate(pieces, axis=1)
+        rows = jnp.dot(select, vis_ref[...], preferred_element_type=jnp.float32)
+        out_ref[0, h * HALF : (h + 1) * HALF, :] = rows.astype(jnp.bfloat16)
+        meta = lax.dot_general(
+            meta_ref[...], select, (((1,), (1,)), ((), ())), preferred_element_type=jnp.float32
+        )
+        meta_parts.append(meta[:META])
+    out_ref[0, 2 * HALF :, :] = jnp.concatenate(meta_parts, axis=0).astype(jnp.bfloat16)
+
+
+def sort_rows(order, patch, meta, vis):
+    count = order.shape[0]
+    return pl.pallas_call(
+        sort_kernel,
+        grid_spec=pltpu.PrefetchScalarGridSpec(
+            num_scalar_prefetch=1,
+            grid=(count,),
+            in_specs=[
+                pl.BlockSpec(patch.shape, lambda i, o: (0, 0)),
+                pl.BlockSpec(meta.shape, lambda i, o: (0, 0)),
+                pl.BlockSpec(vis.shape, lambda i, o: (0, 0)),
+            ],
+            out_specs=pl.BlockSpec((1, 2 * HALF + 2 * META, 256), lambda i, o: (i, 0, 0)),
+            scratch_shapes=[pltpu.VMEM(patch.shape, jnp.float32)],
+        ),
+        out_shape=jax.ShapeDtypeStruct((count, 2 * HALF + 2 * META, 256), jnp.bfloat16),
+        compiler_params=pltpu.CompilerParams(vmem_limit_bytes=VMEM_LIMIT),
+        name="sort_rows",
+    )(order, patch, meta, vis)
+
+
+def spread(taps, start):
+    cell = lax.broadcasted_iota(jnp.int32, (SUBGRID_SIDE, HALF), 0).astype(jnp.float32)
+    offset = cell - start
+    out = jnp.zeros((SUBGRID_SIDE, HALF), jnp.float32)
+    for i in range(KERNEL_TAPS):
+        out = jnp.where(offset == i, taps[i : i + 1, :], out)
+    return out
+
+
+def fill_weights(meta_block, weights_ref):
+    meta = meta_block.astype(jnp.float32)
+    for h in range(2):
+        part = meta[h * META : (h + 1) * META]
+        u = spread(part[:KERNEL_TAPS], part[16:17])
+        v = spread(part[KERNEL_TAPS : 2 * KERNEL_TAPS], part[17:18])
+        for y in range(SUBGRID_SIDE):
+            weights_ref[y * SUBGRID_SIDE : (y + 1) * SUBGRID_SIDE, h * HALF : (h + 1) * HALF] = (
+                v[y : y + 1, :] * u
+            ).astype(jnp.bfloat16)
+
+
+def grid_kernel(place_ref, rows_ref, out_ref, weights_ref, acc_ref):
+    step = pl.program_id(0)
+
+    @pl.when(step == 0)
+    def _():
+        acc_ref[...] = jnp.zeros_like(acc_ref)
+
+    fill_weights(rows_ref[0, 2 * HALF :, :], weights_ref)
+    acc_ref[...] += jnp.dot(
+        weights_ref[...], rows_ref[0, : 2 * HALF, :], preferred_element_type=jnp.float32
+    )
+
+    @pl.when(step == pl.num_programs(0) - 1)
+    def _():
+        part = CELLS // 4
+        for d in range(4):
+            begin = pl.multiple_of((place_ref[0] ^ d) * part, part)
+            out_ref[d] = acc_ref[pl.ds(begin, part), :].astype(jnp.bfloat16)
+
+
+def grid_rows(place, rows):
+    count = rows.shape[0]
+    return pl.pallas_call(
+        grid_kernel,
+        grid_spec=pltpu.PrefetchScalarGridSpec(
+            num_scalar_prefetch=1,
+            grid=(count,),
+            in_specs=[pl.BlockSpec((1,) + rows.shape[1:], lambda i, p: (i, 0, 0))],
+            out_specs=pl.BlockSpec((4, CELLS // 4, 256), lambda i, p: (0, 0, 0)),
+            scratch_shapes=[
+                pltpu.VMEM((CELLS, 2 * HALF), jnp.bfloat16),
+                pltpu.VMEM((CELLS, 256), jnp.float32),
+            ],
+        ),
+        out_shape=jax.ShapeDtypeStruct((4, CELLS // 4, 256), jnp.bfloat16),
+        compiler_params=pltpu.CompilerParams(vmem_limit_bytes=VMEM_LIMIT),
+        name="grid_rows",
+    )(place, rows)
+
+
+def transform_matrix(length, width):
+    n = np.arange(length)
+    angle = (n[:, None] * n[None, :] % length) * (2.0 * np.pi / length)
+    blocks = length // width
+    cos = (np.cos(angle) / math.sqrt(length)).reshape(blocks, width, length)
+    sin = (np.sin(angle) / math.sqrt(length)).reshape(blocks, width, length)
+    whole = np.concatenate([cos, sin], axis=1)
+    high = whole.astype(jnp.bfloat16)
+    low = (whole - high.astype(np.float64)).astype(jnp.bfloat16)
+    return high, low
+
+
+def transform_kernel(place_ref, x0_ref, x1_ref, x2_ref, x3_ref, high_ref, low_ref, out_ref):
+    real = imag = None
+    for d, ref in enumerate((x0_ref, x1_ref, x2_ref, x3_ref)):
+        block = place_ref[0] ^ d
+        x = ref[...]
+        width = x.shape[1] // 2
+        turned = jnp.concatenate([x[:, width:], -x[:, :width]], axis=1)
+        for matrix in (high_ref[block], low_ref[block]):
+            a = jnp.dot(x, matrix, preferred_element_type=jnp.float32)
+            b = jnp.dot(turned, matrix, preferred_element_type=jnp.float32)
+            real = a if real is None else real + a
+            imag = b if imag is None else imag + b
+    out_ref[:, 0, :] = real
+    out_ref[:, 1, :] = imag
+
+
+def transform(place, pieces, high, low):
+    cells = pieces[0].shape[0]
+    length = high.shape[2]
+    vmem = pl.BlockSpec(memory_space=pltpu.VMEM)
+    return pl.pallas_call(
+        transform_kernel,
+        in_specs=[pl.BlockSpec(memory_space=pltpu.SMEM)] + [vmem] * 6,
+        out_specs=vmem,
+        out_shape=jax.ShapeDtypeStruct((cells, 2, length), jnp.float32),
+        compiler_params=pltpu.CompilerParams(vmem_limit_bytes=VMEM_LIMIT),
+        name="transform",
+    )(place, *pieces, high, low)
+
+
+def on_device_small(visibilities, pair_patch_number, baseline_kernel_taps, kernel_start_cells):
+    rows_here, parts_count, channels = visibilities.shape
+    vis = visibilities.reshape(rows_here, parts_count * channels)
+    patch = pair_patch_number.reshape(rows_here // 128, 128)
+    meta = jnp.concatenate(
+        [
+            baseline_kernel_taps.T,
+            kernel_start_cells.astype(jnp.bfloat16).T,
+            jnp.zeros((14, rows_here), jnp.bfloat16),
+        ],
+        axis=0,
+    )
+    chan = lax.axis_index("chan")
+    place = chan.reshape(1).astype(jnp.int32)
+    order = jnp.arange(8, dtype=jnp.int32)
+    blocks = sort_rows(order, patch, meta, vis)
+    got = lax.all_to_all(blocks, "uv", split_axis=0, concat_axis=0, tiled=True)
+    gridded = grid_rows(place, got)
+    pieces = [gridded[0]]
+    for d in range(1, 4):
+        pieces.append(lax.ppermute(gridded[d], "chan", [(c, c ^ d) for c in range(4)]))
+    high, low = transform_matrix(4 * channels, channels)
+    return transform(place, pieces, jnp.asarray(high), jnp.asarray(low))[None]
 
 
 def kernel_rows(taps_float, offsets_float, cells_side):
@@ -66,7 +272,7 @@
     return stacked.reshape(leading, cell_count, parts_count, length)
 
 
-def on_device(visibilities, pair_patch_number, baseline_kernel_taps, kernel_start_cells):
+def on_device_large(visibilities, pair_patch_number, baseline_kernel_taps, kernel_start_cells):
     rows_here, parts_count, frequency_bins = visibilities.shape
     uv_devices = lax.axis_size("uv")
     capacity = 2 * rows_here // uv_devices
@@ -142,6 +348,11 @@
 def solution(mesh):
     in_specs = (P("uv", None, "chan"), P("uv", None), P("uv", None), P("uv", None))
     out_specs = P("uv", "chan", None, None)
+    small = mesh.shape["uv"] == 8 and mesh.shape["chan"] == 4
     return jax.shard_map(
-        on_device, mesh=mesh, in_specs=in_specs, out_specs=out_specs, check_vma=False
-    )
+        on_device_small if small else on_device_large,
+        mesh=mesh,
+        in_specs=in_specs,
+        out_specs=out_specs,
+        check_vma=False,
+    )

time: 133 us -> 102 us (0.77)
  matrix products: 26.1 us -> 0 us
  Pallas kernels: 0 us -> 24.3 us
  local copies, waits for them, and re-layouts: 23.6 us -> 6.73 us
  starting transfers between devices: 14.4 us -> 9.81 us
  other arithmetic: 6.19 us -> 2.29 us
  waiting for transfers between devices: 61 us -> 58.6 us
    dot_general x24 -> x0, matrix products: 26.1 us -> none  [the longest x16 21.5 us: accumulate(): lax.dot_general(weights, vis_block, (((0,), (0,)), ((), ())), preferred_e...]
    pallas_call x0 -> x3, Pallas kernels: none -> 24.3 us  [the longest x1 13 us: sort_rows(): pl.pallas_call(sort_kernel, grid_spec=pltpu.PrefetchScalarGridSpec(num_sc...]
    scatter x2 -> x0, local copies, waits for them, and re-layouts: 17.2 us -> none  [the longest x1 11.2 us: on_device(): vis_buffer = jnp.zeros((slot_count, parts_count * frequency_bins), jnp.bf...]
    all_to_all x3 -> x1, starting transfers between devices: 14.4 us -> 6.32 us  [on_device_small(): got = lax.all_to_all(blocks, 'uv', split_axis=0, concat_axis=0, tiled=True)]
    all_to_all x3 -> x1, waiting for transfers between devices: 61 us -> 53.3 us  [on_device_small(): got = lax.all_to_all(blocks, 'uv', split_axis=0, concat_axis=0, tiled=True)]
    ppermute x0 -> x3, waiting for transfers between devices: none -> 5.31 us  [on_device_small(): lax.ppermute(gridded[d], 'chan', [(c, c ^ d) for c in range(4)])]
    unnamed x4 -> x9, local copies, waits for them, and re-layouts: 0.01 us -> 4.38 us
    ppermute x0 -> x3, starting transfers between devices: none -> 3.49 us  [on_device_small(): lax.ppermute(gridded[d], 'chan', [(c, c ^ d) for c in range(4)])]
  transfers between devices with their start and end apart: 3 -> 4, of which waited for: 3 -> 4; matrix products, arithmetic and copies ran while one was open for 8% -> 0% of each run, Pallas kernels for 0% -> 0%
where the time goes in v1:
time: 102 us
  waiting for transfers between devices  58.6 us (57%)
  Pallas kernels  24.3 us (24%)
  starting transfers between devices  9.81 us (10%)
  local copies, waits for them, and re-layouts  6.73 us (7%)
  other arithmetic  2.29 us (2%)
    all_to_all x1, waiting for transfers between devices, on_device_small(): got = lax.all_to_all(blocks, 'uv', split_axis=0, concat_axis=0, tiled=True)  53.3 us
    pallas_call x1, Pallas kernels, sort_rows(): pl.pallas_call(sort_kernel, grid_spec=pltpu.PrefetchScalarGridSpec(num_sc...  13 us
    pallas_call x1, Pallas kernels, grid_rows(): pl.pallas_call(grid_kernel, grid_spec=pltpu.PrefetchScalarGridSpec(num_sc...  7.27 us
    all_to_all x1, starting transfers between devices, on_device_small(): got = lax.all_to_all(blocks, 'uv', split_axis=0, concat_axis=0, tiled=True)  6.32 us
    ppermute x3, waiting for transfers between devices, on_device_small(): lax.ppermute(gridded[d], 'chan', [(c, c ^ d) for c in range(4)])  5.31 us
    unnamed x9, local copies, waits for them, and re-layouts  4.38 us
    pallas_call x1, Pallas kernels, transform(): pl.pallas_call(transform_kernel, in_specs=[pl.BlockSpec(memory_space=pltp...  4.09 us
    ppermute x3, starting transfers between devices, on_device_small(): lax.ppermute(gridded[d], 'chan', [(c, c ^ d) for c in range(4)])  3.49 us
  transfers between devices with their start and end apart: 4, of which 4 were waited for; matrix products, arithmetic and copies ran while one was open for 0% of the time, Pallas kernels for 0%

profile of v1, /device:TPU:0, one launch (start us, length us, event | category | flops | bytes accessed | tf_op | source)
XLA Modules:
  0.0 101.8 jit_solution(15534591670328616830)
XLA Ops:
  0.0 0.7 convert_bitcast_fusion
  0.7 2.3 %copy.9 = bf16[256,8,2,128]{3,1,2,0:T(8,128)(2,1)} copy(bf16[256,8,2,128]{3,2,1,0:T(2,128)(2,1)} %bitcast.19) | data formatting | bytes 2097152
  3.1 0.1 pad.2.clone
  3.1 1.6 %maximum_maximum_fusion.meta_ref = bf16[32,2048]{1,0:T(8,128)(2,1)} fusion(bf16[2,2048]{1,0:T(2,128)(2,1)S(1)} %convert_bitcast_fusion, bf16[16,2048]{1,0:T(8,128)(2,1)} %bitcast.20, bf16[32]{0:T(256)(128)(2,1)S(1)} %pad.2.clone), kind=kLoop, calls=%fused_computation.5 | loop fusion | flops 393216 | bytes 204864 | tf_op jit(solution)/shard_map/concatenate | solution.py:197
  4.7 0.5 iota.3.order_ref
  5.2 13.0 %sort_rows.1 = bf16[8,560,256]{2,1,0:T(8,128)(2,1)} custom-call(s32[8]{0:T(128)} %iota.3.order_ref, s32[16,128]{1,0:T(8,128)} %bitcast.21, bf16[32,2048]{1,0:T(8,128)(2,1)} %maximum_maximum_fusion.meta_ref, bf16[2048,256]{1,0:T(8,128)(2,1)} %bitcast.18), custom_call_target="tpu_custom_call" | custom-call | tf_op jit(solution)/shard_map/sort_rows/pallas_call | solution.py:71
  18.2 6.3 %all-to-all-start = ((bf16[8,560,256]{2,1,0:T(8,128)(2,1)}), bf16[8,560,256]{2,1,0:T(8,128)(2,1)S(1)}, u32[]{:S(2)}, u32[]{:S(2)}) async-start(bf16[8,560,256]{2,1,0:T(8,128)(2,1)} %sort_rows.1), calls=%async_computation | async-start | bytes 4587520 | tf_op jit(solution)/shard_map/all_to_all | solution.py:209
  24.5 53.3 %all-to-all-done.rows_ref = bf16[8,560,256]{2,1,0:T(8,128)(2,1)S(1)} async-done(((bf16[8,560,256]{2,1,0:T(8,128)(2,1)}), bf16[8,560,256]{2,1,0:T(8,128)(2,1)S(1)}, u32[]{:S(2)}, u32[]{:S(2)}) %all-to-all-start) | async-done | bytes 2293792 | tf_op jit(solution)/shard_map/all_to_all | solution.py:209
  77.8 0.0 copy-start
  77.8 1.4 %copy-done = bf16[8,560,256]{2,1,0:T(8,128)(2,1)} copy-done((bf16[8,560,256]{2,1,0:T(8,128)(2,1)}, bf16[8,560,256]{2,1,0:T(8,128)(2,1)S(1)}, u32[]{:S(2)}) %copy-start) | copy-done | bytes 2293784
  79.2 7.3 %grid_rows.1 = bf16[4,256,256]{2,1,0:T(8,128)(2,1)} custom-call(s32[1]{0:T(128)} %bitcast.place_ref, bf16[8,560,256]{2,1,0:T(8,128)(2,1)} %copy-done), custom_call_target="tpu_custom_call" | custom-call | tf_op jit(solution)/shard_map/grid_rows/pallas_call | solution.py:133
  86.4 1.8 %slice_bitcast_fusion = (bf16[256,256]{1,0:T(8,128)(2,1)S(1)}, bf16[256,256]{1,0:T(8,128)(2,1)S(1)}, bf16[256,256]{1,0:T(8,128)(2,1)S(1)}, bf16[256,256]{1,0:T(8,128)(2,1)}) fusion(bf16[4,256,256]{2,1,0:T(8,128)(2,1)} %grid_rows.1), kind=kLoop, calls=%fused_computation.1 | loop fusion | bytes 1048576 | tf_op jit(solution)/shard_map/squeeze | solution.py:213
  88.2 2.5 %collective-permute-start.2 = (bf16[256,256]{1,0:T(8,128)(2,1)S(1)}, bf16[256,256]{1,0:T(8,128)(2,1)S(1)}, u32[]{:S(2)}, u32[]{:S(2)}) collective-permute-start(bf16[256,256]{1,0:T(8,128)(2,1)S(1)} %get-tuple-element.5), channel_id=1, source_target_pairs={{0,24},{8,16},{16,8},{24,0},{1,25},{9,17},{17,9},{25,1},{2,26},{10... | collective-permute-start | bytes 393224 | tf_op jit(solution)/shard_map/ppermute | solution.py:213
  90.7 0.5 collective-permute-start.1
  91.2 0.5 collective-permute-start
  91.7 2.9 %collective-permute-done.2.x3_ref = bf16[256,256]{1,0:T(8,128)(2,1)S(1)} collective-permute-done((bf16[256,256]{1,0:T(8,128)(2,1)S(1)}, bf16[256,256]{1,0:T(8,128)(2,1)S(1)}, u32[]{:S(2)}, u32[]{:S(2)}) %collective-permute-start.2) | collective-permute-done | bytes 131104 | tf_op jit(solution)/shard_map/ppermute | solution.py:213
  94.6 0.0 copy-start.1
  94.6 2.4 %collective-permute-done.1.x2_ref = bf16[256,256]{1,0:T(8,128)(2,1)S(1)} collective-permute-done((bf16[256,256]{1,0:T(8,128)(2,1)S(1)}, bf16[256,256]{1,0:T(8,128)(2,1)S(1)}, u32[]{:S(2)}, u32[]{:S(2)}) %collective-permute-start.1) | collective-permute-done | bytes 131104 | tf_op jit(solution)/shard_map/ppermute | solution.py:213
  97.0 0.0 copy-start.2
  97.0 0.1 collective-permute-done.x1_ref
  97.0 0.0 copy-start.3
  97.0 0.0 copy-done.1
  97.0 0.6 copy-done.2
  97.6 0.1 copy-done.3
  97.7 4.1 %transform.1 = f32[256,2,512]{2,1,0:T(2,128)} custom-call(s32[1]{0:T(128)} %bitcast.place_ref, bf16[256,256]{1,0:T(8,128)(2,1)} %get-tuple-element.8.x0_ref, bf16[256,256]{1,0:T(8,128)(2,1)} %copy-done.3, bf16[256,256]{1,0:T(8,128)(2,1)} %copy-done.2, bf16[256,256]{1,0:T(8,128)(2,1)} %copy-done.1, bf16[4,256,512]{2,1,0:T(8,128)(2,1)} %constant.11.clone.high_ref, ...), custom_call_target="tpu_custom_call" | custom-call | tf_op jit(solution)/shard_map/transform/pallas_call | solution.py:183
  (1 shorter events, 0.0 us)
Async XLA Ops:
  18.2 59.6 %all-to-all-start = ((bf16[8,560,256]{2,1,0:T(8,128)(2,1)}), bf16[8,560,256]{2,1,0:T(8,128)(2,1)S(1)}, u32[]{:S(2)}, u32[]{:S(2)}) async-start(bf16[8,560,256]{2,1,0:T(8,128)(2,1)} %sort_rows.1), calls=%async_computation | async-start | bytes 4587520 | tf_op jit(solution)/shard_map/all_to_all | solution.py:209
  77.8 1.4 %copy-start = (bf16[8,560,256]{2,1,0:T(8,128)(2,1)}, bf16[8,560,256]{2,1,0:T(8,128)(2,1)S(1)}, u32[]{:S(2)}) copy-start(bf16[8,560,256]{2,1,0:T(8,128)(2,1)S(1)} %all-to-all-done.rows_ref) | copy-start | bytes 6881284
  88.2 6.4 %collective-permute-start.2 = (bf16[256,256]{1,0:T(8,128)(2,1)S(1)}, bf16[256,256]{1,0:T(8,128)(2,1)S(1)}, u32[]{:S(2)}, u32[]{:S(2)}) collective-permute-start(bf16[256,256]{1,0:T(8,128)(2,1)S(1)} %get-tuple-element.5), channel_id=1, source_target_pairs={{0,24},{8,16},{16,8},{24,0},{1,25},{9,17},{17,9},{25,1},{2,26},{10... | collective-permute-start | bytes 393224 | tf_op jit(solution)/shard_map/ppermute | solution.py:213
  90.7 6.3 %collective-permute-start.1 = (bf16[256,256]{1,0:T(8,128)(2,1)S(1)}, bf16[256,256]{1,0:T(8,128)(2,1)S(1)}, u32[]{:S(2)}, u32[]{:S(2)}) collective-permute-start(bf16[256,256]{1,0:T(8,128)(2,1)S(1)} %get-tuple-element.6), channel_id=1, source_target_pairs={{0,16},{8,24},{16,0},{24,8},{1,17},{9,25},{17,1},{25,9},{2,18},{10... | collective-permute-start | bytes 393224 | tf_op jit(solution)/shard_map/ppermute | solution.py:213
  91.2 5.8 %collective-permute-start = (bf16[256,256]{1,0:T(8,128)(2,1)S(1)}, bf16[256,256]{1,0:T(8,128)(2,1)S(1)}, u32[]{:S(2)}, u32[]{:S(2)}) collective-permute-start(bf16[256,256]{1,0:T(8,128)(2,1)S(1)} %get-tuple-element.7), channel_id=1, source_target_pairs={{0,8},{8,0},{16,24},{24,16},{1,9},{9,1},{17,25},{25,17},{2,10},{10... | collective-permute-start | bytes 393224 | tf_op jit(solution)/shard_map/ppermute | solution.py:213
  94.6 2.4 %copy-start.1 = (bf16[256,256]{1,0:T(8,128)(2,1)}, bf16[256,256]{1,0:T(8,128)(2,1)S(1)}, u32[]{:S(2)}) copy-start(bf16[256,256]{1,0:T(8,128)(2,1)S(1)} %collective-permute-done.2.x3_ref) | copy-start | bytes 393220
  97.0 0.6 copy-start.2
  97.0 0.7 copy-start.3

commit v2 on v0

--- a/solution.py
+++ b/solution.py
@@ -1,12 +1,338 @@
+import functools
 import math
 
 import jax
 import jax.numpy as jnp
+import numpy as np
 from jax import lax
+from jax.experimental import pallas as pl
+from jax.experimental.pallas import tpu as pltpu
 from jax.sharding import PartitionSpec as P
 
 SUBGRID_SIDE = 32
 KERNEL_TAPS = 8
+CELLS = SUBGRID_SIDE * SUBGRID_SIDE
+HALF = 256
+SLOTS = 2 * HALF
+META = 32
+VMEM_LIMIT = 24 << 20
+VMEM_SPEC = pl.BlockSpec(memory_space=pltpu.VMEM)
+SMEM_SPEC = pl.BlockSpec(memory_space=pltpu.SMEM)
+PARAMS = pltpu.CompilerParams(vmem_limit_bytes=VMEM_LIMIT)
+
+
+def on_chip(x):
+    return pltpu.with_memory_space_constraint(x, pltpu.VMEM)
+
+
+def tensor_dot(a, b, dims):
+    return lax.dot_general(a, b, (dims, ((), ())), preferred_element_type=jnp.float32)
+
+
+def place_rows(patch):
+    groups, lanes = patch.shape
+    members = jnp.concatenate([(patch == s).astype(jnp.float32) for s in range(8)], axis=0).astype(jnp.bfloat16)
+    row = lax.broadcasted_iota(jnp.int32, (lanes, lanes), 0)
+    col = lax.broadcasted_iota(jnp.int32, (lanes, lanes), 1)
+    before = (row < col).astype(jnp.float32).astype(jnp.bfloat16)
+    ahead = tensor_dot(members, before, ((1,), (0,)))
+    totals = tensor_dot(members, jnp.ones((lanes, lanes), jnp.bfloat16), ((1,), (0,)))
+    r = lax.broadcasted_iota(jnp.int32, (8 * groups, 8 * groups), 0)
+    c = lax.broadcasted_iota(jnp.int32, (8 * groups, 8 * groups), 1)
+    earlier = ((c < r) & (c // groups == r // groups)).astype(jnp.float32).astype(jnp.bfloat16)
+    rank_all = ahead + tensor_dot(earlier, totals.astype(jnp.bfloat16), ((1,), (0,)))
+    rank = jnp.zeros((groups, lanes), jnp.float32)
+    for s in range(8):
+        rank = jnp.where(patch == s, rank_all[s * groups : (s + 1) * groups], rank)
+    return rank
+
+
+def sort_into(target, patch, rank, columns_ref, out_ref):
+    groups, lanes = patch.shape
+    slot = lax.broadcasted_iota(jnp.int32, (HALF, lanes), 0).astype(jnp.float32).astype(jnp.bfloat16)
+    slot = slot.reshape(HALF // 16, 16, lanes)
+    one = jnp.ones((), jnp.bfloat16)
+    zero = jnp.zeros((), jnp.bfloat16)
+
+    def selection(h):
+        key = jnp.where(patch == target, rank - h * HALF, -1.0)
+        key = jnp.where(key < HALF, key, -1.0)
+        pieces = []
+        for k in range(groups):
+            k16 = jnp.broadcast_to(key[k : k + 1, :], (16, lanes)).astype(jnp.bfloat16)
+            pieces.append(jnp.where(slot == k16[None], one, zero).reshape(HALF, lanes))
+        return jnp.concatenate(pieces, axis=1)
+
+    select = jnp.concatenate([selection(0), selection(1)], axis=0)
+    out_ref[...] = tensor_dot(columns_ref[...], select, ((1,), (1,))).astype(jnp.bfloat16)
+
+
+def target_z(z, which):
+    if which == "far":
+        return jnp.where(z < 2, 3, 0)
+    if which == "near":
+        return jnp.where(z < 2, 2, 1)
+    return z ^ 1 if which == "beside" else z
+
+
+def sort_far(uv, patch, taps, starts, vis):
+    rows, parts, channels = vis.shape
+    width = parts * channels
+
+    def kernel(
+        uv_ref, patch_hbm, taps_hbm, starts_hbm, vis_hbm, far0_ref, far1_ref, columns_ref, rank_ref,
+        patch_ref, taps_ref, starts_ref, vis_ref, sems,
+    ):
+        copies = [
+            pltpu.make_async_copy(patch_hbm, patch_ref, sems.at[0]),
+            pltpu.make_async_copy(vis_hbm, vis_ref, sems.at[1]),
+            pltpu.make_async_copy(taps_hbm, taps_ref, sems.at[2]),
+            pltpu.make_async_copy(starts_hbm, starts_ref, sems.at[3]),
+        ]
+        for copy in copies:
+            copy.start()
+        copies[0].wait()
+        patch = patch_ref[...]
+        rank_ref[...] = place_rows(patch)
+        copies[2].wait()
+        copies[3].wait()
+        patch_f = patch.astype(jnp.float32)
+        columns_ref[width:, :] = jnp.concatenate(
+            [
+                taps_ref[...].astype(jnp.float32),
+                starts_ref[...].astype(jnp.float32),
+                jnp.concatenate([patch_f[k : k + 1, :] for k in range(patch.shape[0])], axis=1),
+                jnp.zeros((META - 2 * KERNEL_TAPS - 3, rows), jnp.float32),
+            ],
+            axis=0,
+        ).astype(jnp.bfloat16)
+        copies[1].wait()
+        columns_ref[:width, :] = vis_ref[...].reshape(rows, width).T
+        target = 2 * target_z(uv_ref[0] // 2, "far") + uv_ref[0] % 2
+        sort_into(target, patch, rank_ref[...], columns_ref, far0_ref)
+        sort_into(target ^ 1, patch, rank_ref[...], columns_ref, far1_ref)
+
+    in_hbm = [pltpu.with_memory_space_constraint(x, pltpu.HBM) for x in (patch, taps, starts, vis)]
+    block = pltpu.VMEM((width + META, SLOTS), jnp.bfloat16)
+    return pl.pallas_call(
+        kernel,
+        in_specs=[SMEM_SPEC] + [pl.BlockSpec(memory_space=pl.ANY)] * 4,
+        out_specs=[VMEM_SPEC] * 4,
+        out_shape=[
+            block,
+            block,
+            pltpu.VMEM((width + META, rows), jnp.bfloat16),
+            pltpu.VMEM(patch.shape, jnp.float32),
+        ],
+        scratch_shapes=[pltpu.VMEM(x.shape, x.dtype) for x in (patch, taps, starts, vis)]
+        + [pltpu.SemaphoreType.DMA((4,))],
+        compiler_params=PARAMS,
+        name="sort_far",
+    )(uv, *in_hbm)
+
+
+def patch_of(columns_ref, lanes):
+    at = columns_ref.shape[0] - META + 2 * KERNEL_TAPS
+    row = columns_ref[at : at + 16, :].astype(jnp.float32)[2:3, :]
+    pieces = [row[:, k * lanes : (k + 1) * lanes] for k in range(row.shape[1] // lanes)]
+    return jnp.concatenate(pieces, axis=0).astype(jnp.int32)
+
+
+def sort_near(uv, rank, columns, columns2):
+    def kernel(uv_ref, rank_ref, columns_ref, columns2_ref, near_ref, far_ref, rank2_ref):
+        z, core = uv_ref[0] // 2, uv_ref[0] % 2
+        target = 2 * target_z(z, "near") + core
+        patch2 = patch_of(columns2_ref, rank_ref.shape[1])
+        rank2_ref[...] = place_rows(patch2)
+        sort_into(target, patch_of(columns_ref, rank_ref.shape[1]), rank_ref[...], columns_ref, near_ref.at[0])
+        sort_into(target, patch2, rank2_ref[...], columns2_ref, near_ref.at[1])
+        sort_into(2 * target_z(z, "far") + core, patch2, rank2_ref[...], columns2_ref, far_ref)
+
+    return pl.pallas_call(
+        kernel,
+        in_specs=[SMEM_SPEC] + [VMEM_SPEC] * 3,
+        out_specs=[VMEM_SPEC] * 3,
+        out_shape=[
+            pltpu.VMEM((2, columns.shape[0], SLOTS), jnp.bfloat16),
+            pltpu.VMEM((columns.shape[0], SLOTS), jnp.bfloat16),
+            pltpu.VMEM(rank.shape, jnp.float32),
+        ],
+        compiler_params=PARAMS,
+        name="sort_near",
+    )(uv, on_chip(rank), on_chip(columns), on_chip(columns2))
+
+
+def sort_rest(uv, rank, rank2, columns, columns2):
+    def kernel(uv_ref, rank_ref, rank2_ref, columns_ref, columns2_ref, beside_ref, own_ref):
+        z, core = uv_ref[0] // 2, uv_ref[0] % 2
+        patch = patch_of(columns_ref, rank_ref.shape[1])
+        patch2 = patch_of(columns2_ref, rank_ref.shape[1])
+        for which, ref in (("beside", beside_ref), ("own", own_ref)):
+            target = 2 * target_z(z, which) + core
+            sort_into(target, patch, rank_ref[...], columns_ref, ref.at[0])
+            sort_into(target, patch2, rank2_ref[...], columns2_ref, ref.at[1])
+
+    return pl.pallas_call(
+        kernel,
+        in_specs=[SMEM_SPEC] + [VMEM_SPEC] * 4,
+        out_specs=[VMEM_SPEC] * 2,
+        out_shape=[pltpu.VMEM((2, columns.shape[0], SLOTS), jnp.bfloat16)] * 2,
+        compiler_params=PARAMS,
+        name="sort_rest",
+    )(uv, on_chip(rank), on_chip(rank2), on_chip(columns), on_chip(columns2))
+
+
+def spread(taps, start):
+    cell = lax.broadcasted_iota(jnp.int32, (SUBGRID_SIDE, SLOTS), 0).astype(jnp.float32)
+    offset = cell - start
+    out = jnp.zeros((SUBGRID_SIDE, SLOTS), jnp.float32)
+    for i in range(KERNEL_TAPS):
+        out = jnp.where(offset == i, taps[i : i + 1, :], out)
+    return out
+
+
+def grid_block(block_ref, weights_ref):
+    width = block_ref.shape[0] - META
+    meta = block_ref[width:, :].astype(jnp.float32)
+    u = spread(meta[:KERNEL_TAPS], meta[2 * KERNEL_TAPS : 2 * KERNEL_TAPS + 1])
+    v = spread(meta[KERNEL_TAPS : 2 * KERNEL_TAPS], meta[2 * KERNEL_TAPS + 1 : 2 * KERNEL_TAPS + 2])
+    for y in range(SUBGRID_SIDE):
+        weights_ref[y * SUBGRID_SIDE : (y + 1) * SUBGRID_SIDE, :] = (v[y : y + 1, :] * u).astype(jnp.bfloat16)
+    return tensor_dot(weights_ref[...], block_ref[:width, :], ((1,), (1,)))
+
+
+WEIGHTS = [pltpu.VMEM((CELLS, SLOTS), jnp.bfloat16)]
+
+
+def grid_total(block_refs, weights_ref, total=None):
+    for ref in block_refs:
+        for block_ref in [ref.at[0], ref.at[1]] if len(ref.shape) == 3 else [ref]:
+            term = grid_block(block_ref, weights_ref)
+            total = term if total is None else total + term
+    return total
+
+
+def grid_rows(blocks, dtype, before=None):
+    count = len(blocks)
+    operands = [on_chip(x) for x in blocks]
+    height = operands[0].shape[-2]
+    if before is not None:
+        operands.append(on_chip(before))
+
+    def kernel(*refs):
+        total = None if before is None else refs[count][...]
+        refs[-2][...] = grid_total(refs[:count], refs[-1], total).astype(dtype)
+
+    return pl.pallas_call(
+        kernel,
+        in_specs=[VMEM_SPEC] * len(operands),
+        out_specs=VMEM_SPEC,
+        out_shape=pltpu.VMEM((CELLS, height - META), dtype),
+        scratch_shapes=WEIGHTS,
+        compiler_params=PARAMS,
+        name="grid_rows",
+    )(*operands)
+
+
+def finish(place, blocks, near, far):
+    part = CELLS // 4
+    count = len(blocks)
+
+    def kernel(place_ref, *refs):
+        near_ref, far_ref = refs[count], refs[count + 1]
+        piece_refs, total_ref, weights_ref = refs[count + 2 : count + 6], refs[-2], refs[-1]
+        total = near_ref[...] + far_ref[...].astype(jnp.float32)
+        total_ref[...] = grid_total(refs[:count], weights_ref, total)
+        for d, piece_ref in enumerate(piece_refs):
+            cells = pl.ds(pl.multiple_of((place_ref[0] ^ d) * part, part), part)
+            piece_ref[...] = total_ref[cells, :].astype(jnp.bfloat16)
+
+    piece = pltpu.VMEM((part, near.shape[1]), jnp.bfloat16)
+    return pl.pallas_call(
+        kernel,
+        in_specs=[SMEM_SPEC] + [VMEM_SPEC] * (count + 2),
+        out_specs=[VMEM_SPEC] * 4,
+        out_shape=[piece] * 4,
+        scratch_shapes=[pltpu.VMEM(near.shape, jnp.float32)] + WEIGHTS,
+        compiler_params=PARAMS,
+        name="finish",
+    )(place, *[on_chip(x) for x in blocks], on_chip(near), on_chip(far))
+
+
+def transform_matrix(length, width):
+    n = np.arange(length)
+    angle = (n[:, None] * n[None, :] % length) * (2.0 * np.pi / length)
+    blocks = length // width
+    cos = (np.cos(angle) / math.sqrt(length)).reshape(blocks, width, length)
+    sin = (np.sin(angle) / math.sqrt(length)).reshape(blocks, width, length)
+    whole = np.concatenate([cos, sin], axis=1)
+    high = whole.astype(jnp.bfloat16)
+    low = (whole - high.astype(np.float64)).astype(jnp.bfloat16)
+    return high, low
+
+
+def transform_kernel(place_ref, x0_ref, x1_ref, x2_ref, x3_ref, high_ref, low_ref, out_ref):
+    real = imag = None
+    for d, ref in enumerate((x0_ref, x1_ref, x2_ref, x3_ref)):
+        block = place_ref[0] ^ d
+        x = ref[...]
+        width = x.shape[1] // 2
+        turned = jnp.concatenate([x[:, width:], -x[:, :width]], axis=1)
+        for matrix in (high_ref[block], low_ref[block]):
+            a = jnp.dot(x, matrix, preferred_element_type=jnp.float32)
+            b = jnp.dot(turned, matrix, preferred_element_type=jnp.float32)
+            real = a if real is None else real + a
+            imag = b if imag is None else imag + b
+    out_ref[:, 0, :] = real
+    out_ref[:, 1, :] = imag
+
+
+def transform(place, pieces, high, low):
+    return pl.pallas_call(
+        transform_kernel,
+        in_specs=[SMEM_SPEC] + [VMEM_SPEC] * 6,
+        out_specs=VMEM_SPEC,
+        out_shape=jax.ShapeDtypeStruct((pieces[0].shape[0], 2, high.shape[2]), jnp.float32),
+        compiler_params=PARAMS,
+        name="transform",
+    )(place, *[on_chip(x) for x in pieces], on_chip(high), on_chip(low))
+
+
+def on_device_small(visibilities, pair_patch_number, baseline_kernel_taps, kernel_start_cells):
+    rows_here, parts_count, channels = visibilities.shape
+    patch = pair_patch_number.reshape(rows_here // 128, 128)
+    place = lax.axis_index("chan").astype(jnp.int32).reshape(1)
+    uv = lax.axis_index("uv").astype(jnp.int32).reshape(1)
+
+    def send(block, pairs, j=0):
+        return lax.ppermute(block, "uv", [(2 * a + c, 2 * b + (c ^ j)) for a, b in pairs for c in range(2)])
+
+    def swap(block):
+        return lax.ppermute(block, "uv", [(u, u ^ 1) for u in range(8)])
+
+    far0, far1, columns, rank = sort_far(uv, patch, baseline_kernel_taps.T, kernel_start_cells.T, visibilities)
+    far_in = [send(far0, [(0, 1), (3, 2)]), send(far1, [(0, 1), (3, 2)], 1)]
+    columns2 = swap(columns)
+    near, far2, rank2 = sort_near(uv, rank, columns, columns2)
+    near_in = send(near, [(1, 2), (2, 1)])
+    near_in2 = send(near, [(0, 2), (3, 1)])
+
+    merged = grid_rows([far0, far2, *far_in], jnp.bfloat16)
+    merged_in = send(merged, [(1, 3), (2, 0)])
+    rank2, _ = lax.optimization_barrier((rank2, merged))
+    beside, own = sort_rest(uv, rank, rank2, columns, columns2)
+    beside_in = send(beside, [(0, 1), (1, 0), (2, 3), (3, 2)])
+    near_in, own = lax.optimization_barrier((near_in, own))
+    grid = grid_rows([own, near_in], jnp.float32)
+    near_in2, grid = lax.optimization_barrier((near_in2, grid))
+    grid = grid_rows([near_in2], jnp.float32, grid)
+    beside_in, merged_in, grid = lax.optimization_barrier((beside_in, merged_in, grid))
+    pieces = finish(place, [beside_in], grid, merged_in)
+    got = [pieces[0]]
+    for d in range(1, 4):
+        got.append(lax.ppermute(pieces[d], "chan", [(c, c ^ d) for c in range(4)]))
+    high, low = transform_matrix(4 * channels, channels)
+    return transform(place, got, jnp.asarray(high), jnp.asarray(low))[None]
 
 
 def kernel_rows(taps_float, offsets_float, cells_side):
@@ -66,7 +392,7 @@
     return stacked.reshape(leading, cell_count, parts_count, length)
 
 
-def on_device(visibilities, pair_patch_number, baseline_kernel_taps, kernel_start_cells):
+def on_device_large(visibilities, pair_patch_number, baseline_kernel_taps, kernel_start_cells):
     rows_here, parts_count, frequency_bins = visibilities.shape
     uv_devices = lax.axis_size("uv")
     capacity = 2 * rows_here // uv_devices
@@ -142,6 +468,11 @@
 def solution(mesh):
     in_specs = (P("uv", None, "chan"), P("uv", None), P("uv", None), P("uv", None))
     out_specs = P("uv", "chan", None, None)
+    small = mesh.shape["uv"] == 8 and mesh.shape["chan"] == 4
     return jax.shard_map(
-        on_device, mesh=mesh, in_specs=in_specs, out_specs=out_specs, check_vma=False
-    )
+        on_device_small if small else on_device_large,
+        mesh=mesh,
+        in_specs=in_specs,
+        out_specs=out_specs,
+        check_vma=False,
+    )

time: 133 us -> 65.6 us (0.49)
  waiting for transfers between devices: 61 us -> 31.3 us
  matrix products: 26.1 us -> 0 us
  local copies, waits for them, and re-layouts: 23.6 us -> 0.01 us
  Pallas kernels: 0 us -> 15.3 us
  other arithmetic: 6.19 us -> 0 us
  starting transfers between devices: 14.4 us -> 18.5 us
    all_to_all x3 -> x0, waiting for transfers between devices: 61 us -> none  [the longest x1 49 us: on_device(): lax.all_to_all(vis_buffer, 'uv', split_axis=0, concat_axis=0, tiled=True)]
    ppermute x0 -> x10, waiting for transfers between devices: none -> 31.3 us  [the longest x6 25.5 us: send(): lax.ppermute(block, 'uv', [(2 * a + c, 2 * b + (c ^ j)) for a, b in pairs...]
    dot_general x24 -> x0, matrix products: 26.1 us -> none  [the longest x16 21.5 us: accumulate(): lax.dot_general(weights, vis_block, (((0,), (0,)), ((), ())), preferred_e...]
    ppermute x0 -> x10, starting transfers between devices: none -> 18.5 us  [the longest x6 14.5 us: send(): lax.ppermute(block, 'uv', [(2 * a + c, 2 * b + (c ^ j)) for a, b in pairs...]
    scatter x2 -> x0, local copies, waits for them, and re-layouts: 17.2 us -> none  [the longest x1 11.2 us: on_device(): vis_buffer = jnp.zeros((slot_count, parts_count * frequency_bins), jnp.bf...]
    pallas_call x0 -> x8, Pallas kernels: none -> 15.3 us  [the longest x1 3.48 us: sort_far(): pl.pallas_call(kernel, in_specs=[SMEM_SPEC] + [pl.BlockSpec(memory_space=...]
    all_to_all x3 -> x0, starting transfers between devices: 14.4 us -> none  [the longest x1 6.33 us: on_device(): lax.all_to_all(payload_buffer.reshape(uv_devices, capacity, 2 * SUBGRID_S...]
    convert_element_type x35 -> x0, other arithmetic: 2.99 us -> none  [the longest x16 2 us: accumulate(): weights = (v_block[:, :, None] * u_block[:, None, :]).reshape(stride, SUB...]
  transfers between devices with their start and end apart: 3 -> 10, of which waited for: 3 -> 5; matrix products, arithmetic and copies ran while one was open for 8% -> 0% of each run, Pallas kernels for 0% -> 13%
where the time goes in v2:
time: 65.6 us; the launch traced here: 65.3 us
  waiting for transfers between devices  31.3 us (48%)
  starting transfers between devices  18.5 us (28%)
  Pallas kernels  15.3 us (23%)
    ppermute x6, waiting for transfers between devices, send(): lax.ppermute(block, 'uv', [(2 * a + c, 2 * b + (c ^ j)) for a, b in pairs...  25.5 us
    ppermute x6, starting transfers between devices, send(): lax.ppermute(block, 'uv', [(2 * a + c, 2 * b + (c ^ j)) for a, b in pairs...  14.5 us
    ppermute x3, waiting for transfers between devices, on_device_small(): got.append(lax.ppermute(pieces[d], 'chan', [(c, c ^ d) for c in range(4)]))  5.78 us
    ppermute x3, starting transfers between devices, on_device_small(): got.append(lax.ppermute(pieces[d], 'chan', [(c, c ^ d) for c in range(4)]))  3.55 us
    pallas_call x1, Pallas kernels, sort_far(): pl.pallas_call(kernel, in_specs=[SMEM_SPEC] + [pl.BlockSpec(memory_space=...  3.48 us
    pallas_call x3, Pallas kernels, grid_rows(): pl.pallas_call(kernel, in_specs=[VMEM_SPEC] * len(operands), out_specs=VM...  3.39 us
    pallas_call x1, Pallas kernels, sort_rest(): pl.pallas_call(kernel, in_specs=[SMEM_SPEC] + [VMEM_SPEC] * 4, out_specs=...  2.93 us
    pallas_call x1, Pallas kernels, sort_near(): pl.pallas_call(kernel, in_specs=[SMEM_SPEC] + [VMEM_SPEC] * 3, out_specs=...  2.4 us
  transfers between devices with their start and end apart: 10, of which 5 were waited for; matrix products, arithmetic and copies ran while one was open for 0% of the time, Pallas kernels for 13%

profile of v2, /device:TPU:0, one launch (start us, length us, event | category | flops | bytes accessed | tf_op | source)
XLA Modules:
  0.0 65.3 jit_solution(9809931144932844578)
XLA Ops:
  0.0 3.5 %sort_far.1 = (bf16[288,512]{1,0:T(8,128)(2,1)S(1)}, bf16[288,512]{1,0:T(8,128)(2,1)S(1)}, bf16[288,2048]{1,0:T(8,128)(2,1)S(1)}, f32[16,128]{1,0:T(8,128)S(1)}) custom-call(s32[1]{0:T(128)} %bitcast.1.uv_ref, s32[16,128]{1,0:T(8,128)} %bitcast.8, bf16[16,2048]{1,0:T(8,128)(2,1)} %bitcast.6, s32[2,2048]{1,0:T(2,128)} %bitcast.7, bf16[2048,2,128]{2,1,0:T(2,128)(2,1)} %vis_hbm.1), custom_call_target="tpu_custom_call" | custom-call | tf_op jit(solution)/shard_map/sort_far/pallas_call | solution.py:117
  3.5 0.5 collective-permute-start
  4.0 4.6 %collective-permute-start.2 = (bf16[288,512]{1,0:T(8,128)(2,1)S(1)}, bf16[288,512]{1,0:T(8,128)(2,1)S(1)}, u32[]{:S(2)}, u32[]{:S(2)}) collective-permute-start(bf16[288,512]{1,0:T(8,128)(2,1)S(1)} %get-tuple-element.31), channel_id=1, source_target_pairs={{0,3},{1,2},{6,5},{7,4},{8,11},{9,10},{14,13},{15,12},{16,19},{17,... | collective-permute-start | bytes 884744 | tf_op jit(solution)/shard_map/ppermute | solution.py:308
  8.6 1.3 %collective-permute-start.1 = (bf16[288,512]{1,0:T(8,128)(2,1)S(1)}, bf16[288,512]{1,0:T(8,128)(2,1)S(1)}, u32[]{:S(2)}, u32[]{:S(2)}) collective-permute-start(bf16[288,512]{1,0:T(8,128)(2,1)S(1)} %get-tuple-element.29.refs_0_), channel_id=1, source_target_pairs={{0,2},{1,3},{6,4},{7,5},{8,10},{9,11},{14,12},{15,13},{16,18},{17,... | collective-permute-start | bytes 884744 | tf_op jit(solution)/shard_map/ppermute | solution.py:308
  9.9 0.0 collective-permute-done.columns2_ref
  9.9 2.4 %sort_near.1 = (bf16[2,288,512]{2,1,0:T(8,128)(2,1)}, bf16[288,512]{1,0:T(8,128)(2,1)S(1)}, f32[16,128]{1,0:T(8,128)S(1)}) custom-call(s32[1]{0:T(128)} %bitcast.1.uv_ref, f32[16,128]{1,0:T(8,128)S(1)} %get-tuple-element.26.rank_ref, bf16[288,2048]{1,0:T(8,128)(2,1)S(1)} %get-tuple-element.27.columns_ref, bf16[288,2048]{1,0:T(8,128)(2,1)S(1)} %collective-permute-done.columns2_ref), custom_call_target="tpu_custom_call" | custom-call | tf_op jit(solution)/shard_map/sort_near/pallas_call | solution.py:151
  12.3 0.7 %collective-permute-start.6 = (bf16[2,288,512]{2,1,0:T(8,128)(2,1)}, bf16[2,288,512]{2,1,0:T(8,128)(2,1)S(1)}, u32[]{:S(2)}, u32[]{:S(2)}) collective-permute-start(bf16[2,288,512]{2,1,0:T(8,128)(2,1)} %get-tuple-element.34), channel_id=1, source_target_pairs={{2,4},{3,5},{4,2},{5,3},{10,12},{11,13},{12,10},{13,11},{18,20},{1... | collective-permute-start | bytes 1769480 | tf_op jit(solution)/shard_map/ppermute | solution.py:308
  13.0 4.1 %collective-permute-start.5 = (bf16[2,288,512]{2,1,0:T(8,128)(2,1)}, bf16[2,288,512]{2,1,0:T(8,128)(2,1)S(1)}, u32[]{:S(2)}, u32[]{:S(2)}) collective-permute-start(bf16[2,288,512]{2,1,0:T(8,128)(2,1)} %get-tuple-element.34), channel_id=1, source_target_pairs={{0,4},{1,5},{6,2},{7,3},{8,12},{9,13},{14,10},{15,11},{16,20},{17,... | collective-permute-start | bytes 1769480 | tf_op jit(solution)/shard_map/ppermute | solution.py:308
  17.1 0.0 collective-permute-done.2.refs_3_
  17.2 5.1 %collective-permute-done.1.refs_2_ = bf16[288,512]{1,0:T(8,128)(2,1)S(1)} collective-permute-done((bf16[288,512]{1,0:T(8,128)(2,1)S(1)}, bf16[288,512]{1,0:T(8,128)(2,1)S(1)}, u32[]{:S(2)}, u32[]{:S(2)}) %collective-permute-start.1) | collective-permute-done | bytes 294944 | tf_op jit(solution)/shard_map/ppermute | solution.py:308
  22.3 1.3 %grid_rows.3 = bf16[1024,256]{1,0:T(8,128)(2,1)S(1)} custom-call(bf16[288,512]{1,0:T(8,128)(2,1)S(1)} %get-tuple-element.29.refs_0_, bf16[288,512]{1,0:T(8,128)(2,1)S(1)} %get-tuple-element.30.refs_1_, bf16[288,512]{1,0:T(8,128)(2,1)S(1)} %collective-permute-done.1.refs_2_, bf16[288,512]{1,0:T(8,128)(2,1)S(1)} %collective-permute-done.2.refs_3_), custom_call_target="tpu_custom_call" | custom-call | tf_op jit(solution)/shard_map/grid_rows/pallas_call | solution.py:226
  23.6 2.9 %sort_rest.1 = (bf16[2,288,512]{2,1,0:T(8,128)(2,1)}, bf16[2,288,512]{2,1,0:T(8,128)(2,1)S(1)}) custom-call(s32[1]{0:T(128)} %bitcast.1.uv_ref, f32[16,128]{1,0:T(8,128)S(1)} %get-tuple-element.26.rank_ref, f32[16,128]{1,0:T(8,128)S(1)} %get-tuple-element.32.rank2_ref, bf16[288,2048]{1,0:T(8,128)(2,1)S(1)} %get-tuple-element.27.columns_ref, ...), custom_call_target="tpu_custom_call" | custom-call | tf_op jit(solution)/shard_map/sort_rest/pallas_call | solution.py:175
  26.5 2.5 %collective-permute-start.3 = (bf16[2,288,512]{2,1,0:T(8,128)(2,1)}, bf16[2,288,512]{2,1,0:T(8,128)(2,1)S(1)}, u32[]{:S(2)}, u32[]{:S(2)}) collective-permute-start(bf16[2,288,512]{2,1,0:T(8,128)(2,1)} %get-tuple-element.33), channel_id=1, source_target_pairs={{0,2},{1,3},{2,0},{3,1},{4,6},{5,7},{6,4},{7,5},{8,10},{9,11},{10,... | collective-permute-start | bytes 1769480 | tf_op jit(solution)/shard_map/ppermute | solution.py:308
  29.0 1.3 %collective-permute-start.4 = (bf16[1024,256]{1,0:T(8,128)(2,1)S(1)}, bf16[1024,256]{1,0:T(8,128)(2,1)S(1)}, u32[]{:S(2)}, u32[]{:S(2)}) collective-permute-start(bf16[1024,256]{1,0:T(8,128)(2,1)S(1)} %grid_rows.3), channel_id=1, source_target_pairs={{2,6},{3,7},{4,0},{5,1},{10,14},{11,15},{12,8},{13,9},{18,22},{19,... | collective-permute-start | bytes 1572872 | tf_op jit(solution)/shard_map/ppermute | solution.py:308
  30.3 0.0 collective-permute-done.6.refs_1_
  30.3 1.3 %grid_rows.4.refs_1_ = f32[1024,256]{1,0:T(8,128)S(1)} custom-call(bf16[2,288,512]{2,1,0:T(8,128)(2,1)S(1)} %get-tuple-element.36.refs_0_, bf16[2,288,512]{2,1,0:T(8,128)(2,1)S(1)} %collective-permute-done.6.refs_1_), custom_call_target="tpu_custom_call" | custom-call | tf_op jit(solution)/shard_map/grid_rows/pallas_call | solution.py:226
  31.6 3.4 %collective-permute-done.5.refs_0_ = bf16[2,288,512]{2,1,0:T(8,128)(2,1)S(1)} collective-permute-done((bf16[2,288,512]{2,1,0:T(8,128)(2,1)}, bf16[2,288,512]{2,1,0:T(8,128)(2,1)S(1)}, u32[]{:S(2)}, u32[]{:S(2)}) %collective-permute-start.5) | collective-permute-done | bytes 589856 | tf_op jit(solution)/shard_map/ppermute | solution.py:308
  35.0 0.8 %grid_rows.5.refs_1_ = f32[1024,256]{1,0:T(8,128)S(1)} custom-call(bf16[2,288,512]{2,1,0:T(8,128)(2,1)S(1)} %collective-permute-done.5.refs_0_, f32[1024,256]{1,0:T(8,128)S(1)} %grid_rows.4.refs_1_), custom_call_target="tpu_custom_call" | custom-call | tf_op jit(solution)/shard_map/grid_rows/pallas_call | solution.py:226
  35.8 0.0 copy-start
  35.8 0.0 copy-start.1
  35.8 17.0 %collective-permute-done.4.refs_2_ = bf16[1024,256]{1,0:T(8,128)(2,1)S(1)} collective-permute-done((bf16[1024,256]{1,0:T(8,128)(2,1)S(1)}, bf16[1024,256]{1,0:T(8,128)(2,1)S(1)}, u32[]{:S(2)}, u32[]{:S(2)}) %collective-permute-start.4) | collective-permute-done | bytes 524320 | tf_op jit(solution)/shard_map/ppermute | solution.py:308
  52.8 0.0 collective-permute-done.3.refs_0_
  52.8 0.8 %finish.1 = (bf16[256,256]{1,0:T(8,128)(2,1)S(1)}, bf16[256,256]{1,0:T(8,128)(2,1)S(1)}, bf16[256,256]{1,0:T(8,128)(2,1)S(1)}, bf16[256,256]{1,0:T(8,128)(2,1)S(1)}) custom-call(s32[1]{0:T(128)} %bitcast.place_ref, bf16[2,288,512]{2,1,0:T(8,128)(2,1)S(1)} %collective-permute-done.3.refs_0_, f32[1024,256]{1,0:T(8,128)S(1)} %grid_rows.5.refs_1_, ...), custom_call_target="tpu_custom_call" | custom-call | tf_op jit(solution)/shard_map/finish/pallas_call | solution.py:251
  53.7 1.6 %collective-permute-start.7 = (bf16[256,256]{1,0:T(8,128)(2,1)S(1)}, bf16[256,256]{1,0:T(8,128)(2,1)S(1)}, u32[]{:S(2)}, u32[]{:S(2)}) collective-permute-start(bf16[256,256]{1,0:T(8,128)(2,1)S(1)} %get-tuple-element.44), channel_id=1, source_target_pairs={{0,8},{8,0},{16,24},{24,16},{1,9},{9,1},{17,25},{25,17},{2,10},{10... | collective-permute-start | bytes 393224 | tf_op jit(solution)/shard_map/ppermute | solution.py:333
  55.2 1.5 %collective-permute-start.8 = (bf16[256,256]{1,0:T(8,128)(2,1)S(1)}, bf16[256,256]{1,0:T(8,128)(2,1)S(1)}, u32[]{:S(2)}, u32[]{:S(2)}) collective-permute-start(bf16[256,256]{1,0:T(8,128)(2,1)S(1)} %get-tuple-element.45), channel_id=1, source_target_pairs={{0,16},{8,24},{16,0},{24,8},{1,17},{9,25},{17,1},{25,9},{2,18},{10... | collective-permute-start | bytes 393224 | tf_op jit(solution)/shard_map/ppermute | solution.py:333
  56.7 0.5 collective-permute-start.9
  57.2 2.1 %collective-permute-done.7.x1_ref = bf16[256,256]{1,0:T(8,128)(2,1)S(1)} collective-permute-done((bf16[256,256]{1,0:T(8,128)(2,1)S(1)}, bf16[256,256]{1,0:T(8,128)(2,1)S(1)}, u32[]{:S(2)}, u32[]{:S(2)}) %collective-permute-start.7) | collective-permute-done | bytes 131104 | tf_op jit(solution)/shard_map/ppermute | solution.py:333
  59.3 3.7 %collective-permute-done.8.x2_ref = bf16[256,256]{1,0:T(8,128)(2,1)S(1)} collective-permute-done((bf16[256,256]{1,0:T(8,128)(2,1)S(1)}, bf16[256,256]{1,0:T(8,128)(2,1)S(1)}, u32[]{:S(2)}, u32[]{:S(2)}) %collective-permute-start.8) | collective-permute-done | bytes 131104 | tf_op jit(solution)/shard_map/ppermute | solution.py:333
  63.0 0.0 collective-permute-done.9.x3_ref
  63.0 0.0 copy-done
  63.0 0.0 copy-done.1
  63.0 2.3 %transform.1 = f32[256,2,512]{2,1,0:T(2,128)} custom-call(s32[1]{0:T(128)} %bitcast.place_ref, bf16[256,256]{1,0:T(8,128)(2,1)S(1)} %get-tuple-element.43.x0_ref, bf16[256,256]{1,0:T(8,128)(2,1)S(1)} %collective-permute-done.7.x1_ref, bf16[256,256]{1,0:T(8,128)(2,1)S(1)} %collective-permute-done.8.x2_ref, ...), custom_call_target="tpu_custom_call" | custom-call | tf_op jit(solution)/shard_map/transform/pallas_call | solution.py:291
Async XLA Ops:
  3.5 6.4 %collective-permute-start = (bf16[288,2048]{1,0:T(8,128)(2,1)S(1)}, bf16[288,2048]{1,0:T(8,128)(2,1)S(1)}, u32[]{:S(2)}, u32[]{:S(2)}) collective-permute-start(bf16[288,2048]{1,0:T(8,128)(2,1)S(1)} %get-tuple-element.27.columns_ref), channel_id=1, source_target_pairs={{0,1},{1,0},{2,3},{3,2},{4,5},{5,4},{6,7},{7,6},{8,9},{9,8},{10,11... | collective-permute-start | bytes 3538952 | tf_op jit(solution)/shard_map/ppermute | solution.py:311
  4.0 13.1 %collective-permute-start.2 = (bf16[288,512]{1,0:T(8,128)(2,1)S(1)}, bf16[288,512]{1,0:T(8,128)(2,1)S(1)}, u32[]{:S(2)}, u32[]{:S(2)}) collective-permute-start(bf16[288,512]{1,0:T(8,128)(2,1)S(1)} %get-tuple-element.31), channel_id=1, source_target_pairs={{0,3},{1,2},{6,5},{7,4},{8,11},{9,10},{14,13},{15,12},{16,19},{17,... | collective-permute-start | bytes 884744 | tf_op jit(solution)/shard_map/ppermute | solution.py:308
  8.6 13.6 %collective-permute-start.1 = (bf16[288,512]{1,0:T(8,128)(2,1)S(1)}, bf16[288,512]{1,0:T(8,128)(2,1)S(1)}, u32[]{:S(2)}, u32[]{:S(2)}) collective-permute-start(bf16[288,512]{1,0:T(8,128)(2,1)S(1)} %get-tuple-element.29.refs_0_), channel_id=1, source_target_pairs={{0,2},{1,3},{6,4},{7,5},{8,10},{9,11},{14,12},{15,13},{16,18},{17,... | collective-permute-start | bytes 884744 | tf_op jit(solution)/shard_map/ppermute | solution.py:308
  12.3 17.9 %collective-permute-start.6 = (bf16[2,288,512]{2,1,0:T(8,128)(2,1)}, bf16[2,288,512]{2,1,0:T(8,128)(2,1)S(1)}, u32[]{:S(2)}, u32[]{:S(2)}) collective-permute-start(bf16[2,288,512]{2,1,0:T(8,128)(2,1)} %get-tuple-element.34), channel_id=1, source_target_pairs={{2,4},{3,5},{4,2},{5,3},{10,12},{11,13},{12,10},{13,11},{18,20},{1... | collective-permute-start | bytes 1769480 | tf_op jit(solution)/shard_map/ppermute | solution.py:308
  13.0 22.0 %collective-permute-start.5 = (bf16[2,288,512]{2,1,0:T(8,128)(2,1)}, bf16[2,288,512]{2,1,0:T(8,128)(2,1)S(1)}, u32[]{:S(2)}, u32[]{:S(2)}) collective-permute-start(bf16[2,288,512]{2,1,0:T(8,128)(2,1)} %get-tuple-element.34), channel_id=1, source_target_pairs={{0,4},{1,5},{6,2},{7,3},{8,12},{9,13},{14,10},{15,11},{16,20},{17,... | collective-permute-start | bytes 1769480 | tf_op jit(solution)/shard_map/ppermute | solution.py:308
  26.5 26.3 %collective-permute-start.3 = (bf16[2,288,512]{2,1,0:T(8,128)(2,1)}, bf16[2,288,512]{2,1,0:T(8,128)(2,1)S(1)}, u32[]{:S(2)}, u32[]{:S(2)}) collective-permute-start(bf16[2,288,512]{2,1,0:T(8,128)(2,1)} %get-tuple-element.33), channel_id=1, source_target_pairs={{0,2},{1,3},{2,0},{3,1},{4,6},{5,7},{6,4},{7,5},{8,10},{9,11},{10,... | collective-permute-start | bytes 1769480 | tf_op jit(solution)/shard_map/ppermute | solution.py:308
  29.0 23.8 %collective-permute-start.4 = (bf16[1024,256]{1,0:T(8,128)(2,1)S(1)}, bf16[1024,256]{1,0:T(8,128)(2,1)S(1)}, u32[]{:S(2)}, u32[]{:S(2)}) collective-permute-start(bf16[1024,256]{1,0:T(8,128)(2,1)S(1)} %grid_rows.3), channel_id=1, source_target_pairs={{2,6},{3,7},{4,0},{5,1},{10,14},{11,15},{12,8},{13,9},{18,22},{19,... | collective-permute-start | bytes 1572872 | tf_op jit(solution)/shard_map/ppermute | solution.py:308
  35.8 27.2 %copy-start = (bf16[4,256,512]{2,1,0:T(8,128)(2,1)S(1)}, bf16[4,256,512]{2,1,0:T(8,128)(2,1)}, u32[]{:S(2)}) copy-start(bf16[4,256,512]{2,1,0:T(8,128)(2,1)} %constant.13.clone.low_ref) | copy-start | bytes 3145732
  35.8 27.2 %copy-start.1 = (bf16[4,256,512]{2,1,0:T(8,128)(2,1)S(1)}, bf16[4,256,512]{2,1,0:T(8,128)(2,1)}, u32[]{:S(2)}) copy-start(bf16[4,256,512]{2,1,0:T(8,128)(2,1)} %constant.12.clone.high_ref) | copy-start | bytes 3145732
  53.7 5.6 %collective-permute-start.7 = (bf16[256,256]{1,0:T(8,128)(2,1)S(1)}, bf16[256,256]{1,0:T(8,128)(2,1)S(1)}, u32[]{:S(2)}, u32[]{:S(2)}) collective-permute-start(bf16[256,256]{1,0:T(8,128)(2,1)S(1)} %get-tuple-element.44), channel_id=1, source_target_pairs={{0,8},{8,0},{16,24},{24,16},{1,9},{9,1},{17,25},{25,17},{2,10},{10... | collective-permute-start | bytes 393224 | tf_op jit(solution)/shard_map/ppermute | solution.py:333
  55.2 7.8 %collective-permute-start.8 = (bf16[256,256]{1,0:T(8,128)(2,1)S(1)}, bf16[256,256]{1,0:T(8,128)(2,1)S(1)}, u32[]{:S(2)}, u32[]{:S(2)}) collective-permute-start(bf16[256,256]{1,0:T(8,128)(2,1)S(1)} %get-tuple-element.45), channel_id=1, source_target_pairs={{0,16},{8,24},{16,0},{24,8},{1,17},{9,25},{17,1},{25,9},{2,18},{10... | collective-permute-start | bytes 393224 | tf_op jit(solution)/shard_map/ppermute | solution.py:333
  56.7 6.3 %collective-permute-start.9 = (bf16[256,256]{1,0:T(8,128)(2,1)S(1)}, bf16[256,256]{1,0:T(8,128)(2,1)S(1)}, u32[]{:S(2)}, u32[]{:S(2)}) collective-permute-start(bf16[256,256]{1,0:T(8,128)(2,1)S(1)} %get-tuple-element.46), channel_id=1, source_target_pairs={{0,24},{8,16},{16,8},{24,0},{1,25},{9,17},{17,9},{25,1},{2,26},{10... | collective-permute-start | bytes 393224 | tf_op jit(solution)/shard_map/ppermute | solution.py:333

commit v3 on v2

--- a/solution.py
+++ b/solution.py
@@ -67,20 +67,12 @@
     out_ref[...] = tensor_dot(columns_ref[...], select, ((1,), (1,))).astype(jnp.bfloat16)
 
 
-def target_z(z, which):
-    if which == "far":
-        return jnp.where(z < 2, 3, 0)
-    if which == "near":
-        return jnp.where(z < 2, 2, 1)
-    return z ^ 1 if which == "beside" else z
-
-
-def sort_far(uv, patch, taps, starts, vis):
+def sort_first(uv, patch, taps, starts, vis):
     rows, parts, channels = vis.shape
     width = parts * channels
 
     def kernel(
-        uv_ref, patch_hbm, taps_hbm, starts_hbm, vis_hbm, far0_ref, far1_ref, columns_ref, rank_ref,
+        uv_ref, patch_hbm, taps_hbm, starts_hbm, vis_hbm, first0_ref, first1_ref, first_ref, columns_ref, rank_ref,
         patch_ref, taps_ref, starts_ref, vis_ref, sems,
     ):
         copies = [
@@ -108,26 +100,27 @@
         ).astype(jnp.bfloat16)
         copies[1].wait()
         columns_ref[:width, :] = vis_ref[...].reshape(rows, width).T
-        target = 2 * target_z(uv_ref[0] // 2, "far") + uv_ref[0] % 2
-        sort_into(target, patch, rank_ref[...], columns_ref, far0_ref)
-        sort_into(target ^ 1, patch, rank_ref[...], columns_ref, far1_ref)
+        target = 2 * (3 - uv_ref[0] // 2) + uv_ref[0] % 2
+        for j, ref in enumerate((first0_ref, first1_ref)):
+            sort_into(target ^ j, patch, rank_ref[...], columns_ref, ref)
+            first_ref[j] = ref[...]
 
     in_hbm = [pltpu.with_memory_space_constraint(x, pltpu.HBM) for x in (patch, taps, starts, vis)]
-    block = pltpu.VMEM((width + META, SLOTS), jnp.bfloat16)
     return pl.pallas_call(
         kernel,
         in_specs=[SMEM_SPEC] + [pl.BlockSpec(memory_space=pl.ANY)] * 4,
-        out_specs=[VMEM_SPEC] * 4,
+        out_specs=[VMEM_SPEC] * 5,
         out_shape=[
-            block,
-            block,
+            pltpu.VMEM((width + META, SLOTS), jnp.bfloat16),
+            pltpu.VMEM((width + META, SLOTS), jnp.bfloat16),
+            pltpu.VMEM((2, width + META, SLOTS), jnp.bfloat16),
             pltpu.VMEM((width + META, rows), jnp.bfloat16),
             pltpu.VMEM(patch.shape, jnp.float32),
         ],
         scratch_shapes=[pltpu.VMEM(x.shape, x.dtype) for x in (patch, taps, starts, vis)]
         + [pltpu.SemaphoreType.DMA((4,))],
         compiler_params=PARAMS,
-        name="sort_far",
+        name="sort_first",
     )(uv, *in_hbm)
 
 
@@ -138,37 +131,39 @@
     return jnp.concatenate(pieces, axis=0).astype(jnp.int32)
 
 
-def sort_near(uv, rank, columns, columns2):
-    def kernel(uv_ref, rank_ref, columns_ref, columns2_ref, near_ref, far_ref, rank2_ref):
+def at_ends(z, end, middle):
+    return jnp.where((z == 0) | (z == 3), end, middle)
+
+
+def sort_second(uv, rank, columns, columns2):
+    def kernel(uv_ref, rank_ref, columns_ref, columns2_ref, second_ref, rank2_ref):
         z, core = uv_ref[0] // 2, uv_ref[0] % 2
-        target = 2 * target_z(z, "near") + core
+        target = 2 * at_ends(z, (3 - z) ^ 1, z ^ 1) + core
         patch2 = patch_of(columns2_ref, rank_ref.shape[1])
         rank2_ref[...] = place_rows(patch2)
-        sort_into(target, patch_of(columns_ref, rank_ref.shape[1]), rank_ref[...], columns_ref, near_ref.at[0])
-        sort_into(target, patch2, rank2_ref[...], columns2_ref, near_ref.at[1])
-        sort_into(2 * target_z(z, "far") + core, patch2, rank2_ref[...], columns2_ref, far_ref)
+        sort_into(target, patch_of(columns_ref, rank_ref.shape[1]), rank_ref[...], columns_ref, second_ref.at[0])
+        sort_into(target, patch2, rank2_ref[...], columns2_ref, second_ref.at[1])
 
     return pl.pallas_call(
         kernel,
         in_specs=[SMEM_SPEC] + [VMEM_SPEC] * 3,
-        out_specs=[VMEM_SPEC] * 3,
+        out_specs=[VMEM_SPEC] * 2,
         out_shape=[
             pltpu.VMEM((2, columns.shape[0], SLOTS), jnp.bfloat16),
-            pltpu.VMEM((columns.shape[0], SLOTS), jnp.bfloat16),
             pltpu.VMEM(rank.shape, jnp.float32),
         ],
         compiler_params=PARAMS,
-        name="sort_near",
+        name="sort_second",
     )(uv, on_chip(rank), on_chip(columns), on_chip(columns2))
 
 
 def sort_rest(uv, rank, rank2, columns, columns2):
-    def kernel(uv_ref, rank_ref, rank2_ref, columns_ref, columns2_ref, beside_ref, own_ref):
+    def kernel(uv_ref, rank_ref, rank2_ref, columns_ref, columns2_ref, third_ref, own_ref):
         z, core = uv_ref[0] // 2, uv_ref[0] % 2
         patch = patch_of(columns_ref, rank_ref.shape[1])
         patch2 = patch_of(columns2_ref, rank_ref.shape[1])
-        for which, ref in (("beside", beside_ref), ("own", own_ref)):
-            target = 2 * target_z(z, which) + core
+        third = 2 * at_ends(z, z ^ 1, (3 - z) ^ 1) + core
+        for target, ref in ((third, third_ref), (uv_ref[0], own_ref)):
             sort_into(target, patch, rank_ref[...], columns_ref, ref.at[0])
             sort_into(target, patch2, rank2_ref[...], columns2_ref, ref.at[1])
 
@@ -191,72 +186,86 @@
     return out
 
 
-def grid_block(block_ref, weights_ref):
-    width = block_ref.shape[0] - META
-    meta = block_ref[width:, :].astype(jnp.float32)
+def fill_weights(meta, weights_ref):
+    meta = meta.astype(jnp.float32)
     u = spread(meta[:KERNEL_TAPS], meta[2 * KERNEL_TAPS : 2 * KERNEL_TAPS + 1])
     v = spread(meta[KERNEL_TAPS : 2 * KERNEL_TAPS], meta[2 * KERNEL_TAPS + 1 : 2 * KERNEL_TAPS + 2])
     for y in range(SUBGRID_SIDE):
         weights_ref[y * SUBGRID_SIDE : (y + 1) * SUBGRID_SIDE, :] = (v[y : y + 1, :] * u).astype(jnp.bfloat16)
-    return tensor_dot(weights_ref[...], block_ref[:width, :], ((1,), (1,)))
 
 
 WEIGHTS = [pltpu.VMEM((CELLS, SLOTS), jnp.bfloat16)]
 
 
-def grid_total(block_refs, weights_ref, total=None):
-    for ref in block_refs:
-        for block_ref in [ref.at[0], ref.at[1]] if len(ref.shape) == 3 else [ref]:
-            term = grid_block(block_ref, weights_ref)
-            total = term if total is None else total + term
+def grid_total(blocks, weights_ref, total=None):
+    for block in blocks:
+        width = block.shape[0] - META
+        fill_weights(block[width:, :], weights_ref)
+        term = tensor_dot(weights_ref[...], block[:width, :], ((1,), (1,)))
+        total = term if total is None else total + term
     return total
 
 
-def grid_rows(blocks, dtype, before=None):
+def grid_rows(blocks, dtype):
     count = len(blocks)
-    operands = [on_chip(x) for x in blocks]
-    height = operands[0].shape[-2]
-    if before is not None:
-        operands.append(on_chip(before))
 
     def kernel(*refs):
-        total = None if before is None else refs[count][...]
-        refs[-2][...] = grid_total(refs[:count], refs[-1], total).astype(dtype)
-
-    return pl.pallas_call(
-        kernel,
-        in_specs=[VMEM_SPEC] * len(operands),
+        parts = []
+        for (_, which), ref in zip(blocks, refs):
+            parts += [ref] if which is None else [ref.at[j] for j in which]
+        refs[-2][...] = grid_total(parts, refs[-1]).astype(dtype)
+
+    return pl.pallas_call(
+        kernel,
+        in_specs=[VMEM_SPEC] * count,
         out_specs=VMEM_SPEC,
-        out_shape=pltpu.VMEM((CELLS, height - META), dtype),
+        out_shape=pltpu.VMEM((CELLS, blocks[0][0].shape[-2] - META), dtype),
         scratch_shapes=WEIGHTS,
         compiler_params=PARAMS,
         name="grid_rows",
-    )(*operands)
-
-
-def finish(place, blocks, near, far):
-    part = CELLS // 4
+    )(*[on_chip(x) for x, _ in blocks])
+
+
+def grid_pieces(place, blocks, before=None):
+    cells = CELLS // 4
     count = len(blocks)
+    width = blocks[0][0].shape[-2] - META
+    operands = [x for x, _ in blocks] + ([] if before is None else [before])
 
     def kernel(place_ref, *refs):
-        near_ref, far_ref = refs[count], refs[count + 1]
-        piece_refs, total_ref, weights_ref = refs[count + 2 : count + 6], refs[-2], refs[-1]
-        total = near_ref[...] + far_ref[...].astype(jnp.float32)
-        total_ref[...] = grid_total(refs[:count], weights_ref, total)
+        piece_refs, total_ref, weights_ref = refs[-6:-2], refs[-2], refs[-1]
+        parts = []
+        for (_, which), ref in zip(blocks, refs):
+            parts += [ref] if which is None else [ref.at[j] for j in which]
+        total_ref[...] = grid_total(parts, weights_ref, None if before is None else refs[count][...])
         for d, piece_ref in enumerate(piece_refs):
-            cells = pl.ds(pl.multiple_of((place_ref[0] ^ d) * part, part), part)
-            piece_ref[...] = total_ref[cells, :].astype(jnp.bfloat16)
-
-    piece = pltpu.VMEM((part, near.shape[1]), jnp.bfloat16)
-    return pl.pallas_call(
-        kernel,
-        in_specs=[SMEM_SPEC] + [VMEM_SPEC] * (count + 2),
+            at = pl.ds(pl.multiple_of((place_ref[0] ^ d) * cells, cells), cells)
+            piece_ref[...] = total_ref[at, :].astype(jnp.bfloat16)
+
+    return pl.pallas_call(
+        kernel,
+        in_specs=[SMEM_SPEC] + [VMEM_SPEC] * len(operands),
         out_specs=[VMEM_SPEC] * 4,
-        out_shape=[piece] * 4,
-        scratch_shapes=[pltpu.VMEM(near.shape, jnp.float32)] + WEIGHTS,
-        compiler_params=PARAMS,
-        name="finish",
-    )(place, *[on_chip(x) for x in blocks], on_chip(near), on_chip(far))
+        out_shape=[pltpu.VMEM((cells, width), jnp.bfloat16)] * 4,
+        scratch_shapes=[pltpu.VMEM((CELLS, width), jnp.float32)] + WEIGHTS,
+        compiler_params=PARAMS,
+        name="grid_pieces",
+    )(place, *[on_chip(x) for x in operands])
+
+
+def stack(pieces):
+    def kernel(*refs):
+        for d, ref in enumerate(refs[:-1]):
+            refs[-1][d] = ref[...]
+
+    return pl.pallas_call(
+        kernel,
+        in_specs=[VMEM_SPEC] * len(pieces),
+        out_specs=VMEM_SPEC,
+        out_shape=pltpu.VMEM((len(pieces), *pieces[0].shape), pieces[0].dtype),
+        compiler_params=PARAMS,
+        name="stack",
+    )(*[on_chip(x) for x in pieces])
 
 
 def transform_matrix(length, width):
@@ -271,31 +280,32 @@
     return high, low
 
 
-def transform_kernel(place_ref, x0_ref, x1_ref, x2_ref, x3_ref, high_ref, low_ref, out_ref):
+def transform_kernel(place_ref, x0_ref, x1_ref, x2_ref, x3_ref, y0_ref, y_ref, high_ref, low_ref, out_ref):
     real = imag = None
     for d, ref in enumerate((x0_ref, x1_ref, x2_ref, x3_ref)):
         block = place_ref[0] ^ d
-        x = ref[...]
+        more = y0_ref[...] if d == 0 else y_ref[d - 1]
+        x = (ref[...].astype(jnp.float32) + more.astype(jnp.float32)).astype(jnp.bfloat16)
         width = x.shape[1] // 2
         turned = jnp.concatenate([x[:, width:], -x[:, :width]], axis=1)
         for matrix in (high_ref[block], low_ref[block]):
-            a = jnp.dot(x, matrix, preferred_element_type=jnp.float32)
-            b = jnp.dot(turned, matrix, preferred_element_type=jnp.float32)
+            a = tensor_dot(x, matrix, ((1,), (0,)))
+            b = tensor_dot(turned, matrix, ((1,), (0,)))
             real = a if real is None else real + a
             imag = b if imag is None else imag + b
     out_ref[:, 0, :] = real
     out_ref[:, 1, :] = imag
 
 
-def transform(place, pieces, high, low):
+def transform(place, pieces, first, rest, high, low):
     return pl.pallas_call(
         transform_kernel,
-        in_specs=[SMEM_SPEC] + [VMEM_SPEC] * 6,
+        in_specs=[SMEM_SPEC] + [VMEM_SPEC] * 8,
         out_specs=VMEM_SPEC,
         out_shape=jax.ShapeDtypeStruct((pieces[0].shape[0], 2, high.shape[2]), jnp.float32),
         compiler_params=PARAMS,
         name="transform",
-    )(place, *[on_chip(x) for x in pieces], on_chip(high), on_chip(low))
+    )(place, *[on_chip(x) for x in (*pieces, first, rest, high, low)])
 
 
 def on_device_small(visibilities, pair_patch_number, baseline_kernel_taps, kernel_start_cells):
@@ -310,29 +320,27 @@
     def swap(block):
         return lax.ppermute(block, "uv", [(u, u ^ 1) for u in range(8)])
 
-    far0, far1, columns, rank = sort_far(uv, patch, baseline_kernel_taps.T, kernel_start_cells.T, visibilities)
-    far_in = [send(far0, [(0, 1), (3, 2)]), send(far1, [(0, 1), (3, 2)], 1)]
+    def exchange(pieces):
+        return [pieces[0]] + [lax.ppermute(pieces[d], "chan", [(c, c ^ d) for c in range(4)]) for d in range(1, 4)]
+
+    first0, first1, first, columns, rank = sort_first(
+        uv, patch, baseline_kernel_taps.T, kernel_start_cells.T, visibilities
+    )
     columns2 = swap(columns)
-    near, far2, rank2 = sort_near(uv, rank, columns, columns2)
-    near_in = send(near, [(1, 2), (2, 1)])
-    near_in2 = send(near, [(0, 2), (3, 1)])
-
-    merged = grid_rows([far0, far2, *far_in], jnp.bfloat16)
-    merged_in = send(merged, [(1, 3), (2, 0)])
-    rank2, _ = lax.optimization_barrier((rank2, merged))
-    beside, own = sort_rest(uv, rank, rank2, columns, columns2)
-    beside_in = send(beside, [(0, 1), (1, 0), (2, 3), (3, 2)])
-    near_in, own = lax.optimization_barrier((near_in, own))
-    grid = grid_rows([own, near_in], jnp.float32)
-    near_in2, grid = lax.optimization_barrier((near_in2, grid))
-    grid = grid_rows([near_in2], jnp.float32, grid)
-    beside_in, merged_in, grid = lax.optimization_barrier((beside_in, merged_in, grid))
-    pieces = finish(place, [beside_in], grid, merged_in)
-    got = [pieces[0]]
-    for d in range(1, 4):
-        got.append(lax.ppermute(pieces[d], "chan", [(c, c ^ d) for c in range(4)]))
+    far_in = [send(first0, [(0, 1), (3, 2)]), send(first1, [(0, 1), (3, 2)], 1)]
+    near_in = send(first, [(1, 2), (2, 1)])
+    second, rank2 = sort_second(uv, rank, columns, columns2)
+    second_in = send(second, [(0, 2), (3, 1), (1, 0), (2, 3)])
+    third, own = sort_rest(uv, rank, rank2, columns, columns2)
+    sums = exchange(grid_pieces(place, [(third, (0, 1)), (far_in[0], None), (far_in[1], None)]))
+    onward = [(0, 1), (3, 2), (1, 3), (2, 0)]
+    sum_first, sum_rest = send(sums[0], onward), send(stack(sums[1:]), onward)
+    near_in, own, _ = lax.optimization_barrier((near_in, own, sums[0]))
+    grid = grid_rows([(own, (0, 1)), (near_in, (0,)), (swap(near_in[1]), None)], jnp.float32)
+    second_in, grid = lax.optimization_barrier((second_in, grid))
+    pieces = exchange(grid_pieces(place, [(second_in, (0, 1))], grid))
     high, low = transform_matrix(4 * channels, channels)
-    return transform(place, got, jnp.asarray(high), jnp.asarray(low))[None]
+    return transform(place, pieces, sum_first, sum_rest, jnp.asarray(high), jnp.asarray(low))[None]
 
 
 def kernel_rows(taps_float, offsets_float, cells_side):

time: 65.6 us -> 55.9 us (0.85)
  waiting for transfers between devices: 31.3 us -> 18.2 us
  starting transfers between devices: 18.5 us -> 20.9 us
  Pallas kernels: 15.3 us -> 16.3 us
    ppermute x6, waiting for transfers between devices: 25.5 us -> 12.7 us  [send(): lax.ppermute(block, 'uv', [(2 * a + c, 2 * b + (c ^ j)) for a, b in pairs...]
    ppermute x3 -> x6, starting transfers between devices: 3.55 us -> 7.11 us  [exchange(): lax.ppermute(pieces[d], 'chan', [(c, c ^ d) for c in range(4)])]
    pallas_call x7, Pallas kernels: 12.4 us -> 13.7 us  [the longest x1 4.42 us: sort_first(): pl.pallas_call(kernel, in_specs=[SMEM_SPEC] + [pl.BlockSpec(memory_space=...]
    ppermute x6, starting transfers between devices: 14.5 us -> 13.2 us  [send(): lax.ppermute(block, 'uv', [(2 * a + c, 2 * b + (c ^ j)) for a, b in pairs...]
    ppermute x3 -> x6, waiting for transfers between devices: 5.78 us -> 5.45 us  [exchange(): lax.ppermute(pieces[d], 'chan', [(c, c ^ d) for c in range(4)])]
  transfers between devices with their start and end apart: 10 -> 14, of which waited for: 5 -> 4; matrix products, arithmetic and copies ran while one was open for 0% -> 0% of each run, Pallas kernels for 13% -> 17%
where the time goes in v3:
time: 55.9 us; the launch traced here: 55.6 us
  starting transfers between devices  20.9 us (37%)
  waiting for transfers between devices  18.2 us (33%)
  Pallas kernels  16.3 us (29%)
    ppermute x6, starting transfers between devices, send(): lax.ppermute(block, 'uv', [(2 * a + c, 2 * b + (c ^ j)) for a, b in pairs...  13.2 us
    ppermute x6, waiting for transfers between devices, send(): lax.ppermute(block, 'uv', [(2 * a + c, 2 * b + (c ^ j)) for a, b in pairs...  12.7 us
    ppermute x6, starting transfers between devices, exchange(): lax.ppermute(pieces[d], 'chan', [(c, c ^ d) for c in range(4)])  7.11 us
    ppermute x6, waiting for transfers between devices, exchange(): lax.ppermute(pieces[d], 'chan', [(c, c ^ d) for c in range(4)])  5.45 us
    pallas_call x1, Pallas kernels, sort_first(): pl.pallas_call(kernel, in_specs=[SMEM_SPEC] + [pl.BlockSpec(memory_space=...  4.42 us
    pallas_call x2, Pallas kernels, grid_pieces(): pl.pallas_call(kernel, in_specs=[SMEM_SPEC] + [VMEM_SPEC] * len(operands)...  3.24 us
    pallas_call x1, Pallas kernels, sort_rest(): pl.pallas_call(kernel, in_specs=[SMEM_SPEC] + [VMEM_SPEC] * 4, out_specs=...  2.64 us
    pallas_call x1, Pallas kernels, sort_second(): pl.pallas_call(kernel, in_specs=[SMEM_SPEC] + [VMEM_SPEC] * 3, out_specs=...  2.4 us
  transfers between devices with their start and end apart: 14, of which 4 were waited for; matrix products, arithmetic and copies ran while one was open for 0% of the time, Pallas kernels for 17%

profile of v3, /device:TPU:0, one launch (start us, length us, event | category | flops | bytes accessed | tf_op | source)
XLA Modules:
  0.0 55.6 jit_solution(9583356157507061274)
XLA Ops:
  0.0 4.4 %sort_first.1 = (bf16[288,512]{1,0:T(8,128)(2,1)}, bf16[288,512]{1,0:T(8,128)(2,1)}, bf16[2,288,512]{2,1,0:T(8,128)(2,1)}, bf16[288,2048]{1,0:T(8,128)(2,1)S(1)}, f32[16,128]{1,0:T(8,128)S(1)}) custom-call(s32[1]{0:T(128)} %bitcast.1.uv_ref, s32[16,128]{1,0:T(8,128)} %bitcast.10, bf16[16,2048]{1,0:T(8,128)(2,1)} %bitcast.8, s32[2,2048]{1,0:T(2,128)} %bitcast.9, ...), custom_call_target="tpu_custom_call" | custom-call | tf_op jit(solution)/shard_map/sort_first/pallas_call | solution.py:109
  4.4 0.5 collective-permute-start
  4.9 0.7 %collective-permute-start.2 = (bf16[2,288,512]{2,1,0:T(8,128)(2,1)}, bf16[2,288,512]{2,1,0:T(8,128)(2,1)S(1)}, u32[]{:S(2)}, u32[]{:S(2)}) collective-permute-start(bf16[2,288,512]{2,1,0:T(8,128)(2,1)} %get-tuple-element.29), channel_id=1, source_target_pairs={{2,4},{3,5},{4,2},{5,3},{10,12},{11,13},{12,10},{13,11},{18,20},{1... | collective-permute-start | bytes 1769480 | tf_op jit(solution)/shard_map/ppermute | solution.py:318
  5.6 8.0 %collective-permute-start.3 = (bf16[288,512]{1,0:T(8,128)(2,1)}, bf16[288,512]{1,0:T(8,128)(2,1)}, u32[]{:S(2)}, u32[]{:S(2)}) collective-permute-start(bf16[288,512]{1,0:T(8,128)(2,1)} %get-tuple-element.33), channel_id=1, source_target_pairs={{0,2},{1,3},{6,4},{7,5},{8,10},{9,11},{14,12},{15,13},{16,18},{17,... | collective-permute-start | bytes 884744 | tf_op jit(solution)/shard_map/ppermute | solution.py:318
  13.7 2.0 %collective-permute-start.4 = (bf16[288,512]{1,0:T(8,128)(2,1)}, bf16[288,512]{1,0:T(8,128)(2,1)}, u32[]{:S(2)}, u32[]{:S(2)}) collective-permute-start(bf16[288,512]{1,0:T(8,128)(2,1)} %get-tuple-element.34), channel_id=1, source_target_pairs={{0,3},{1,2},{6,5},{7,4},{8,11},{9,10},{14,13},{15,12},{16,19},{17,... | collective-permute-start | bytes 884744 | tf_op jit(solution)/shard_map/ppermute | solution.py:318
  15.7 0.0 collective-permute-done.columns2_ref
  15.7 2.4 %sort_second.1 = (bf16[2,288,512]{2,1,0:T(8,128)(2,1)}, f32[16,128]{1,0:T(8,128)S(1)}) custom-call(s32[1]{0:T(128)} %bitcast.1.uv_ref, f32[16,128]{1,0:T(8,128)S(1)} %get-tuple-element.26.rank_ref, bf16[288,2048]{1,0:T(8,128)(2,1)S(1)} %get-tuple-element.27.columns_ref, bf16[288,2048]{1,0:T(8,128)(2,1)S(1)} %collective-permute-done.columns2_ref), custom_call_target="tpu_custom_call" | custom-call | tf_op jit(solution)/shard_map/sort_second/pallas_call | solution.py:147
  18.1 0.0 collective-permute-start.1
  18.1 2.6 %sort_rest.1 = (bf16[2,288,512]{2,1,0:T(8,128)(2,1)S(1)}, bf16[2,288,512]{2,1,0:T(8,128)(2,1)S(1)}) custom-call(s32[1]{0:T(128)} %bitcast.1.uv_ref, f32[16,128]{1,0:T(8,128)S(1)} %get-tuple-element.26.rank_ref, f32[16,128]{1,0:T(8,128)S(1)} %get-tuple-element.30.rank2_ref, bf16[288,2048]{1,0:T(8,128)(2,1)S(1)} %get-tuple-element.27.columns_ref, ...), custom_call_target="tpu_custom_call" | custom-call | tf_op jit(solution)/shard_map/sort_rest/pallas_call | solution.py:170
  20.7 0.0 collective-permute-done.3.refs_1_
  20.7 6.2 %collective-permute-done.4.refs_2_ = bf16[288,512]{1,0:T(8,128)(2,1)} collective-permute-done((bf16[288,512]{1,0:T(8,128)(2,1)}, bf16[288,512]{1,0:T(8,128)(2,1)}, u32[]{:S(2)}, u32[]{:S(2)}) %collective-permute-start.4) | collective-permute-done | bytes 294944 | tf_op jit(solution)/shard_map/ppermute | solution.py:318
  26.9 2.4 %grid_pieces.2 = (bf16[256,256]{1,0:T(8,128)(2,1)S(1)}, bf16[256,256]{1,0:T(8,128)(2,1)S(1)}, bf16[256,256]{1,0:T(8,128)(2,1)S(1)}, bf16[256,256]{1,0:T(8,128)(2,1)S(1)}) custom-call(s32[1]{0:T(128)} %bitcast.place_ref, bf16[2,288,512]{2,1,0:T(8,128)(2,1)S(1)} %get-tuple-element.32.refs_0_, bf16[288,512]{1,0:T(8,128)(2,1)} %collective-permute-done.3.refs_1_, ...), custom_call_target="tpu_custom_call" | custom-call | tf_op jit(solution)/shard_map/grid_pieces/pallas_call | solution.py:245
  29.3 0.0 collective-permute-done.2.refs_1_
  29.4 1.6 %collective-permute-start.10 = (bf16[256,256]{1,0:T(8,128)(2,1)S(1)}, bf16[256,256]{1,0:T(8,128)(2,1)S(1)}, u32[]{:S(2)}, u32[]{:S(2)}) collective-permute-start(bf16[256,256]{1,0:T(8,128)(2,1)S(1)} %get-tuple-element.44), channel_id=1, source_target_pairs={{0,8},{8,0},{16,24},{24,16},{1,9},{9,1},{17,25},{25,17},{2,10},{10... | collective-permute-start | bytes 393224 | tf_op jit(solution)/shard_map/ppermute | solution.py:324
  30.9 1.5 %collective-permute-start.11 = (bf16[256,256]{1,0:T(8,128)(2,1)S(1)}, bf16[256,256]{1,0:T(8,128)(2,1)S(1)}, u32[]{:S(2)}, u32[]{:S(2)}) collective-permute-start(bf16[256,256]{1,0:T(8,128)(2,1)S(1)} %get-tuple-element.45), channel_id=1, source_target_pairs={{0,16},{8,24},{16,0},{24,8},{1,17},{9,25},{17,1},{25,9},{2,18},{10... | collective-permute-start | bytes 393224 | tf_op jit(solution)/shard_map/ppermute | solution.py:324
  32.4 0.5 collective-permute-start.12
  32.9 0.1 collective-permute-start.5
  33.0 2.7 %collective-permute-done.10.refs_0_ = bf16[256,256]{1,0:T(8,128)(2,1)S(1)} collective-permute-done((bf16[256,256]{1,0:T(8,128)(2,1)S(1)}, bf16[256,256]{1,0:T(8,128)(2,1)S(1)}, u32[]{:S(2)}, u32[]{:S(2)}) %collective-permute-start.10) | collective-permute-done | bytes 131104 | tf_op jit(solution)/shard_map/ppermute | solution.py:324
  35.7 2.7 %collective-permute-done.11.refs_1_ = bf16[256,256]{1,0:T(8,128)(2,1)S(1)} collective-permute-done((bf16[256,256]{1,0:T(8,128)(2,1)S(1)}, bf16[256,256]{1,0:T(8,128)(2,1)S(1)}, u32[]{:S(2)}, u32[]{:S(2)}) %collective-permute-start.11) | collective-permute-done | bytes 131104 | tf_op jit(solution)/shard_map/ppermute | solution.py:324
  38.5 0.0 collective-permute-done.12.refs_2_
  38.5 2.5 %collective-permute-start.13 = (bf16[3,256,256]{2,1,0:T(8,128)(2,1)S(1)}, bf16[3,256,256]{2,1,0:T(8,128)(2,1)S(1)}, u32[]{:S(2)}, u32[]{:S(2)}) collective-permute-start(bf16[3,256,256]{2,1,0:T(8,128)(2,1)S(1)} %stack.1), channel_id=1, source_target_pairs={{0,2},{1,3},{6,4},{7,5},{2,6},{3,7},{4,0},{5,1},{8,10},{9,11},{14,... | collective-permute-start | bytes 1179656 | tf_op jit(solution)/shard_map/ppermute | solution.py:318
  41.0 0.0 collective-permute-start.9
  41.0 0.0 collective-permute-done.5.refs_2_
  41.0 0.0 copy-start.1
  41.0 1.3 %grid_rows.1.refs_1_ = f32[1024,256]{1,0:T(8,128)S(1)} custom-call(bf16[2,288,512]{2,1,0:T(8,128)(2,1)S(1)} %get-tuple-element.36.refs_0_, bf16[2,288,512]{2,1,0:T(8,128)(2,1)S(1)} %collective-permute-done.2.refs_1_, bf16[288,512]{1,0:T(8,128)(2,1)S(1)} %collective-permute-done.5.refs_2_), custom_call_target="tpu_custom_call" | custom-call | tf_op jit(solution)/shard_map/grid_rows/pallas_call | solution.py:218
  42.4 0.0 copy-start
  42.4 0.0 collective-permute-done.1.refs_0_
  42.4 0.8 %grid_pieces.3 = (bf16[256,256]{1,0:T(8,128)(2,1)S(1)}, bf16[256,256]{1,0:T(8,128)(2,1)S(1)}, bf16[256,256]{1,0:T(8,128)(2,1)S(1)}, bf16[256,256]{1,0:T(8,128)(2,1)S(1)}) custom-call(s32[1]{0:T(128)} %bitcast.place_ref, bf16[2,288,512]{2,1,0:T(8,128)(2,1)S(1)} %collective-permute-done.1.refs_0_, f32[1024,256]{1,0:T(8,128)S(1)} %grid_rows.1.refs_1_), custom_call_target="tpu_custom_call" | custom-call | tf_op jit(solution)/shard_map/grid_pieces/pallas_call | solution.py:245
  43.2 0.8 %collective-permute-start.6 = (bf16[256,256]{1,0:T(8,128)(2,1)S(1)}, bf16[256,256]{1,0:T(8,128)(2,1)S(1)}, u32[]{:S(2)}, u32[]{:S(2)}) collective-permute-start(bf16[256,256]{1,0:T(8,128)(2,1)S(1)} %get-tuple-element.41), channel_id=1, source_target_pairs={{0,8},{8,0},{16,24},{24,16},{1,9},{9,1},{17,25},{25,17},{2,10},{10... | collective-permute-start | bytes 393224 | tf_op jit(solution)/shard_map/ppermute | solution.py:324
  44.0 1.3 %collective-permute-start.7 = (bf16[256,256]{1,0:T(8,128)(2,1)S(1)}, bf16[256,256]{1,0:T(8,128)(2,1)S(1)}, u32[]{:S(2)}, u32[]{:S(2)}) collective-permute-start(bf16[256,256]{1,0:T(8,128)(2,1)S(1)} %get-tuple-element.42), channel_id=1, source_target_pairs={{0,16},{8,24},{16,0},{24,8},{1,17},{9,25},{17,1},{25,9},{2,18},{10... | collective-permute-start | bytes 393224 | tf_op jit(solution)/shard_map/ppermute | solution.py:324
  45.3 1.4 %collective-permute-start.8 = (bf16[256,256]{1,0:T(8,128)(2,1)S(1)}, bf16[256,256]{1,0:T(8,128)(2,1)S(1)}, u32[]{:S(2)}, u32[]{:S(2)}) collective-permute-start(bf16[256,256]{1,0:T(8,128)(2,1)S(1)} %get-tuple-element.43), channel_id=1, source_target_pairs={{0,24},{8,16},{16,8},{24,0},{1,25},{9,17},{17,9},{25,1},{2,26},{10... | collective-permute-start | bytes 393224 | tf_op jit(solution)/shard_map/ppermute | solution.py:324
  46.8 6.5 %collective-permute-done.9.y0_ref = bf16[256,256]{1,0:T(8,128)(2,1)S(1)} collective-permute-done((bf16[256,256]{1,0:T(8,128)(2,1)S(1)}, bf16[256,256]{1,0:T(8,128)(2,1)S(1)}, u32[]{:S(2)}, u32[]{:S(2)}) %collective-permute-start.9) | collective-permute-done | bytes 131104 | tf_op jit(solution)/shard_map/ppermute | solution.py:318
  53.3 0.0 collective-permute-done.13.y_ref
  53.3 0.0 collective-permute-done.6.x1_ref
  53.3 0.0 collective-permute-done.7.x2_ref
  53.3 0.0 collective-permute-done.8.x3_ref
  53.3 0.0 copy-done.1
  53.3 0.0 copy-done
  53.3 2.3 %transform.1 = f32[256,2,512]{2,1,0:T(2,128)} custom-call(s32[1]{0:T(128)} %bitcast.place_ref, bf16[256,256]{1,0:T(8,128)(2,1)S(1)} %get-tuple-element.40.x0_ref, bf16[256,256]{1,0:T(8,128)(2,1)S(1)} %collective-permute-done.6.x1_ref, bf16[256,256]{1,0:T(8,128)(2,1)S(1)} %collective-permute-done.7.x2_ref, ...), custom_call_target="tpu_custom_call" | custom-call | tf_op jit(solution)/shard_map/transform/pallas_call | solution.py:301
  (2 shorter events, 0.0 us)
Async XLA Ops:
  4.4 11.2 %collective-permute-start = (bf16[288,2048]{1,0:T(8,128)(2,1)S(1)}, bf16[288,2048]{1,0:T(8,128)(2,1)S(1)}, u32[]{:S(2)}, u32[]{:S(2)}) collective-permute-start(bf16[288,2048]{1,0:T(8,128)(2,1)S(1)} %get-tuple-element.27.columns_ref), channel_id=1, source_target_pairs={{0,1},{1,0},{2,3},{3,2},{4,5},{5,4},{6,7},{7,6},{8,9},{9,8},{10,11... | collective-permute-start | bytes 3538952 | tf_op jit(solution)/shard_map/ppermute | solution.py:321
  4.9 24.4 %collective-permute-start.2 = (bf16[2,288,512]{2,1,0:T(8,128)(2,1)}, bf16[2,288,512]{2,1,0:T(8,128)(2,1)S(1)}, u32[]{:S(2)}, u32[]{:S(2)}) collective-permute-start(bf16[2,288,512]{2,1,0:T(8,128)(2,1)} %get-tuple-element.29), channel_id=1, source_target_pairs={{2,4},{3,5},{4,2},{5,3},{10,12},{11,13},{12,10},{13,11},{18,20},{1... | collective-permute-start | bytes 1769480 | tf_op jit(solution)/shard_map/ppermute | solution.py:318
  5.6 15.1 %collective-permute-start.3 = (bf16[288,512]{1,0:T(8,128)(2,1)}, bf16[288,512]{1,0:T(8,128)(2,1)}, u32[]{:S(2)}, u32[]{:S(2)}) collective-permute-start(bf16[288,512]{1,0:T(8,128)(2,1)} %get-tuple-element.33), channel_id=1, source_target_pairs={{0,2},{1,3},{6,4},{7,5},{8,10},{9,11},{14,12},{15,13},{16,18},{17,... | collective-permute-start | bytes 884744 | tf_op jit(solution)/shard_map/ppermute | solution.py:318
  13.7 13.3 %collective-permute-start.4 = (bf16[288,512]{1,0:T(8,128)(2,1)}, bf16[288,512]{1,0:T(8,128)(2,1)}, u32[]{:S(2)}, u32[]{:S(2)}) collective-permute-start(bf16[288,512]{1,0:T(8,128)(2,1)} %get-tuple-element.34), channel_id=1, source_target_pairs={{0,3},{1,2},{6,5},{7,4},{8,11},{9,10},{14,13},{15,12},{16,19},{17,... | collective-permute-start | bytes 884744 | tf_op jit(solution)/shard_map/ppermute | solution.py:318
  18.1 24.3 %collective-permute-start.1 = (bf16[2,288,512]{2,1,0:T(8,128)(2,1)}, bf16[2,288,512]{2,1,0:T(8,128)(2,1)S(1)}, u32[]{:S(2)}, u32[]{:S(2)}) collective-permute-start(bf16[2,288,512]{2,1,0:T(8,128)(2,1)} %get-tuple-element.28), channel_id=1, source_target_pairs={{0,4},{1,5},{6,2},{7,3},{2,0},{3,1},{4,6},{5,7},{8,12},{9,13},{14,... | collective-permute-start | bytes 1769480 | tf_op jit(solution)/shard_map/ppermute | solution.py:318
  29.4 6.4 %collective-permute-start.10 = (bf16[256,256]{1,0:T(8,128)(2,1)S(1)}, bf16[256,256]{1,0:T(8,128)(2,1)S(1)}, u32[]{:S(2)}, u32[]{:S(2)}) collective-permute-start(bf16[256,256]{1,0:T(8,128)(2,1)S(1)} %get-tuple-element.44), channel_id=1, source_target_pairs={{0,8},{8,0},{16,24},{24,16},{1,9},{9,1},{17,25},{25,17},{2,10},{10... | collective-permute-start | bytes 393224 | tf_op jit(solution)/shard_map/ppermute | solution.py:324
  30.9 7.5 %collective-permute-start.11 = (bf16[256,256]{1,0:T(8,128)(2,1)S(1)}, bf16[256,256]{1,0:T(8,128)(2,1)S(1)}, u32[]{:S(2)}, u32[]{:S(2)}) collective-permute-start(bf16[256,256]{1,0:T(8,128)(2,1)S(1)} %get-tuple-element.45), channel_id=1, source_target_pairs={{0,16},{8,24},{16,0},{24,8},{1,17},{9,25},{17,1},{25,9},{2,18},{10... | collective-permute-start | bytes 393224 | tf_op jit(solution)/shard_map/ppermute | solution.py:324
  32.4 6.0 %collective-permute-start.12 = (bf16[256,256]{1,0:T(8,128)(2,1)S(1)}, bf16[256,256]{1,0:T(8,128)(2,1)S(1)}, u32[]{:S(2)}, u32[]{:S(2)}) collective-permute-start(bf16[256,256]{1,0:T(8,128)(2,1)S(1)} %get-tuple-element.46), channel_id=1, source_target_pairs={{0,24},{8,16},{16,8},{24,0},{1,25},{9,17},{17,9},{25,1},{2,26},{10... | collective-permute-start | bytes 393224 | tf_op jit(solution)/shard_map/ppermute | solution.py:324
  32.9 8.1 %collective-permute-start.5 = (bf16[288,512]{1,0:T(8,128)(2,1)S(1)}, bf16[288,512]{1,0:T(8,128)(2,1)S(1)}, u32[]{:S(2)}, u32[]{:S(2)}) collective-permute-start(bf16[288,512]{1,0:T(8,128)(2,1)S(1)} %slice_bitcast_fusion), channel_id=1, source_target_pairs={{0,1},{1,0},{2,3},{3,2},{4,5},{5,4},{6,7},{7,6},{8,9},{9,8},{10,11... | collective-permute-start | bytes 884744 | tf_op jit(solution)/shard_map/ppermute | solution.py:321
  38.5 14.8 %collective-permute-start.13 = (bf16[3,256,256]{2,1,0:T(8,128)(2,1)S(1)}, bf16[3,256,256]{2,1,0:T(8,128)(2,1)S(1)}, u32[]{:S(2)}, u32[]{:S(2)}) collective-permute-start(bf16[3,256,256]{2,1,0:T(8,128)(2,1)S(1)} %stack.1), channel_id=1, source_target_pairs={{0,2},{1,3},{6,4},{7,5},{2,6},{3,7},{4,0},{5,1},{8,10},{9,11},{14,... | collective-permute-start | bytes 1179656 | tf_op jit(solution)/shard_map/ppermute | solution.py:318
  41.0 12.3 %collective-permute-start.9 = (bf16[256,256]{1,0:T(8,128)(2,1)S(1)}, bf16[256,256]{1,0:T(8,128)(2,1)S(1)}, u32[]{:S(2)}, u32[]{:S(2)}) collective-permute-start(bf16[256,256]{1,0:T(8,128)(2,1)S(1)} %get-tuple-element.35), channel_id=1, source_target_pairs={{0,2},{1,3},{6,4},{7,5},{2,6},{3,7},{4,0},{5,1},{8,10},{9,11},{14,... | collective-permute-start | bytes 393224 | tf_op jit(solution)/shard_map/ppermute | solution.py:318
  41.0 12.3 %copy-start.1 = (bf16[4,256,512]{2,1,0:T(8,128)(2,1)S(1)}, bf16[4,256,512]{2,1,0:T(8,128)(2,1)}, u32[]{:S(2)}) copy-start(bf16[4,256,512]{2,1,0:T(8,128)(2,1)} %constant.12.clone.high_ref) | copy-start | bytes 3145732
  42.4 11.0 %copy-start = (bf16[4,256,512]{2,1,0:T(8,128)(2,1)S(1)}, bf16[4,256,512]{2,1,0:T(8,128)(2,1)}, u32[]{:S(2)}) copy-start(bf16[4,256,512]{2,1,0:T(8,128)(2,1)} %constant.13.clone.low_ref) | copy-start | bytes 3145732
  43.2 10.1 %collective-permute-start.6 = (bf16[256,256]{1,0:T(8,128)(2,1)S(1)}, bf16[256,256]{1,0:T(8,128)(2,1)S(1)}, u32[]{:S(2)}, u32[]{:S(2)}) collective-permute-start(bf16[256,256]{1,0:T(8,128)(2,1)S(1)} %get-tuple-element.41), channel_id=1, source_target_pairs={{0,8},{8,0},{16,24},{24,16},{1,9},{9,1},{17,25},{25,17},{2,10},{10... | collective-permute-start | bytes 393224 | tf_op jit(solution)/shard_map/ppermute | solution.py:324
  44.0 9.3 %collective-permute-start.7 = (bf16[256,256]{1,0:T(8,128)(2,1)S(1)}, bf16[256,256]{1,0:T(8,128)(2,1)S(1)}, u32[]{:S(2)}, u32[]{:S(2)}) collective-permute-start(bf16[256,256]{1,0:T(8,128)(2,1)S(1)} %get-tuple-element.42), channel_id=1, source_target_pairs={{0,16},{8,24},{16,0},{24,8},{1,17},{9,25},{17,1},{25,9},{2,18},{10... | collective-permute-start | bytes 393224 | tf_op jit(solution)/shard_map/ppermute | solution.py:324
  45.3 8.0 %collective-permute-start.8 = (bf16[256,256]{1,0:T(8,128)(2,1)S(1)}, bf16[256,256]{1,0:T(8,128)(2,1)S(1)}, u32[]{:S(2)}, u32[]{:S(2)}) collective-permute-start(bf16[256,256]{1,0:T(8,128)(2,1)S(1)} %get-tuple-element.43), channel_id=1, source_target_pairs={{0,24},{8,16},{16,8},{24,0},{1,25},{9,17},{17,9},{25,1},{2,26},{10... | collective-permute-start | bytes 393224 | tf_op jit(solution)/shard_map/ppermute | solution.py:324

commit v4 on v3

--- a/solution.py
+++ b/solution.py
@@ -14,7 +14,9 @@
 CELLS = SUBGRID_SIDE * SUBGRID_SIDE
 HALF = 256
 SLOTS = 2 * HALF
-META = 32
+META = 24
+PATCH = 2
+RANK = 3
 VMEM_LIMIT = 24 << 20
 VMEM_SPEC = pl.BlockSpec(memory_space=pltpu.VMEM)
 SMEM_SPEC = pl.BlockSpec(memory_space=pltpu.SMEM)
@@ -47,19 +49,25 @@
     return rank
 
 
-def sort_into(target, patch, rank, columns_ref, out_ref):
-    groups, lanes = patch.shape
+def sort_into(target, columns_ref, out_ref):
+    lanes = 128
+    groups = columns_ref.shape[1] // lanes
+    at = columns_ref.shape[0] - META + 2 * KERNEL_TAPS
+    data = columns_ref[at : at + META - 2 * KERNEL_TAPS, :].astype(jnp.float32)
+    patch = data[PATCH : PATCH + 1, :]
+    rank = data[RANK : RANK + 1, :] * HALF + data[RANK + 1 : RANK + 2, :]
+    mine = patch == target.astype(jnp.float32)
     slot = lax.broadcasted_iota(jnp.int32, (HALF, lanes), 0).astype(jnp.float32).astype(jnp.bfloat16)
     slot = slot.reshape(HALF // 16, 16, lanes)
     one = jnp.ones((), jnp.bfloat16)
     zero = jnp.zeros((), jnp.bfloat16)
 
     def selection(h):
-        key = jnp.where(patch == target, rank - h * HALF, -1.0)
+        key = jnp.where(mine, rank - h * HALF, -1.0)
         key = jnp.where(key < HALF, key, -1.0)
         pieces = []
         for k in range(groups):
-            k16 = jnp.broadcast_to(key[k : k + 1, :], (16, lanes)).astype(jnp.bfloat16)
+            k16 = jnp.broadcast_to(key[:, k * lanes : (k + 1) * lanes], (16, lanes)).astype(jnp.bfloat16)
             pieces.append(jnp.where(slot == k16[None], one, zero).reshape(HALF, lanes))
         return jnp.concatenate(pieces, axis=1)
 
@@ -67,12 +75,12 @@
     out_ref[...] = tensor_dot(columns_ref[...], select, ((1,), (1,))).astype(jnp.bfloat16)
 
 
-def sort_first(uv, patch, taps, starts, vis):
+def prepare(patch, taps, starts, vis):
     rows, parts, channels = vis.shape
     width = parts * channels
 
     def kernel(
-        uv_ref, patch_hbm, taps_hbm, starts_hbm, vis_hbm, first0_ref, first1_ref, first_ref, columns_ref, rank_ref,
+        patch_hbm, taps_hbm, starts_hbm, vis_hbm, columns_ref,
         patch_ref, taps_ref, starts_ref, vis_ref, sems,
     ):
         copies = [
@@ -85,96 +93,61 @@
             copy.start()
         copies[0].wait()
         patch = patch_ref[...]
-        rank_ref[...] = place_rows(patch)
+        rank = place_rows(patch)
+        high = jnp.floor(rank * (1.0 / HALF))
         copies[2].wait()
         copies[3].wait()
-        patch_f = patch.astype(jnp.float32)
+
+        def row_of(x):
+            return jnp.concatenate([x[k : k + 1, :] for k in range(x.shape[0])], axis=1)
+
         columns_ref[width:, :] = jnp.concatenate(
             [
                 taps_ref[...].astype(jnp.float32),
                 starts_ref[...].astype(jnp.float32),
-                jnp.concatenate([patch_f[k : k + 1, :] for k in range(patch.shape[0])], axis=1),
-                jnp.zeros((META - 2 * KERNEL_TAPS - 3, rows), jnp.float32),
+                row_of(patch.astype(jnp.float32)),
+                row_of(high),
+                row_of(rank - high * HALF),
+                jnp.zeros((META - 2 * KERNEL_TAPS - 5, rows), jnp.float32),
             ],
             axis=0,
         ).astype(jnp.bfloat16)
         copies[1].wait()
         columns_ref[:width, :] = vis_ref[...].reshape(rows, width).T
-        target = 2 * (3 - uv_ref[0] // 2) + uv_ref[0] % 2
-        for j, ref in enumerate((first0_ref, first1_ref)):
-            sort_into(target ^ j, patch, rank_ref[...], columns_ref, ref)
-            first_ref[j] = ref[...]
 
     in_hbm = [pltpu.with_memory_space_constraint(x, pltpu.HBM) for x in (patch, taps, starts, vis)]
     return pl.pallas_call(
         kernel,
-        in_specs=[SMEM_SPEC] + [pl.BlockSpec(memory_space=pl.ANY)] * 4,
-        out_specs=[VMEM_SPEC] * 5,
-        out_shape=[
-            pltpu.VMEM((width + META, SLOTS), jnp.bfloat16),
-            pltpu.VMEM((width + META, SLOTS), jnp.bfloat16),
-            pltpu.VMEM((2, width + META, SLOTS), jnp.bfloat16),
-            pltpu.VMEM((width + META, rows), jnp.bfloat16),
-            pltpu.VMEM(patch.shape, jnp.float32),
-        ],
+        in_specs=[pl.BlockSpec(memory_space=pl.ANY)] * 4,
+        out_specs=VMEM_SPEC,
+        out_shape=pltpu.VMEM((width + META, rows), jnp.bfloat16),
         scratch_shapes=[pltpu.VMEM(x.shape, x.dtype) for x in (patch, taps, starts, vis)]
         + [pltpu.SemaphoreType.DMA((4,))],
         compiler_params=PARAMS,
-        name="sort_first",
-    )(uv, *in_hbm)
-
-
-def patch_of(columns_ref, lanes):
-    at = columns_ref.shape[0] - META + 2 * KERNEL_TAPS
-    row = columns_ref[at : at + 16, :].astype(jnp.float32)[2:3, :]
-    pieces = [row[:, k * lanes : (k + 1) * lanes] for k in range(row.shape[1] // lanes)]
-    return jnp.concatenate(pieces, axis=0).astype(jnp.int32)
+        name="prepare",
+    )(*in_hbm)
 
 
 def at_ends(z, end, middle):
     return jnp.where((z == 0) | (z == 3), end, middle)
 
 
-def sort_second(uv, rank, columns, columns2):
-    def kernel(uv_ref, rank_ref, columns_ref, columns2_ref, second_ref, rank2_ref):
-        z, core = uv_ref[0] // 2, uv_ref[0] % 2
-        target = 2 * at_ends(z, (3 - z) ^ 1, z ^ 1) + core
-        patch2 = patch_of(columns2_ref, rank_ref.shape[1])
-        rank2_ref[...] = place_rows(patch2)
-        sort_into(target, patch_of(columns_ref, rank_ref.shape[1]), rank_ref[...], columns_ref, second_ref.at[0])
-        sort_into(target, patch2, rank2_ref[...], columns2_ref, second_ref.at[1])
+def sort_pairs(which, uv, columns, columns2):
+    def kernel(uv_ref, columns_ref, columns2_ref, *pair_refs):
+        z = uv_ref[0] // 2
+        for target_z, ref in zip(which, pair_refs):
+            target = 2 * target_z(z) + uv_ref[0] % 2
+            sort_into(target, columns_ref, ref.at[0])
+            sort_into(target, columns2_ref, ref.at[1])
 
     return pl.pallas_call(
         kernel,
-        in_specs=[SMEM_SPEC] + [VMEM_SPEC] * 3,
-        out_specs=[VMEM_SPEC] * 2,
-        out_shape=[
-            pltpu.VMEM((2, columns.shape[0], SLOTS), jnp.bfloat16),
-            pltpu.VMEM(rank.shape, jnp.float32),
-        ],
-        compiler_params=PARAMS,
-        name="sort_second",
-    )(uv, on_chip(rank), on_chip(columns), on_chip(columns2))
-
-
-def sort_rest(uv, rank, rank2, columns, columns2):
-    def kernel(uv_ref, rank_ref, rank2_ref, columns_ref, columns2_ref, third_ref, own_ref):
-        z, core = uv_ref[0] // 2, uv_ref[0] % 2
-        patch = patch_of(columns_ref, rank_ref.shape[1])
-        patch2 = patch_of(columns2_ref, rank_ref.shape[1])
-        third = 2 * at_ends(z, z ^ 1, (3 - z) ^ 1) + core
-        for target, ref in ((third, third_ref), (uv_ref[0], own_ref)):
-            sort_into(target, patch, rank_ref[...], columns_ref, ref.at[0])
-            sort_into(target, patch2, rank2_ref[...], columns2_ref, ref.at[1])
-
-    return pl.pallas_call(
-        kernel,
-        in_specs=[SMEM_SPEC] + [VMEM_SPEC] * 4,
-        out_specs=[VMEM_SPEC] * 2,
-        out_shape=[pltpu.VMEM((2, columns.shape[0], SLOTS), jnp.bfloat16)] * 2,
-        compiler_params=PARAMS,
-        name="sort_rest",
-    )(uv, on_chip(rank), on_chip(rank2), on_chip(columns), on_chip(columns2))
+        in_specs=[SMEM_SPEC] + [VMEM_SPEC] * 2,
+        out_specs=[VMEM_SPEC] * len(which),
+        out_shape=[pltpu.VMEM((2, columns.shape[0], SLOTS), jnp.bfloat16)] * len(which),
+        compiler_params=PARAMS,
+        name="sort_pairs",
+    )(uv, on_chip(columns), on_chip(columns2))
 
 
 def spread(taps, start):
@@ -280,32 +253,31 @@
     return high, low
 
 
-def transform_kernel(place_ref, x0_ref, x1_ref, x2_ref, x3_ref, y0_ref, y_ref, high_ref, low_ref, out_ref):
-    real = imag = None
+def transform_kernel(place_ref, x0_ref, x1_ref, x2_ref, x3_ref, late_ref, high_ref, low_ref, out_ref):
+    total = None
     for d, ref in enumerate((x0_ref, x1_ref, x2_ref, x3_ref)):
         block = place_ref[0] ^ d
-        more = y0_ref[...] if d == 0 else y_ref[d - 1]
-        x = (ref[...].astype(jnp.float32) + more.astype(jnp.float32)).astype(jnp.bfloat16)
+        x = (ref[...].astype(jnp.float32) + late_ref[d].astype(jnp.float32)).astype(jnp.bfloat16)
         width = x.shape[1] // 2
         turned = jnp.concatenate([x[:, width:], -x[:, :width]], axis=1)
+        x = jnp.concatenate([x, turned], axis=0)
         for matrix in (high_ref[block], low_ref[block]):
-            a = tensor_dot(x, matrix, ((1,), (0,)))
-            b = tensor_dot(turned, matrix, ((1,), (0,)))
-            real = a if real is None else real + a
-            imag = b if imag is None else imag + b
-    out_ref[:, 0, :] = real
-    out_ref[:, 1, :] = imag
-
-
-def transform(place, pieces, first, rest, high, low):
+            term = tensor_dot(x, matrix, ((1,), (0,)))
+            total = term if total is None else total + term
+    cells = out_ref.shape[0]
+    out_ref[:, 0, :] = total[:cells]
+    out_ref[:, 1, :] = total[cells:]
+
+
+def transform(place, pieces, late, high, low):
     return pl.pallas_call(
         transform_kernel,
-        in_specs=[SMEM_SPEC] + [VMEM_SPEC] * 8,
+        in_specs=[SMEM_SPEC] + [VMEM_SPEC] * 7,
         out_specs=VMEM_SPEC,
         out_shape=jax.ShapeDtypeStruct((pieces[0].shape[0], 2, high.shape[2]), jnp.float32),
         compiler_params=PARAMS,
         name="transform",
-    )(place, *[on_chip(x) for x in (*pieces, first, rest, high, low)])
+    )(place, *[on_chip(x) for x in (*pieces, late, high, low)])
 
 
 def on_device_small(visibilities, pair_patch_number, baseline_kernel_taps, kernel_start_cells):
@@ -323,24 +295,26 @@
     def exchange(pieces):
         return [pieces[0]] + [lax.ppermute(pieces[d], "chan", [(c, c ^ d) for c in range(4)]) for d in range(1, 4)]
 
-    first0, first1, first, columns, rank = sort_first(
-        uv, patch, baseline_kernel_taps.T, kernel_start_cells.T, visibilities
-    )
+    columns = prepare(patch, baseline_kernel_taps.T, kernel_start_cells.T, visibilities)
     columns2 = swap(columns)
-    far_in = [send(first0, [(0, 1), (3, 2)]), send(first1, [(0, 1), (3, 2)], 1)]
+    (first,) = sort_pairs([lambda z: 3 - z], uv, columns, columns2)
+    far_in = send(first, [(0, 1), (3, 2)])
     near_in = send(first, [(1, 2), (2, 1)])
-    second, rank2 = sort_second(uv, rank, columns, columns2)
+    (second,) = sort_pairs([lambda z: at_ends(z, (3 - z) ^ 1, z ^ 1)], uv, columns, columns2)
     second_in = send(second, [(0, 2), (3, 1), (1, 0), (2, 3)])
-    third, own = sort_rest(uv, rank, rank2, columns, columns2)
-    sums = exchange(grid_pieces(place, [(third, (0, 1)), (far_in[0], None), (far_in[1], None)]))
+    third, own = sort_pairs([lambda z: at_ends(z, z ^ 1, (3 - z) ^ 1), lambda z: z], uv, columns, columns2)
+    pair = (0, 1)
+    sums = grid_rows([(third, pair)], jnp.float32)
+    far_in, sums = lax.optimization_barrier((far_in, sums))
+    sums = exchange(grid_pieces(place, [(far_in, pair)], sums))
     onward = [(0, 1), (3, 2), (1, 3), (2, 0)]
-    sum_first, sum_rest = send(sums[0], onward), send(stack(sums[1:]), onward)
+    late = send(stack(sums), onward)
     near_in, own, _ = lax.optimization_barrier((near_in, own, sums[0]))
-    grid = grid_rows([(own, (0, 1)), (near_in, (0,)), (swap(near_in[1]), None)], jnp.float32)
+    grid = grid_rows([(own, pair), (near_in, pair)], jnp.float32)
     second_in, grid = lax.optimization_barrier((second_in, grid))
-    pieces = exchange(grid_pieces(place, [(second_in, (0, 1))], grid))
+    pieces = exchange(grid_pieces(place, [(second_in, pair)], grid))
     high, low = transform_matrix(4 * channels, channels)
-    return transform(place, pieces, sum_first, sum_rest, jnp.asarray(high), jnp.asarray(low))[None]
+    return transform(place, pieces, late, jnp.asarray(high), jnp.asarray(low))[None]
 
 
 def kernel_rows(taps_float, offsets_float, cells_side):

time: 55.9 us -> 54.4 us (0.973)
  starting transfers between devices: 20.9 us -> 17.8 us
  waiting for transfers between devices: 18.2 us -> 19.7 us
    ppermute x6 -> x4, waiting for transfers between devices: 12.7 us -> 8.36 us  [send(): lax.ppermute(block, 'uv', [(2 * a + c, 2 * b + (c ^ j)) for a, b in pairs...]
    ppermute x6, waiting for transfers between devices: 5.45 us -> 8.94 us  [exchange(): lax.ppermute(pieces[d], 'chan', [(c, c ^ d) for c in range(4)])]
    ppermute x6 -> x4, starting transfers between devices: 13.2 us -> 10.1 us  [send(): lax.ppermute(block, 'uv', [(2 * a + c, 2 * b + (c ^ j)) for a, b in pairs...]
    ppermute x2 -> x1, waiting for transfers between devices: 0.01 us -> 2.43 us  [swap(): return lax.ppermute(block, 'uv', [(u, u ^ 1) for u in range(8)])]
    pallas_call x1 -> x2, Pallas kernels: 1.32 us -> 2.08 us  [grid_rows(): pl.pallas_call(kernel, in_specs=[VMEM_SPEC] * count, out_specs=VMEM_SPEC,...]
    pallas_call x4 -> x5, Pallas kernels: 11.8 us -> 11.8 us  [the longest x3 7.13 us: sort_pairs(): pl.pallas_call(kernel, in_specs=[SMEM_SPEC] + [VMEM_SPEC] * 2, out_specs=...]
  transfers between devices with their start and end apart: 14 -> 11, of which waited for: 4 -> 9; matrix products, arithmetic and copies ran while one was open for 0% -> 0% of each run, Pallas kernels for 17% -> 18%
where the time goes in v4:
time: 54.4 us; the launch traced here: 54.2 us
  waiting for transfers between devices  19.7 us (36%)
  starting transfers between devices  17.8 us (33%)
  Pallas kernels  16.6 us (31%)
    ppermute x4, starting transfers between devices, send(): lax.ppermute(block, 'uv', [(2 * a + c, 2 * b + (c ^ j)) for a, b in pairs...  10.1 us
    ppermute x6, waiting for transfers between devices, exchange(): lax.ppermute(pieces[d], 'chan', [(c, c ^ d) for c in range(4)])  8.94 us
    ppermute x4, waiting for transfers between devices, send(): lax.ppermute(block, 'uv', [(2 * a + c, 2 * b + (c ^ j)) for a, b in pairs...  8.36 us
    pallas_call x3, Pallas kernels, sort_pairs(): pl.pallas_call(kernel, in_specs=[SMEM_SPEC] + [VMEM_SPEC] * 2, out_specs=...  7.13 us
    ppermute x6, starting transfers between devices, exchange(): lax.ppermute(pieces[d], 'chan', [(c, c ^ d) for c in range(4)])  7.11 us
    pallas_call x2, Pallas kernels, grid_pieces(): pl.pallas_call(kernel, in_specs=[SMEM_SPEC] + [VMEM_SPEC] * len(operands)...  2.69 us
    ppermute x1, waiting for transfers between devices, swap(): return lax.ppermute(block, 'uv', [(u, u ^ 1) for u in range(8)])  2.43 us
    pallas_call x1, Pallas kernels, prepare(): pl.pallas_call(kernel, in_specs=[pl.BlockSpec(memory_space=pl.ANY)] * 4,...  2.35 us
  transfers between devices with their start and end apart: 11, of which 9 were waited for; matrix products, arithmetic and copies ran while one was open for 0% of the time, Pallas kernels for 18%

profile of v4, /device:TPU:0, one launch (start us, length us, event | category | flops | bytes accessed | tf_op | source)
XLA Modules:
  0.0 54.2 jit_solution(302662581151093259)
XLA Ops:
  0.0 2.3 %prepare.1.columns_ref = bf16[280,2048]{1,0:T(8,128)(2,1)S(1)} custom-call(s32[16,128]{1,0:T(8,128)} %bitcast.8, bf16[16,2048]{1,0:T(8,128)(2,1)} %bitcast.6, s32[2,2048]{1,0:T(2,128)} %bitcast.7, bf16[2048,2,128]{2,1,0:T(2,128)(2,1)} %vis_hbm.1), custom_call_target="tpu_custom_call" | custom-call | tf_op jit(solution)/shard_map/prepare/pallas_call | solution.py:119
  2.4 0.5 collective-permute-start
  2.9 2.4 %collective-permute-done.columns2_ref = bf16[280,2048]{1,0:T(8,128)(2,1)S(1)} collective-permute-done((bf16[280,2048]{1,0:T(8,128)(2,1)S(1)}, bf16[280,2048]{1,0:T(8,128)(2,1)S(1)}, u32[]{:S(2)}, u32[]{:S(2)}) %collective-permute-start) | collective-permute-done | bytes 1146912 | tf_op jit(solution)/shard_map/ppermute | solution.py:293
  5.3 2.2 %sort_pairs.4 = bf16[2,280,512]{2,1,0:T(8,128)(2,1)} custom-call(s32[1]{0:T(128)} %bitcast.1.uv_ref, bf16[280,2048]{1,0:T(8,128)(2,1)S(1)} %prepare.1.columns_ref, bf16[280,2048]{1,0:T(8,128)(2,1)S(1)} %collective-permute-done.columns2_ref), custom_call_target="tpu_custom_call" | custom-call | tf_op jit(solution)/shard_map/sort_pairs/pallas_call | solution.py:143
  7.5 5.7 %collective-permute-start.3 = (bf16[2,280,512]{2,1,0:T(8,128)(2,1)}, bf16[2,280,512]{2,1,0:T(8,128)(2,1)}, u32[]{:S(2)}, u32[]{:S(2)}) collective-permute-start(bf16[2,280,512]{2,1,0:T(8,128)(2,1)} %sort_pairs.4), channel_id=1, source_target_pairs={{0,2},{1,3},{6,4},{7,5},{8,10},{9,11},{14,12},{15,13},{16,18},{17,... | collective-permute-start | bytes 1720328 | tf_op jit(solution)/shard_map/ppermute | solution.py:290
  13.2 0.7 %collective-permute-start.2 = (bf16[2,280,512]{2,1,0:T(8,128)(2,1)}, bf16[2,280,512]{2,1,0:T(8,128)(2,1)S(1)}, u32[]{:S(2)}, u32[]{:S(2)}) collective-permute-start(bf16[2,280,512]{2,1,0:T(8,128)(2,1)} %sort_pairs.4), channel_id=1, source_target_pairs={{2,4},{3,5},{4,2},{5,3},{10,12},{11,13},{12,10},{13,11},{18,20},{1... | collective-permute-start | bytes 1720328 | tf_op jit(solution)/shard_map/ppermute | solution.py:290
  13.9 2.2 %sort_pairs.3 = bf16[2,280,512]{2,1,0:T(8,128)(2,1)} custom-call(s32[1]{0:T(128)} %bitcast.1.uv_ref, bf16[280,2048]{1,0:T(8,128)(2,1)S(1)} %prepare.1.columns_ref, bf16[280,2048]{1,0:T(8,128)(2,1)S(1)} %collective-permute-done.columns2_ref), custom_call_target="tpu_custom_call" | custom-call | tf_op jit(solution)/shard_map/sort_pairs/pallas_call | solution.py:143
  16.1 1.3 %collective-permute-start.1 = (bf16[2,280,512]{2,1,0:T(8,128)(2,1)}, bf16[2,280,512]{2,1,0:T(8,128)(2,1)S(1)}, u32[]{:S(2)}, u32[]{:S(2)}) collective-permute-start(bf16[2,280,512]{2,1,0:T(8,128)(2,1)} %sort_pairs.3), channel_id=1, source_target_pairs={{0,4},{1,5},{6,2},{7,3},{2,0},{3,1},{4,6},{5,7},{8,12},{9,13},{14,... | collective-permute-start | bytes 1720328 | tf_op jit(solution)/shard_map/ppermute | solution.py:290
  17.4 2.6 %sort_pairs.5 = (bf16[2,280,512]{2,1,0:T(8,128)(2,1)S(1)}, bf16[2,280,512]{2,1,0:T(8,128)(2,1)S(1)}) custom-call(s32[1]{0:T(128)} %bitcast.1.uv_ref, bf16[280,2048]{1,0:T(8,128)(2,1)S(1)} %prepare.1.columns_ref, bf16[280,2048]{1,0:T(8,128)(2,1)S(1)} %collective-permute-done.columns2_ref), custom_call_target="tpu_custom_call" | custom-call | tf_op jit(solution)/shard_map/sort_pairs/pallas_call | solution.py:143
  20.0 0.8 %grid_rows.2.refs_1_ = f32[1024,256]{1,0:T(8,128)S(1)} custom-call(bf16[2,280,512]{2,1,0:T(8,128)(2,1)S(1)} %get-tuple-element.22.refs_0_), custom_call_target="tpu_custom_call" | custom-call | tf_op jit(solution)/shard_map/grid_rows/pallas_call | solution.py:191
  20.8 5.2 %collective-permute-done.3.refs_0_ = bf16[2,280,512]{2,1,0:T(8,128)(2,1)} collective-permute-done((bf16[2,280,512]{2,1,0:T(8,128)(2,1)}, bf16[2,280,512]{2,1,0:T(8,128)(2,1)}, u32[]{:S(2)}, u32[]{:S(2)}) %collective-permute-start.3) | collective-permute-done | bytes 573472 | tf_op jit(solution)/shard_map/ppermute | solution.py:290
  26.0 1.9 %grid_pieces.2 = (bf16[256,256]{1,0:T(8,128)(2,1)S(1)}, bf16[256,256]{1,0:T(8,128)(2,1)S(1)}, bf16[256,256]{1,0:T(8,128)(2,1)S(1)}, bf16[256,256]{1,0:T(8,128)(2,1)S(1)}) custom-call(s32[1]{0:T(128)} %bitcast.place_ref, bf16[2,280,512]{2,1,0:T(8,128)(2,1)} %collective-permute-done.3.refs_0_, f32[1024,256]{1,0:T(8,128)S(1)} %grid_rows.2.refs_1_), custom_call_target="tpu_custom_call" | custom-call | tf_op jit(solution)/shard_map/grid_pieces/pallas_call | solution.py:218
  27.9 1.6 %collective-permute-start.7 = (bf16[256,256]{1,0:T(8,128)(2,1)S(1)}, bf16[256,256]{1,0:T(8,128)(2,1)S(1)}, u32[]{:S(2)}, u32[]{:S(2)}) collective-permute-start(bf16[256,256]{1,0:T(8,128)(2,1)S(1)} %get-tuple-element.34), channel_id=1, source_target_pairs={{0,8},{8,0},{16,24},{24,16},{1,9},{9,1},{17,25},{25,17},{2,10},{10... | collective-permute-start | bytes 393224 | tf_op jit(solution)/shard_map/ppermute | solution.py:296
  29.5 1.5 %collective-permute-start.8 = (bf16[256,256]{1,0:T(8,128)(2,1)S(1)}, bf16[256,256]{1,0:T(8,128)(2,1)S(1)}, u32[]{:S(2)}, u32[]{:S(2)}) collective-permute-start(bf16[256,256]{1,0:T(8,128)(2,1)S(1)} %get-tuple-element.35), channel_id=1, source_target_pairs={{0,16},{8,24},{16,0},{24,8},{1,17},{9,25},{17,1},{25,9},{2,18},{10... | collective-permute-start | bytes 393224 | tf_op jit(solution)/shard_map/ppermute | solution.py:296
  31.0 0.5 collective-permute-start.9
  31.5 2.8 %collective-permute-done.7.refs_1_ = bf16[256,256]{1,0:T(8,128)(2,1)S(1)} collective-permute-done((bf16[256,256]{1,0:T(8,128)(2,1)S(1)}, bf16[256,256]{1,0:T(8,128)(2,1)S(1)}, u32[]{:S(2)}, u32[]{:S(2)}) %collective-permute-start.7) | collective-permute-done | bytes 131104 | tf_op jit(solution)/shard_map/ppermute | solution.py:296
  34.3 1.2 %collective-permute-done.8.refs_2_ = bf16[256,256]{1,0:T(8,128)(2,1)S(1)} collective-permute-done((bf16[256,256]{1,0:T(8,128)(2,1)S(1)}, bf16[256,256]{1,0:T(8,128)(2,1)S(1)}, u32[]{:S(2)}, u32[]{:S(2)}) %collective-permute-start.8) | collective-permute-done | bytes 131104 | tf_op jit(solution)/shard_map/ppermute | solution.py:296
  35.5 1.4 %collective-permute-done.9.refs_3_ = bf16[256,256]{1,0:T(8,128)(2,1)S(1)} collective-permute-done((bf16[256,256]{1,0:T(8,128)(2,1)S(1)}, bf16[256,256]{1,0:T(8,128)(2,1)S(1)}, u32[]{:S(2)}, u32[]{:S(2)}) %collective-permute-start.9) | collective-permute-done | bytes 131104 | tf_op jit(solution)/shard_map/ppermute | solution.py:296
  36.9 2.5 %collective-permute-start.10 = (bf16[4,256,256]{2,1,0:T(8,128)(2,1)S(1)}, bf16[4,256,256]{2,1,0:T(8,128)(2,1)S(1)}, u32[]{:S(2)}, u32[]{:S(2)}) collective-permute-start(bf16[4,256,256]{2,1,0:T(8,128)(2,1)S(1)} %stack.1), channel_id=1, source_target_pairs={{0,2},{1,3},{6,4},{7,5},{2,6},{3,7},{4,0},{5,1},{8,10},{9,11},{14,... | collective-permute-start | bytes 1572872 | tf_op jit(solution)/shard_map/ppermute | solution.py:290
  39.5 0.0 collective-permute-done.2.refs_1_
  39.5 0.0 copy-start.1
  39.5 1.3 %grid_rows.3.refs_1_ = f32[1024,256]{1,0:T(8,128)S(1)} custom-call(bf16[2,280,512]{2,1,0:T(8,128)(2,1)S(1)} %get-tuple-element.26.refs_0_, bf16[2,280,512]{2,1,0:T(8,128)(2,1)S(1)} %collective-permute-done.2.refs_1_), custom_call_target="tpu_custom_call" | custom-call | tf_op jit(solution)/shard_map/grid_rows/pallas_call | solution.py:191
  40.8 0.0 copy-start
  40.8 0.0 collective-permute-done.1.refs_0_
  40.8 0.8 %grid_pieces.3 = (bf16[256,256]{1,0:T(8,128)(2,1)S(1)}, bf16[256,256]{1,0:T(8,128)(2,1)S(1)}, bf16[256,256]{1,0:T(8,128)(2,1)S(1)}, bf16[256,256]{1,0:T(8,128)(2,1)S(1)}) custom-call(s32[1]{0:T(128)} %bitcast.place_ref, bf16[2,280,512]{2,1,0:T(8,128)(2,1)S(1)} %collective-permute-done.1.refs_0_, f32[1024,256]{1,0:T(8,128)S(1)} %grid_rows.3.refs_1_), custom_call_target="tpu_custom_call" | custom-call | tf_op jit(solution)/shard_map/grid_pieces/pallas_call | solution.py:218
  41.7 0.6 %collective-permute-start.4 = (bf16[256,256]{1,0:T(8,128)(2,1)S(1)}, bf16[256,256]{1,0:T(8,128)(2,1)S(1)}, u32[]{:S(2)}, u32[]{:S(2)}) collective-permute-start(bf16[256,256]{1,0:T(8,128)(2,1)S(1)} %get-tuple-element.31), channel_id=1, source_target_pairs={{0,8},{8,0},{16,24},{24,16},{1,9},{9,1},{17,25},{25,17},{2,10},{10... | collective-permute-start | bytes 393224 | tf_op jit(solution)/shard_map/ppermute | solution.py:296
  42.2 0.6 %collective-permute-start.5 = (bf16[256,256]{1,0:T(8,128)(2,1)S(1)}, bf16[256,256]{1,0:T(8,128)(2,1)S(1)}, u32[]{:S(2)}, u32[]{:S(2)}) collective-permute-start(bf16[256,256]{1,0:T(8,128)(2,1)S(1)} %get-tuple-element.32), channel_id=1, source_target_pairs={{0,16},{8,24},{16,0},{24,8},{1,17},{9,25},{17,1},{25,9},{2,18},{10... | collective-permute-start | bytes 393224 | tf_op jit(solution)/shard_map/ppermute | solution.py:296
  42.8 2.4 %collective-permute-start.6 = (bf16[256,256]{1,0:T(8,128)(2,1)S(1)}, bf16[256,256]{1,0:T(8,128)(2,1)S(1)}, u32[]{:S(2)}, u32[]{:S(2)}) collective-permute-start(bf16[256,256]{1,0:T(8,128)(2,1)S(1)} %get-tuple-element.33), channel_id=1, source_target_pairs={{0,24},{8,16},{16,8},{24,0},{1,25},{9,17},{17,9},{25,1},{2,26},{10... | collective-permute-start | bytes 393224 | tf_op jit(solution)/shard_map/ppermute | solution.py:296
  45.2 1.5 %collective-permute-done.4.x1_ref = bf16[256,256]{1,0:T(8,128)(2,1)S(1)} collective-permute-done((bf16[256,256]{1,0:T(8,128)(2,1)S(1)}, bf16[256,256]{1,0:T(8,128)(2,1)S(1)}, u32[]{:S(2)}, u32[]{:S(2)}) %collective-permute-start.4) | collective-permute-done | bytes 131104 | tf_op jit(solution)/shard_map/ppermute | solution.py:296
  46.7 0.5 collective-permute-done.5.x2_ref
  47.2 1.5 %collective-permute-done.6.x3_ref = bf16[256,256]{1,0:T(8,128)(2,1)S(1)} collective-permute-done((bf16[256,256]{1,0:T(8,128)(2,1)S(1)}, bf16[256,256]{1,0:T(8,128)(2,1)S(1)}, u32[]{:S(2)}, u32[]{:S(2)}) %collective-permute-start.6) | collective-permute-done | bytes 131104 | tf_op jit(solution)/shard_map/ppermute | solution.py:296
  48.7 3.1 %collective-permute-done.10.late_ref = bf16[4,256,256]{2,1,0:T(8,128)(2,1)S(1)} collective-permute-done((bf16[4,256,256]{2,1,0:T(8,128)(2,1)S(1)}, bf16[4,256,256]{2,1,0:T(8,128)(2,1)S(1)}, u32[]{:S(2)}, u32[]{:S(2)}) %collective-permute-start.10) | collective-permute-done | bytes 524320 | tf_op jit(solution)/shard_map/ppermute | solution.py:290
  51.9 0.0 copy-done.1
  51.9 0.0 copy-done
  51.9 2.3 %transform.1 = f32[256,2,512]{2,1,0:T(2,128)} custom-call(s32[1]{0:T(128)} %bitcast.place_ref, bf16[256,256]{1,0:T(8,128)(2,1)S(1)} %get-tuple-element.30.x0_ref, bf16[256,256]{1,0:T(8,128)(2,1)S(1)} %collective-permute-done.4.x1_ref, bf16[256,256]{1,0:T(8,128)(2,1)S(1)} %collective-permute-done.5.x2_ref, ...), custom_call_target="tpu_custom_call" | custom-call | tf_op jit(solution)/shard_map/transform/pallas_call | solution.py:273
  (1 shorter events, 0.0 us)
Async XLA Ops:
  2.4 2.9 %collective-permute-start = (bf16[280,2048]{1,0:T(8,128)(2,1)S(1)}, bf16[280,2048]{1,0:T(8,128)(2,1)S(1)}, u32[]{:S(2)}, u32[]{:S(2)}) collective-permute-start(bf16[280,2048]{1,0:T(8,128)(2,1)S(1)} %prepare.1.columns_ref), channel_id=1, source_target_pairs={{0,1},{1,0},{2,3},{3,2},{4,5},{5,4},{6,7},{7,6},{8,9},{9,8},{10,11... | collective-permute-start | bytes 3440648 | tf_op jit(solution)/shard_map/ppermute | solution.py:293
  7.5 18.5 %collective-permute-start.3 = (bf16[2,280,512]{2,1,0:T(8,128)(2,1)}, bf16[2,280,512]{2,1,0:T(8,128)(2,1)}, u32[]{:S(2)}, u32[]{:S(2)}) collective-permute-start(bf16[2,280,512]{2,1,0:T(8,128)(2,1)} %sort_pairs.4), channel_id=1, source_target_pairs={{0,2},{1,3},{6,4},{7,5},{8,10},{9,11},{14,12},{15,13},{16,18},{17,... | collective-permute-start | bytes 1720328 | tf_op jit(solution)/shard_map/ppermute | solution.py:290
  13.2 26.3 %collective-permute-start.2 = (bf16[2,280,512]{2,1,0:T(8,128)(2,1)}, bf16[2,280,512]{2,1,0:T(8,128)(2,1)S(1)}, u32[]{:S(2)}, u32[]{:S(2)}) collective-permute-start(bf16[2,280,512]{2,1,0:T(8,128)(2,1)} %sort_pairs.4), channel_id=1, source_target_pairs={{2,4},{3,5},{4,2},{5,3},{10,12},{11,13},{12,10},{13,11},{18,20},{1... | collective-permute-start | bytes 1720328 | tf_op jit(solution)/shard_map/ppermute | solution.py:290
  16.1 24.7 %collective-permute-start.1 = (bf16[2,280,512]{2,1,0:T(8,128)(2,1)}, bf16[2,280,512]{2,1,0:T(8,128)(2,1)S(1)}, u32[]{:S(2)}, u32[]{:S(2)}) collective-permute-start(bf16[2,280,512]{2,1,0:T(8,128)(2,1)} %sort_pairs.3), channel_id=1, source_target_pairs={{0,4},{1,5},{6,2},{7,3},{2,0},{3,1},{4,6},{5,7},{8,12},{9,13},{14,... | collective-permute-start | bytes 1720328 | tf_op jit(solution)/shard_map/ppermute | solution.py:290
  27.9 6.4 %collective-permute-start.7 = (bf16[256,256]{1,0:T(8,128)(2,1)S(1)}, bf16[256,256]{1,0:T(8,128)(2,1)S(1)}, u32[]{:S(2)}, u32[]{:S(2)}) collective-permute-start(bf16[256,256]{1,0:T(8,128)(2,1)S(1)} %get-tuple-element.34), channel_id=1, source_target_pairs={{0,8},{8,0},{16,24},{24,16},{1,9},{9,1},{17,25},{25,17},{2,10},{10... | collective-permute-start | bytes 393224 | tf_op jit(solution)/shard_map/ppermute | solution.py:296
  29.5 6.0 %collective-permute-start.8 = (bf16[256,256]{1,0:T(8,128)(2,1)S(1)}, bf16[256,256]{1,0:T(8,128)(2,1)S(1)}, u32[]{:S(2)}, u32[]{:S(2)}) collective-permute-start(bf16[256,256]{1,0:T(8,128)(2,1)S(1)} %get-tuple-element.35), channel_id=1, source_target_pairs={{0,16},{8,24},{16,0},{24,8},{1,17},{9,25},{17,1},{25,9},{2,18},{10... | collective-permute-start | bytes 393224 | tf_op jit(solution)/shard_map/ppermute | solution.py:296
  31.0 5.9 %collective-permute-start.9 = (bf16[256,256]{1,0:T(8,128)(2,1)S(1)}, bf16[256,256]{1,0:T(8,128)(2,1)S(1)}, u32[]{:S(2)}, u32[]{:S(2)}) collective-permute-start(bf16[256,256]{1,0:T(8,128)(2,1)S(1)} %get-tuple-element.36), channel_id=1, source_target_pairs={{0,24},{8,16},{16,8},{24,0},{1,25},{9,17},{17,9},{25,1},{2,26},{10... | collective-permute-start | bytes 393224 | tf_op jit(solution)/shard_map/ppermute | solution.py:296
  36.9 14.9 %collective-permute-start.10 = (bf16[4,256,256]{2,1,0:T(8,128)(2,1)S(1)}, bf16[4,256,256]{2,1,0:T(8,128)(2,1)S(1)}, u32[]{:S(2)}, u32[]{:S(2)}) collective-permute-start(bf16[4,256,256]{2,1,0:T(8,128)(2,1)S(1)} %stack.1), channel_id=1, source_target_pairs={{0,2},{1,3},{6,4},{7,5},{2,6},{3,7},{4,0},{5,1},{8,10},{9,11},{14,... | collective-permute-start | bytes 1572872 | tf_op jit(solution)/shard_map/ppermute | solution.py:290
  39.5 12.4 %copy-start.1 = (bf16[4,256,512]{2,1,0:T(8,128)(2,1)S(1)}, bf16[4,256,512]{2,1,0:T(8,128)(2,1)}, u32[]{:S(2)}) copy-start(bf16[4,256,512]{2,1,0:T(8,128)(2,1)} %constant.12.clone.high_ref) | copy-start | bytes 3145732
  40.8 11.1 %copy-start = (bf16[4,256,512]{2,1,0:T(8,128)(2,1)S(1)}, bf16[4,256,512]{2,1,0:T(8,128)(2,1)}, u32[]{:S(2)}) copy-start(bf16[4,256,512]{2,1,0:T(8,128)(2,1)} %constant.13.clone.low_ref) | copy-start | bytes 3145732
  41.7 5.0 %collective-permute-start.4 = (bf16[256,256]{1,0:T(8,128)(2,1)S(1)}, bf16[256,256]{1,0:T(8,128)(2,1)S(1)}, u32[]{:S(2)}, u32[]{:S(2)}) collective-permute-start(bf16[256,256]{1,0:T(8,128)(2,1)S(1)} %get-tuple-element.31), channel_id=1, source_target_pairs={{0,8},{8,0},{16,24},{24,16},{1,9},{9,1},{17,25},{25,17},{2,10},{10... | collective-permute-start | bytes 393224 | tf_op jit(solution)/shard_map/ppermute | solution.py:296
  42.2 5.0 %collective-permute-start.5 = (bf16[256,256]{1,0:T(8,128)(2,1)S(1)}, bf16[256,256]{1,0:T(8,128)(2,1)S(1)}, u32[]{:S(2)}, u32[]{:S(2)}) collective-permute-start(bf16[256,256]{1,0:T(8,128)(2,1)S(1)} %get-tuple-element.32), channel_id=1, source_target_pairs={{0,16},{8,24},{16,0},{24,8},{1,17},{9,25},{17,1},{25,9},{2,18},{10... | collective-permute-start | bytes 393224 | tf_op jit(solution)/shard_map/ppermute | solution.py:296
  42.8 5.9 %collective-permute-start.6 = (bf16[256,256]{1,0:T(8,128)(2,1)S(1)}, bf16[256,256]{1,0:T(8,128)(2,1)S(1)}, u32[]{:S(2)}, u32[]{:S(2)}) collective-permute-start(bf16[256,256]{1,0:T(8,128)(2,1)S(1)} %get-tuple-element.33), channel_id=1, source_target_pairs={{0,24},{8,16},{16,8},{24,0},{1,25},{9,17},{17,9},{25,1},{2,26},{10... | collective-permute-start | bytes 393224 | tf_op jit(solution)/shard_map/ppermute | solution.py:296

commit v5 on v4

--- a/solution.py
+++ b/solution.py
@@ -132,22 +132,24 @@
     return jnp.where((z == 0) | (z == 3), end, middle)
 
 
-def sort_pairs(which, uv, columns, columns2):
-    def kernel(uv_ref, columns_ref, columns2_ref, *pair_refs):
+def sort_pairs(which, uv, columns, columns2, after=()):
+    count = len(which)
+
+    def kernel(uv_ref, columns_ref, columns2_ref, *refs):
         z = uv_ref[0] // 2
-        for target_z, ref in zip(which, pair_refs):
+        for target_z, ref in zip(which, refs[len(after) :]):
             target = 2 * target_z(z) + uv_ref[0] % 2
             sort_into(target, columns_ref, ref.at[0])
             sort_into(target, columns2_ref, ref.at[1])
 
     return pl.pallas_call(
         kernel,
-        in_specs=[SMEM_SPEC] + [VMEM_SPEC] * 2,
-        out_specs=[VMEM_SPEC] * len(which),
-        out_shape=[pltpu.VMEM((2, columns.shape[0], SLOTS), jnp.bfloat16)] * len(which),
+        in_specs=[SMEM_SPEC] + [VMEM_SPEC] * (2 + len(after)),
+        out_specs=[VMEM_SPEC] * count,
+        out_shape=[pltpu.VMEM((2, columns.shape[0], SLOTS), jnp.bfloat16)] * count,
         compiler_params=PARAMS,
         name="sort_pairs",
-    )(uv, on_chip(columns), on_chip(columns2))
+    )(uv, *[on_chip(x) for x in (columns, columns2, *after)])
 
 
 def spread(taps, start):
@@ -300,9 +302,10 @@
     (first,) = sort_pairs([lambda z: 3 - z], uv, columns, columns2)
     far_in = send(first, [(0, 1), (3, 2)])
     near_in = send(first, [(1, 2), (2, 1)])
-    (second,) = sort_pairs([lambda z: at_ends(z, (3 - z) ^ 1, z ^ 1)], uv, columns, columns2)
+    (second,) = sort_pairs([lambda z: at_ends(z, (3 - z) ^ 1, z ^ 1)], uv, columns, columns2, [first])
     second_in = send(second, [(0, 2), (3, 1), (1, 0), (2, 3)])
-    third, own = sort_pairs([lambda z: at_ends(z, z ^ 1, (3 - z) ^ 1), lambda z: z], uv, columns, columns2)
+    last = [lambda z: at_ends(z, z ^ 1, (3 - z) ^ 1), lambda z: z]
+    third, own = sort_pairs(last, uv, columns, columns2)
     pair = (0, 1)
     sums = grid_rows([(third, pair)], jnp.float32)
     far_in, sums = lax.optimization_barrier((far_in, sums))

time: 54.4 us -> 53.4 us (0.982)
  waiting for transfers between devices: 19.7 us -> 18.3 us
    ppermute x4, waiting for transfers between devices: 8.36 us -> 6.89 us  [send(): lax.ppermute(block, 'uv', [(2 * a + c, 2 * b + (c ^ j)) for a, b in pairs...]
    pallas_call x2, Pallas kernels: 2.08 us -> 3.23 us  [grid_rows(): pl.pallas_call(kernel, in_specs=[VMEM_SPEC] * count, out_specs=VMEM_SPEC,...]
    pallas_call x3, Pallas kernels: 7.13 us -> 6.3 us  [sort_pairs(): pl.pallas_call(kernel, in_specs=[SMEM_SPEC] + [VMEM_SPEC] * (2 + len(afte...]
  transfers between devices with their start and end apart: 11 -> 11, of which waited for: 9 -> 9; matrix products, arithmetic and copies ran while one was open for 0% -> 0% of each run, Pallas kernels for 18% -> 20%
where the time goes in v5:
time: 53.4 us; the launch traced here: 53.1 us
  waiting for transfers between devices  18.3 us (34%)
  starting transfers between devices  17.9 us (34%)
  Pallas kernels  16.9 us (32%)
    ppermute x4, starting transfers between devices, send(): lax.ppermute(block, 'uv', [(2 * a + c, 2 * b + (c ^ j)) for a, b in pairs...  10.3 us
    ppermute x6, waiting for transfers between devices, exchange(): lax.ppermute(pieces[d], 'chan', [(c, c ^ d) for c in range(4)])  8.96 us
    ppermute x6, starting transfers between devices, exchange(): lax.ppermute(pieces[d], 'chan', [(c, c ^ d) for c in range(4)])  7.11 us
    ppermute x4, waiting for transfers between devices, send(): lax.ppermute(block, 'uv', [(2 * a + c, 2 * b + (c ^ j)) for a, b in pairs...  6.89 us
    pallas_call x3, Pallas kernels, sort_pairs(): pl.pallas_call(kernel, in_specs=[SMEM_SPEC] + [VMEM_SPEC] * (2 + len(afte...  6.3 us
    pallas_call x2, Pallas kernels, grid_rows(): pl.pallas_call(kernel, in_specs=[VMEM_SPEC] * count, out_specs=VMEM_SPEC,...  3.23 us
    pallas_call x2, Pallas kernels, grid_pieces(): pl.pallas_call(kernel, in_specs=[SMEM_SPEC] + [VMEM_SPEC] * len(operands)...  2.69 us
    ppermute x1, waiting for transfers between devices, swap(): return lax.ppermute(block, 'uv', [(u, u ^ 1) for u in range(8)])  2.43 us
  transfers between devices with their start and end apart: 11, of which 9 were waited for; matrix products, arithmetic and copies ran while one was open for 0% of the time, Pallas kernels for 20%

profile of v5, /device:TPU:0, one launch (start us, length us, event | category | flops | bytes accessed | tf_op | source)
XLA Modules:
  0.0 53.1 jit_solution(4885756430196718045)
XLA Ops:
  0.0 2.3 %prepare.1.columns_ref = bf16[280,2048]{1,0:T(8,128)(2,1)S(1)} custom-call(s32[16,128]{1,0:T(8,128)} %bitcast.8, bf16[16,2048]{1,0:T(8,128)(2,1)} %bitcast.6, s32[2,2048]{1,0:T(2,128)} %bitcast.7, bf16[2048,2,128]{2,1,0:T(2,128)(2,1)} %vis_hbm.1), custom_call_target="tpu_custom_call" | custom-call | tf_op jit(solution)/shard_map/prepare/pallas_call | solution.py:119
  2.4 0.5 collective-permute-start
  2.9 2.4 %collective-permute-done.columns2_ref = bf16[280,2048]{1,0:T(8,128)(2,1)S(1)} collective-permute-done((bf16[280,2048]{1,0:T(8,128)(2,1)S(1)}, bf16[280,2048]{1,0:T(8,128)(2,1)S(1)}, u32[]{:S(2)}, u32[]{:S(2)}) %collective-permute-start) | collective-permute-done | bytes 1146912 | tf_op jit(solution)/shard_map/ppermute | solution.py:295
  5.3 1.4 %sort_pairs.3.refs_0_ = bf16[2,280,512]{2,1,0:T(8,128)(2,1)S(1)} custom-call(s32[1]{0:T(128)} %bitcast.1.uv_ref, bf16[280,2048]{1,0:T(8,128)(2,1)S(1)} %prepare.1.columns_ref, bf16[280,2048]{1,0:T(8,128)(2,1)S(1)} %collective-permute-done.columns2_ref), custom_call_target="tpu_custom_call" | custom-call | tf_op jit(solution)/shard_map/sort_pairs/pallas_call | solution.py:145
  6.7 5.7 %collective-permute-start.3 = (bf16[2,280,512]{2,1,0:T(8,128)(2,1)S(1)}, bf16[2,280,512]{2,1,0:T(8,128)(2,1)}, u32[]{:S(2)}, u32[]{:S(2)}) collective-permute-start(bf16[2,280,512]{2,1,0:T(8,128)(2,1)S(1)} %sort_pairs.3.refs_0_), channel_id=1, source_target_pairs={{0,2},{1,3},{6,4},{7,5},{8,10},{9,11},{14,12},{15,13},{16,18},{17,... | collective-permute-start | bytes 1720328 | tf_op jit(solution)/shard_map/ppermute | solution.py:292
  12.4 1.5 %collective-permute-start.2 = (bf16[2,280,512]{2,1,0:T(8,128)(2,1)S(1)}, bf16[2,280,512]{2,1,0:T(8,128)(2,1)}, u32[]{:S(2)}, u32[]{:S(2)}) collective-permute-start(bf16[2,280,512]{2,1,0:T(8,128)(2,1)S(1)} %sort_pairs.3.refs_0_), channel_id=1, source_target_pairs={{2,4},{3,5},{4,2},{5,3},{10,12},{11,13},{12,10},{13,11},{18,20},{1... | collective-permute-start | bytes 1720328 | tf_op jit(solution)/shard_map/ppermute | solution.py:292
  13.9 2.2 %sort_pairs.4 = bf16[2,280,512]{2,1,0:T(8,128)(2,1)} custom-call(s32[1]{0:T(128)} %bitcast.1.uv_ref, bf16[280,2048]{1,0:T(8,128)(2,1)S(1)} %prepare.1.columns_ref, bf16[280,2048]{1,0:T(8,128)(2,1)S(1)} %collective-permute-done.columns2_ref, bf16[2,280,512]{2,1,0:T(8,128)(2,1)S(1)} %sort_pairs.3.refs_0_), custom_call_target="tpu_custom_call" | custom-call | tf_op jit(solution)/shard_map/sort_pairs/pallas_call | solution.py:145
  16.1 0.5 collective-permute-start.1
  16.6 2.6 %sort_pairs.5 = (bf16[2,280,512]{2,1,0:T(8,128)(2,1)S(1)}, bf16[2,280,512]{2,1,0:T(8,128)(2,1)S(1)}) custom-call(s32[1]{0:T(128)} %bitcast.1.uv_ref, bf16[280,2048]{1,0:T(8,128)(2,1)S(1)} %prepare.1.columns_ref, bf16[280,2048]{1,0:T(8,128)(2,1)S(1)} %collective-permute-done.columns2_ref), custom_call_target="tpu_custom_call" | custom-call | tf_op jit(solution)/shard_map/sort_pairs/pallas_call | solution.py:145
  19.2 0.8 %grid_rows.2.refs_1_ = f32[1024,256]{1,0:T(8,128)S(1)} custom-call(bf16[2,280,512]{2,1,0:T(8,128)(2,1)S(1)} %get-tuple-element.22.refs_0_), custom_call_target="tpu_custom_call" | custom-call | tf_op jit(solution)/shard_map/grid_rows/pallas_call | solution.py:193
  20.0 4.9 %collective-permute-done.3.refs_0_ = bf16[2,280,512]{2,1,0:T(8,128)(2,1)} collective-permute-done((bf16[2,280,512]{2,1,0:T(8,128)(2,1)S(1)}, bf16[2,280,512]{2,1,0:T(8,128)(2,1)}, u32[]{:S(2)}, u32[]{:S(2)}) %collective-permute-start.3) | collective-permute-done | bytes 573472 | tf_op jit(solution)/shard_map/ppermute | solution.py:292
  24.9 1.9 %grid_pieces.2 = (bf16[256,256]{1,0:T(8,128)(2,1)S(1)}, bf16[256,256]{1,0:T(8,128)(2,1)S(1)}, bf16[256,256]{1,0:T(8,128)(2,1)S(1)}, bf16[256,256]{1,0:T(8,128)(2,1)S(1)}) custom-call(s32[1]{0:T(128)} %bitcast.place_ref, bf16[2,280,512]{2,1,0:T(8,128)(2,1)} %collective-permute-done.3.refs_0_, f32[1024,256]{1,0:T(8,128)S(1)} %grid_rows.2.refs_1_), custom_call_target="tpu_custom_call" | custom-call | tf_op jit(solution)/shard_map/grid_pieces/pallas_call | solution.py:220
  26.8 1.6 %collective-permute-start.7 = (bf16[256,256]{1,0:T(8,128)(2,1)S(1)}, bf16[256,256]{1,0:T(8,128)(2,1)S(1)}, u32[]{:S(2)}, u32[]{:S(2)}) collective-permute-start(bf16[256,256]{1,0:T(8,128)(2,1)S(1)} %get-tuple-element.34), channel_id=1, source_target_pairs={{0,8},{8,0},{16,24},{24,16},{1,9},{9,1},{17,25},{25,17},{2,10},{10... | collective-permute-start | bytes 393224 | tf_op jit(solution)/shard_map/ppermute | solution.py:298
  28.3 1.5 %collective-permute-start.8 = (bf16[256,256]{1,0:T(8,128)(2,1)S(1)}, bf16[256,256]{1,0:T(8,128)(2,1)S(1)}, u32[]{:S(2)}, u32[]{:S(2)}) collective-permute-start(bf16[256,256]{1,0:T(8,128)(2,1)S(1)} %get-tuple-element.35), channel_id=1, source_target_pairs={{0,16},{8,24},{16,0},{24,8},{1,17},{9,25},{17,1},{25,9},{2,18},{10... | collective-permute-start | bytes 393224 | tf_op jit(solution)/shard_map/ppermute | solution.py:298
  29.9 0.5 collective-permute-start.9
  30.3 2.8 %collective-permute-done.7.refs_1_ = bf16[256,256]{1,0:T(8,128)(2,1)S(1)} collective-permute-done((bf16[256,256]{1,0:T(8,128)(2,1)S(1)}, bf16[256,256]{1,0:T(8,128)(2,1)S(1)}, u32[]{:S(2)}, u32[]{:S(2)}) %collective-permute-start.7) | collective-permute-done | bytes 131104 | tf_op jit(solution)/shard_map/ppermute | solution.py:298
  33.1 1.2 %collective-permute-done.8.refs_2_ = bf16[256,256]{1,0:T(8,128)(2,1)S(1)} collective-permute-done((bf16[256,256]{1,0:T(8,128)(2,1)S(1)}, bf16[256,256]{1,0:T(8,128)(2,1)S(1)}, u32[]{:S(2)}, u32[]{:S(2)}) %collective-permute-start.8) | collective-permute-done | bytes 131104 | tf_op jit(solution)/shard_map/ppermute | solution.py:298
  34.4 1.4 %collective-permute-done.9.refs_3_ = bf16[256,256]{1,0:T(8,128)(2,1)S(1)} collective-permute-done((bf16[256,256]{1,0:T(8,128)(2,1)S(1)}, bf16[256,256]{1,0:T(8,128)(2,1)S(1)}, u32[]{:S(2)}, u32[]{:S(2)}) %collective-permute-start.9) | collective-permute-done | bytes 131104 | tf_op jit(solution)/shard_map/ppermute | solution.py:298
  35.8 2.6 %collective-permute-start.10 = (bf16[4,256,256]{2,1,0:T(8,128)(2,1)S(1)}, bf16[4,256,256]{2,1,0:T(8,128)(2,1)S(1)}, u32[]{:S(2)}, u32[]{:S(2)}) collective-permute-start(bf16[4,256,256]{2,1,0:T(8,128)(2,1)S(1)} %stack.1), channel_id=1, source_target_pairs={{0,2},{1,3},{6,4},{7,5},{2,6},{3,7},{4,0},{5,1},{8,10},{9,11},{14,... | collective-permute-start | bytes 1572872 | tf_op jit(solution)/shard_map/ppermute | solution.py:292
  38.5 0.0 collective-permute-done.2.refs_1_
  38.5 0.0 copy-start.1
  38.5 2.5 %grid_rows.3.refs_1_ = f32[1024,256]{1,0:T(8,128)S(1)} custom-call(bf16[2,280,512]{2,1,0:T(8,128)(2,1)S(1)} %get-tuple-element.26.refs_0_, bf16[2,280,512]{2,1,0:T(8,128)(2,1)} %collective-permute-done.2.refs_1_), custom_call_target="tpu_custom_call" | custom-call | tf_op jit(solution)/shard_map/grid_rows/pallas_call | solution.py:193
  40.9 0.0 copy-start
  40.9 0.0 collective-permute-done.1.refs_0_
  41.0 0.8 %grid_pieces.3 = (bf16[256,256]{1,0:T(8,128)(2,1)S(1)}, bf16[256,256]{1,0:T(8,128)(2,1)S(1)}, bf16[256,256]{1,0:T(8,128)(2,1)S(1)}, bf16[256,256]{1,0:T(8,128)(2,1)S(1)}) custom-call(s32[1]{0:T(128)} %bitcast.place_ref, bf16[2,280,512]{2,1,0:T(8,128)(2,1)S(1)} %collective-permute-done.1.refs_0_, f32[1024,256]{1,0:T(8,128)S(1)} %grid_rows.3.refs_1_), custom_call_target="tpu_custom_call" | custom-call | tf_op jit(solution)/shard_map/grid_pieces/pallas_call | solution.py:220
  41.8 0.6 %collective-permute-start.4 = (bf16[256,256]{1,0:T(8,128)(2,1)S(1)}, bf16[256,256]{1,0:T(8,128)(2,1)S(1)}, u32[]{:S(2)}, u32[]{:S(2)}) collective-permute-start(bf16[256,256]{1,0:T(8,128)(2,1)S(1)} %get-tuple-element.31), channel_id=1, source_target_pairs={{0,8},{8,0},{16,24},{24,16},{1,9},{9,1},{17,25},{25,17},{2,10},{10... | collective-permute-start | bytes 393224 | tf_op jit(solution)/shard_map/ppermute | solution.py:298
  42.3 0.7 %collective-permute-start.5 = (bf16[256,256]{1,0:T(8,128)(2,1)S(1)}, bf16[256,256]{1,0:T(8,128)(2,1)S(1)}, u32[]{:S(2)}, u32[]{:S(2)}) collective-permute-start(bf16[256,256]{1,0:T(8,128)(2,1)S(1)} %get-tuple-element.32), channel_id=1, source_target_pairs={{0,16},{8,24},{16,0},{24,8},{1,17},{9,25},{17,1},{25,9},{2,18},{10... | collective-permute-start | bytes 393224 | tf_op jit(solution)/shard_map/ppermute | solution.py:298
  43.0 2.3 %collective-permute-start.6 = (bf16[256,256]{1,0:T(8,128)(2,1)S(1)}, bf16[256,256]{1,0:T(8,128)(2,1)S(1)}, u32[]{:S(2)}, u32[]{:S(2)}) collective-permute-start(bf16[256,256]{1,0:T(8,128)(2,1)S(1)} %get-tuple-element.33), channel_id=1, source_target_pairs={{0,24},{8,16},{16,8},{24,0},{1,25},{9,17},{17,9},{25,1},{2,26},{10... | collective-permute-start | bytes 393224 | tf_op jit(solution)/shard_map/ppermute | solution.py:298
  45.3 1.5 %collective-permute-done.4.x1_ref = bf16[256,256]{1,0:T(8,128)(2,1)S(1)} collective-permute-done((bf16[256,256]{1,0:T(8,128)(2,1)S(1)}, bf16[256,256]{1,0:T(8,128)(2,1)S(1)}, u32[]{:S(2)}, u32[]{:S(2)}) %collective-permute-start.4) | collective-permute-done | bytes 131104 | tf_op jit(solution)/shard_map/ppermute | solution.py:298
  46.8 0.5 collective-permute-done.5.x2_ref
  47.3 1.5 %collective-permute-done.6.x3_ref = bf16[256,256]{1,0:T(8,128)(2,1)S(1)} collective-permute-done((bf16[256,256]{1,0:T(8,128)(2,1)S(1)}, bf16[256,256]{1,0:T(8,128)(2,1)S(1)}, u32[]{:S(2)}, u32[]{:S(2)}) %collective-permute-start.6) | collective-permute-done | bytes 131104 | tf_op jit(solution)/shard_map/ppermute | solution.py:298
  48.9 2.0 %collective-permute-done.10.late_ref = bf16[4,256,256]{2,1,0:T(8,128)(2,1)S(1)} collective-permute-done((bf16[4,256,256]{2,1,0:T(8,128)(2,1)S(1)}, bf16[4,256,256]{2,1,0:T(8,128)(2,1)S(1)}, u32[]{:S(2)}, u32[]{:S(2)}) %collective-permute-start.10) | collective-permute-done | bytes 524320 | tf_op jit(solution)/shard_map/ppermute | solution.py:292
  50.8 0.0 copy-done.1
  50.9 0.0 copy-done
  50.9 2.3 %transform.1 = f32[256,2,512]{2,1,0:T(2,128)} custom-call(s32[1]{0:T(128)} %bitcast.place_ref, bf16[256,256]{1,0:T(8,128)(2,1)S(1)} %get-tuple-element.30.x0_ref, bf16[256,256]{1,0:T(8,128)(2,1)S(1)} %collective-permute-done.4.x1_ref, bf16[256,256]{1,0:T(8,128)(2,1)S(1)} %collective-permute-done.5.x2_ref, ...), custom_call_target="tpu_custom_call" | custom-call | tf_op jit(solution)/shard_map/transform/pallas_call | solution.py:275
  (1 shorter events, 0.0 us)
Async XLA Ops:
  2.4 2.9 %collective-permute-start = (bf16[280,2048]{1,0:T(8,128)(2,1)S(1)}, bf16[280,2048]{1,0:T(8,128)(2,1)S(1)}, u32[]{:S(2)}, u32[]{:S(2)}) collective-permute-start(bf16[280,2048]{1,0:T(8,128)(2,1)S(1)} %prepare.1.columns_ref), channel_id=1, source_target_pairs={{0,1},{1,0},{2,3},{3,2},{4,5},{5,4},{6,7},{7,6},{8,9},{9,8},{10,11... | collective-permute-start | bytes 3440648 | tf_op jit(solution)/shard_map/ppermute | solution.py:295
  6.7 18.2 %collective-permute-start.3 = (bf16[2,280,512]{2,1,0:T(8,128)(2,1)S(1)}, bf16[2,280,512]{2,1,0:T(8,128)(2,1)}, u32[]{:S(2)}, u32[]{:S(2)}) collective-permute-start(bf16[2,280,512]{2,1,0:T(8,128)(2,1)S(1)} %sort_pairs.3.refs_0_), channel_id=1, source_target_pairs={{0,2},{1,3},{6,4},{7,5},{8,10},{9,11},{14,12},{15,13},{16,18},{17,... | collective-permute-start | bytes 1720328 | tf_op jit(solution)/shard_map/ppermute | solution.py:292
  12.4 26.1 %collective-permute-start.2 = (bf16[2,280,512]{2,1,0:T(8,128)(2,1)S(1)}, bf16[2,280,512]{2,1,0:T(8,128)(2,1)}, u32[]{:S(2)}, u32[]{:S(2)}) collective-permute-start(bf16[2,280,512]{2,1,0:T(8,128)(2,1)S(1)} %sort_pairs.3.refs_0_), channel_id=1, source_target_pairs={{2,4},{3,5},{4,2},{5,3},{10,12},{11,13},{12,10},{13,11},{18,20},{1... | collective-permute-start | bytes 1720328 | tf_op jit(solution)/shard_map/ppermute | solution.py:292
  16.1 24.8 %collective-permute-start.1 = (bf16[2,280,512]{2,1,0:T(8,128)(2,1)}, bf16[2,280,512]{2,1,0:T(8,128)(2,1)S(1)}, u32[]{:S(2)}, u32[]{:S(2)}) collective-permute-start(bf16[2,280,512]{2,1,0:T(8,128)(2,1)} %sort_pairs.4), channel_id=1, source_target_pairs={{0,4},{1,5},{6,2},{7,3},{2,0},{3,1},{4,6},{5,7},{8,12},{9,13},{14,... | collective-permute-start | bytes 1720328 | tf_op jit(solution)/shard_map/ppermute | solution.py:292
  26.8 6.4 %collective-permute-start.7 = (bf16[256,256]{1,0:T(8,128)(2,1)S(1)}, bf16[256,256]{1,0:T(8,128)(2,1)S(1)}, u32[]{:S(2)}, u32[]{:S(2)}) collective-permute-start(bf16[256,256]{1,0:T(8,128)(2,1)S(1)} %get-tuple-element.34), channel_id=1, source_target_pairs={{0,8},{8,0},{16,24},{24,16},{1,9},{9,1},{17,25},{25,17},{2,10},{10... | collective-permute-start | bytes 393224 | tf_op jit(solution)/shard_map/ppermute | solution.py:298
  28.3 6.0 %collective-permute-start.8 = (bf16[256,256]{1,0:T(8,128)(2,1)S(1)}, bf16[256,256]{1,0:T(8,128)(2,1)S(1)}, u32[]{:S(2)}, u32[]{:S(2)}) collective-permute-start(bf16[256,256]{1,0:T(8,128)(2,1)S(1)} %get-tuple-element.35), channel_id=1, source_target_pairs={{0,16},{8,24},{16,0},{24,8},{1,17},{9,25},{17,1},{25,9},{2,18},{10... | collective-permute-start | bytes 393224 | tf_op jit(solution)/shard_map/ppermute | solution.py:298
  29.9 5.9 %collective-permute-start.9 = (bf16[256,256]{1,0:T(8,128)(2,1)S(1)}, bf16[256,256]{1,0:T(8,128)(2,1)S(1)}, u32[]{:S(2)}, u32[]{:S(2)}) collective-permute-start(bf16[256,256]{1,0:T(8,128)(2,1)S(1)} %get-tuple-element.36), channel_id=1, source_target_pairs={{0,24},{8,16},{16,8},{24,0},{1,25},{9,17},{17,9},{25,1},{2,26},{10... | collective-permute-start | bytes 393224 | tf_op jit(solution)/shard_map/ppermute | solution.py:298
  35.8 15.0 %collective-permute-start.10 = (bf16[4,256,256]{2,1,0:T(8,128)(2,1)S(1)}, bf16[4,256,256]{2,1,0:T(8,128)(2,1)S(1)}, u32[]{:S(2)}, u32[]{:S(2)}) collective-permute-start(bf16[4,256,256]{2,1,0:T(8,128)(2,1)S(1)} %stack.1), channel_id=1, source_target_pairs={{0,2},{1,3},{6,4},{7,5},{2,6},{3,7},{4,0},{5,1},{8,10},{9,11},{14,... | collective-permute-start | bytes 1572872 | tf_op jit(solution)/shard_map/ppermute | solution.py:292
  38.5 12.4 %copy-start.1 = (bf16[4,256,512]{2,1,0:T(8,128)(2,1)S(1)}, bf16[4,256,512]{2,1,0:T(8,128)(2,1)}, u32[]{:S(2)}) copy-start(bf16[4,256,512]{2,1,0:T(8,128)(2,1)} %constant.12.clone.high_ref) | copy-start | bytes 3145732
  40.9 9.9 %copy-start = (bf16[4,256,512]{2,1,0:T(8,128)(2,1)S(1)}, bf16[4,256,512]{2,1,0:T(8,128)(2,1)}, u32[]{:S(2)}) copy-start(bf16[4,256,512]{2,1,0:T(8,128)(2,1)} %constant.13.clone.low_ref) | copy-start | bytes 3145732
  41.8 5.0 %collective-permute-start.4 = (bf16[256,256]{1,0:T(8,128)(2,1)S(1)}, bf16[256,256]{1,0:T(8,128)(2,1)S(1)}, u32[]{:S(2)}, u32[]{:S(2)}) collective-permute-start(bf16[256,256]{1,0:T(8,128)(2,1)S(1)} %get-tuple-element.31), channel_id=1, source_target_pairs={{0,8},{8,0},{16,24},{24,16},{1,9},{9,1},{17,25},{25,17},{2,10},{10... | collective-permute-start | bytes 393224 | tf_op jit(solution)/shard_map/ppermute | solution.py:298
  42.3 5.0 %collective-permute-start.5 = (bf16[256,256]{1,0:T(8,128)(2,1)S(1)}, bf16[256,256]{1,0:T(8,128)(2,1)S(1)}, u32[]{:S(2)}, u32[]{:S(2)}) collective-permute-start(bf16[256,256]{1,0:T(8,128)(2,1)S(1)} %get-tuple-element.32), channel_id=1, source_target_pairs={{0,16},{8,24},{16,0},{24,8},{1,17},{9,25},{17,1},{25,9},{2,18},{10... | collective-permute-start | bytes 393224 | tf_op jit(solution)/shard_map/ppermute | solution.py:298
  43.0 5.9 %collective-permute-start.6 = (bf16[256,256]{1,0:T(8,128)(2,1)S(1)}, bf16[256,256]{1,0:T(8,128)(2,1)S(1)}, u32[]{:S(2)}, u32[]{:S(2)}) collective-permute-start(bf16[256,256]{1,0:T(8,128)(2,1)S(1)} %get-tuple-element.33), channel_id=1, source_target_pairs={{0,24},{8,16},{16,8},{24,0},{1,25},{9,17},{17,9},{25,1},{2,26},{10... | collective-permute-start | bytes 393224 | tf_op jit(solution)/shard_map/ppermute | solution.py:298

commit v6 on v5

--- a/solution.py
+++ b/solution.py
@@ -272,11 +272,19 @@
 
 
 def transform(place, pieces, late, high, low):
+    cells, width = pieces[0].shape
+    half = cells // 2
+    piece = pl.BlockSpec((half, width), lambda i, p: (i, 0))
+    matrix = pl.BlockSpec(high.shape, lambda i, p: (0, 0, 0))
     return pl.pallas_call(
         transform_kernel,
-        in_specs=[SMEM_SPEC] + [VMEM_SPEC] * 7,
-        out_specs=VMEM_SPEC,
-        out_shape=jax.ShapeDtypeStruct((pieces[0].shape[0], 2, high.shape[2]), jnp.float32),
+        grid_spec=pltpu.PrefetchScalarGridSpec(
+            num_scalar_prefetch=1,
+            grid=(2,),
+            in_specs=[piece] * 4 + [pl.BlockSpec((4, half, width), lambda i, p: (0, i, 0)), matrix, matrix],
+            out_specs=pl.BlockSpec((half, 2, high.shape[2]), lambda i, p: (i, 0, 0)),
+        ),
+        out_shape=jax.ShapeDtypeStruct((cells, 2, high.shape[2]), jnp.float32),
         compiler_params=PARAMS,
         name="transform",
     )(place, *[on_chip(x) for x in (*pieces, late, high, low)])

time: 53.4 us -> 53.5 us (level)
  no operation moved by 1% of the time
where the time goes in v6:
time: 53.5 us; the launch traced here: 53.2 us
  waiting for transfers between devices  18.3 us (34%)
  starting transfers between devices  17.9 us (33%)
  Pallas kernels  17 us (32%)
    ppermute x4, starting transfers between devices, send(): lax.ppermute(block, 'uv', [(2 * a + c, 2 * b + (c ^ j)) for a, b in pairs...  10.3 us
    ppermute x6, waiting for transfers between devices, exchange(): lax.ppermute(pieces[d], 'chan', [(c, c ^ d) for c in range(4)])  8.96 us
    ppermute x6, starting transfers between devices, exchange(): lax.ppermute(pieces[d], 'chan', [(c, c ^ d) for c in range(4)])  7.11 us
    ppermute x4, waiting for transfers between devices, send(): lax.ppermute(block, 'uv', [(2 * a + c, 2 * b + (c ^ j)) for a, b in pairs...  6.89 us
    pallas_call x3, Pallas kernels, sort_pairs(): pl.pallas_call(kernel, in_specs=[SMEM_SPEC] + [VMEM_SPEC] * (2 + len(afte...  6.3 us
    pallas_call x2, Pallas kernels, grid_rows(): pl.pallas_call(kernel, in_specs=[VMEM_SPEC] * count, out_specs=VMEM_SPEC,...  3.23 us
    pallas_call x2, Pallas kernels, grid_pieces(): pl.pallas_call(kernel, in_specs=[SMEM_SPEC] + [VMEM_SPEC] * len(operands)...  2.69 us
    ppermute x1, waiting for transfers between devices, swap(): return lax.ppermute(block, 'uv', [(u, u ^ 1) for u in range(8)])  2.43 us
  transfers between devices with their start and end apart: 11, of which 9 were waited for; matrix products, arithmetic and copies ran while one was open for 0% of the time, Pallas kernels for 20%

profile of v6, /device:TPU:0, one launch (start us, length us, event | category | flops | bytes accessed | tf_op | source)
XLA Modules:
  0.0 53.2 jit_solution(9971031013453570118)
XLA Ops:
  0.0 2.3 %prepare.1.columns_ref = bf16[280,2048]{1,0:T(8,128)(2,1)S(1)} custom-call(s32[16,128]{1,0:T(8,128)} %bitcast.8, bf16[16,2048]{1,0:T(8,128)(2,1)} %bitcast.6, s32[2,2048]{1,0:T(2,128)} %bitcast.7, bf16[2048,2,128]{2,1,0:T(2,128)(2,1)} %vis_hbm.1), custom_call_target="tpu_custom_call" | custom-call | tf_op jit(solution)/shard_map/prepare/pallas_call | solution.py:119
  2.4 0.5 collective-permute-start
  2.9 2.4 %collective-permute-done.columns2_ref = bf16[280,2048]{1,0:T(8,128)(2,1)S(1)} collective-permute-done((bf16[280,2048]{1,0:T(8,128)(2,1)S(1)}, bf16[280,2048]{1,0:T(8,128)(2,1)S(1)}, u32[]{:S(2)}, u32[]{:S(2)}) %collective-permute-start) | collective-permute-done | bytes 1146912 | tf_op jit(solution)/shard_map/ppermute | solution.py:303
  5.3 1.4 %sort_pairs.3.refs_0_ = bf16[2,280,512]{2,1,0:T(8,128)(2,1)S(1)} custom-call(s32[1]{0:T(128)} %bitcast.1.uv_ref, bf16[280,2048]{1,0:T(8,128)(2,1)S(1)} %prepare.1.columns_ref, bf16[280,2048]{1,0:T(8,128)(2,1)S(1)} %collective-permute-done.columns2_ref), custom_call_target="tpu_custom_call" | custom-call | tf_op jit(solution)/shard_map/sort_pairs/pallas_call | solution.py:145
  6.7 5.7 %collective-permute-start.3 = (bf16[2,280,512]{2,1,0:T(8,128)(2,1)S(1)}, bf16[2,280,512]{2,1,0:T(8,128)(2,1)}, u32[]{:S(2)}, u32[]{:S(2)}) collective-permute-start(bf16[2,280,512]{2,1,0:T(8,128)(2,1)S(1)} %sort_pairs.3.refs_0_), channel_id=1, source_target_pairs={{0,2},{1,3},{6,4},{7,5},{8,10},{9,11},{14,12},{15,13},{16,18},{17,... | collective-permute-start | bytes 1720328 | tf_op jit(solution)/shard_map/ppermute | solution.py:300
  12.4 1.5 %collective-permute-start.2 = (bf16[2,280,512]{2,1,0:T(8,128)(2,1)S(1)}, bf16[2,280,512]{2,1,0:T(8,128)(2,1)}, u32[]{:S(2)}, u32[]{:S(2)}) collective-permute-start(bf16[2,280,512]{2,1,0:T(8,128)(2,1)S(1)} %sort_pairs.3.refs_0_), channel_id=1, source_target_pairs={{2,4},{3,5},{4,2},{5,3},{10,12},{11,13},{12,10},{13,11},{18,20},{1... | collective-permute-start | bytes 1720328 | tf_op jit(solution)/shard_map/ppermute | solution.py:300
  13.9 2.2 %sort_pairs.4 = bf16[2,280,512]{2,1,0:T(8,128)(2,1)} custom-call(s32[1]{0:T(128)} %bitcast.1.uv_ref, bf16[280,2048]{1,0:T(8,128)(2,1)S(1)} %prepare.1.columns_ref, bf16[280,2048]{1,0:T(8,128)(2,1)S(1)} %collective-permute-done.columns2_ref, bf16[2,280,512]{2,1,0:T(8,128)(2,1)S(1)} %sort_pairs.3.refs_0_), custom_call_target="tpu_custom_call" | custom-call | tf_op jit(solution)/shard_map/sort_pairs/pallas_call | solution.py:145
  16.1 0.5 collective-permute-start.1
  16.6 2.6 %sort_pairs.5 = (bf16[2,280,512]{2,1,0:T(8,128)(2,1)S(1)}, bf16[2,280,512]{2,1,0:T(8,128)(2,1)S(1)}) custom-call(s32[1]{0:T(128)} %bitcast.1.uv_ref, bf16[280,2048]{1,0:T(8,128)(2,1)S(1)} %prepare.1.columns_ref, bf16[280,2048]{1,0:T(8,128)(2,1)S(1)} %collective-permute-done.columns2_ref), custom_call_target="tpu_custom_call" | custom-call | tf_op jit(solution)/shard_map/sort_pairs/pallas_call | solution.py:145
  19.2 0.8 %grid_rows.2.refs_1_ = f32[1024,256]{1,0:T(8,128)S(1)} custom-call(bf16[2,280,512]{2,1,0:T(8,128)(2,1)S(1)} %get-tuple-element.22.refs_0_), custom_call_target="tpu_custom_call" | custom-call | tf_op jit(solution)/shard_map/grid_rows/pallas_call | solution.py:193
  20.0 4.9 %collective-permute-done.3.refs_0_ = bf16[2,280,512]{2,1,0:T(8,128)(2,1)} collective-permute-done((bf16[2,280,512]{2,1,0:T(8,128)(2,1)S(1)}, bf16[2,280,512]{2,1,0:T(8,128)(2,1)}, u32[]{:S(2)}, u32[]{:S(2)}) %collective-permute-start.3) | collective-permute-done | bytes 573472 | tf_op jit(solution)/shard_map/ppermute | solution.py:300
  24.9 1.9 %grid_pieces.2 = (bf16[256,256]{1,0:T(8,128)(2,1)S(1)}, bf16[256,256]{1,0:T(8,128)(2,1)S(1)}, bf16[256,256]{1,0:T(8,128)(2,1)S(1)}, bf16[256,256]{1,0:T(8,128)(2,1)S(1)}) custom-call(s32[1]{0:T(128)} %bitcast.place_ref, bf16[2,280,512]{2,1,0:T(8,128)(2,1)} %collective-permute-done.3.refs_0_, f32[1024,256]{1,0:T(8,128)S(1)} %grid_rows.2.refs_1_), custom_call_target="tpu_custom_call" | custom-call | tf_op jit(solution)/shard_map/grid_pieces/pallas_call | solution.py:220
  26.8 1.6 %collective-permute-start.7 = (bf16[256,256]{1,0:T(8,128)(2,1)S(1)}, bf16[256,256]{1,0:T(8,128)(2,1)S(1)}, u32[]{:S(2)}, u32[]{:S(2)}) collective-permute-start(bf16[256,256]{1,0:T(8,128)(2,1)S(1)} %get-tuple-element.34), channel_id=1, source_target_pairs={{0,8},{8,0},{16,24},{24,16},{1,9},{9,1},{17,25},{25,17},{2,10},{10... | collective-permute-start | bytes 393224 | tf_op jit(solution)/shard_map/ppermute | solution.py:306
  28.3 1.5 %collective-permute-start.8 = (bf16[256,256]{1,0:T(8,128)(2,1)S(1)}, bf16[256,256]{1,0:T(8,128)(2,1)S(1)}, u32[]{:S(2)}, u32[]{:S(2)}) collective-permute-start(bf16[256,256]{1,0:T(8,128)(2,1)S(1)} %get-tuple-element.35), channel_id=1, source_target_pairs={{0,16},{8,24},{16,0},{24,8},{1,17},{9,25},{17,1},{25,9},{2,18},{10... | collective-permute-start | bytes 393224 | tf_op jit(solution)/shard_map/ppermute | solution.py:306
  29.9 0.5 collective-permute-start.9
  30.3 2.8 %collective-permute-done.7.refs_1_ = bf16[256,256]{1,0:T(8,128)(2,1)S(1)} collective-permute-done((bf16[256,256]{1,0:T(8,128)(2,1)S(1)}, bf16[256,256]{1,0:T(8,128)(2,1)S(1)}, u32[]{:S(2)}, u32[]{:S(2)}) %collective-permute-start.7) | collective-permute-done | bytes 131104 | tf_op jit(solution)/shard_map/ppermute | solution.py:306
  33.1 1.2 %collective-permute-done.8.refs_2_ = bf16[256,256]{1,0:T(8,128)(2,1)S(1)} collective-permute-done((bf16[256,256]{1,0:T(8,128)(2,1)S(1)}, bf16[256,256]{1,0:T(8,128)(2,1)S(1)}, u32[]{:S(2)}, u32[]{:S(2)}) %collective-permute-start.8) | collective-permute-done | bytes 131104 | tf_op jit(solution)/shard_map/ppermute | solution.py:306
  34.4 1.4 %collective-permute-done.9.refs_3_ = bf16[256,256]{1,0:T(8,128)(2,1)S(1)} collective-permute-done((bf16[256,256]{1,0:T(8,128)(2,1)S(1)}, bf16[256,256]{1,0:T(8,128)(2,1)S(1)}, u32[]{:S(2)}, u32[]{:S(2)}) %collective-permute-start.9) | collective-permute-done | bytes 131104 | tf_op jit(solution)/shard_map/ppermute | solution.py:306
  35.8 2.6 %collective-permute-start.10 = (bf16[4,256,256]{2,1,0:T(8,128)(2,1)S(1)}, bf16[4,256,256]{2,1,0:T(8,128)(2,1)S(1)}, u32[]{:S(2)}, u32[]{:S(2)}) collective-permute-start(bf16[4,256,256]{2,1,0:T(8,128)(2,1)S(1)} %stack.1), channel_id=1, source_target_pairs={{0,2},{1,3},{6,4},{7,5},{2,6},{3,7},{4,0},{5,1},{8,10},{9,11},{14,... | collective-permute-start | bytes 1572872 | tf_op jit(solution)/shard_map/ppermute | solution.py:300
  38.5 0.0 collective-permute-done.2.refs_1_
  38.5 0.0 copy-start.1
  38.5 2.5 %grid_rows.3.refs_1_ = f32[1024,256]{1,0:T(8,128)S(1)} custom-call(bf16[2,280,512]{2,1,0:T(8,128)(2,1)S(1)} %get-tuple-element.26.refs_0_, bf16[2,280,512]{2,1,0:T(8,128)(2,1)} %collective-permute-done.2.refs_1_), custom_call_target="tpu_custom_call" | custom-call | tf_op jit(solution)/shard_map/grid_rows/pallas_call | solution.py:193
  40.9 0.0 copy-start
  40.9 0.0 collective-permute-done.1.refs_0_
  41.0 0.8 %grid_pieces.3 = (bf16[256,256]{1,0:T(8,128)(2,1)S(1)}, bf16[256,256]{1,0:T(8,128)(2,1)S(1)}, bf16[256,256]{1,0:T(8,128)(2,1)S(1)}, bf16[256,256]{1,0:T(8,128)(2,1)S(1)}) custom-call(s32[1]{0:T(128)} %bitcast.place_ref, bf16[2,280,512]{2,1,0:T(8,128)(2,1)S(1)} %collective-permute-done.1.refs_0_, f32[1024,256]{1,0:T(8,128)S(1)} %grid_rows.3.refs_1_), custom_call_target="tpu_custom_call" | custom-call | tf_op jit(solution)/shard_map/grid_pieces/pallas_call | solution.py:220
  41.8 0.6 %collective-permute-start.4 = (bf16[256,256]{1,0:T(8,128)(2,1)S(1)}, bf16[256,256]{1,0:T(8,128)(2,1)S(1)}, u32[]{:S(2)}, u32[]{:S(2)}) collective-permute-start(bf16[256,256]{1,0:T(8,128)(2,1)S(1)} %get-tuple-element.31), channel_id=1, source_target_pairs={{0,8},{8,0},{16,24},{24,16},{1,9},{9,1},{17,25},{25,17},{2,10},{10... | collective-permute-start | bytes 393224 | tf_op jit(solution)/shard_map/ppermute | solution.py:306
  42.3 0.7 %collective-permute-start.5 = (bf16[256,256]{1,0:T(8,128)(2,1)S(1)}, bf16[256,256]{1,0:T(8,128)(2,1)S(1)}, u32[]{:S(2)}, u32[]{:S(2)}) collective-permute-start(bf16[256,256]{1,0:T(8,128)(2,1)S(1)} %get-tuple-element.32), channel_id=1, source_target_pairs={{0,16},{8,24},{16,0},{24,8},{1,17},{9,25},{17,1},{25,9},{2,18},{10... | collective-permute-start | bytes 393224 | tf_op jit(solution)/shard_map/ppermute | solution.py:306
  43.0 2.3 %collective-permute-start.6 = (bf16[256,256]{1,0:T(8,128)(2,1)S(1)}, bf16[256,256]{1,0:T(8,128)(2,1)S(1)}, u32[]{:S(2)}, u32[]{:S(2)}) collective-permute-start(bf16[256,256]{1,0:T(8,128)(2,1)S(1)} %get-tuple-element.33), channel_id=1, source_target_pairs={{0,24},{8,16},{16,8},{24,0},{1,25},{9,17},{17,9},{25,1},{2,26},{10... | collective-permute-start | bytes 393224 | tf_op jit(solution)/shard_map/ppermute | solution.py:306
  45.3 1.5 %collective-permute-done.4.x1_ref = bf16[256,256]{1,0:T(8,128)(2,1)S(1)} collective-permute-done((bf16[256,256]{1,0:T(8,128)(2,1)S(1)}, bf16[256,256]{1,0:T(8,128)(2,1)S(1)}, u32[]{:S(2)}, u32[]{:S(2)}) %collective-permute-start.4) | collective-permute-done | bytes 131104 | tf_op jit(solution)/shard_map/ppermute | solution.py:306
  46.8 0.5 collective-permute-done.5.x2_ref
  47.3 1.5 %collective-permute-done.6.x3_ref = bf16[256,256]{1,0:T(8,128)(2,1)S(1)} collective-permute-done((bf16[256,256]{1,0:T(8,128)(2,1)S(1)}, bf16[256,256]{1,0:T(8,128)(2,1)S(1)}, u32[]{:S(2)}, u32[]{:S(2)}) %collective-permute-start.6) | collective-permute-done | bytes 131104 | tf_op jit(solution)/shard_map/ppermute | solution.py:306
  48.9 2.0 %collective-permute-done.10.late_ref = bf16[4,256,256]{2,1,0:T(8,128)(2,1)S(1)} collective-permute-done((bf16[4,256,256]{2,1,0:T(8,128)(2,1)S(1)}, bf16[4,256,256]{2,1,0:T(8,128)(2,1)S(1)}, u32[]{:S(2)}, u32[]{:S(2)}) %collective-permute-start.10) | collective-permute-done | bytes 524320 | tf_op jit(solution)/shard_map/ppermute | solution.py:300
  50.8 0.0 copy-done.1
  50.9 0.0 copy-done
  50.9 2.4 %transform.1 = f32[256,2,512]{2,1,0:T(2,128)} custom-call(s32[1]{0:T(128)} %bitcast.place_ref, bf16[256,256]{1,0:T(8,128)(2,1)S(1)} %get-tuple-element.30.x0_ref, bf16[256,256]{1,0:T(8,128)(2,1)S(1)} %collective-permute-done.4.x1_ref, bf16[256,256]{1,0:T(8,128)(2,1)S(1)} %collective-permute-done.5.x2_ref, ...), custom_call_target="tpu_custom_call" | custom-call | tf_op jit(solution)/shard_map/transform/pallas_call | solution.py:279
  (1 shorter events, 0.0 us)
Async XLA Ops:
  2.4 2.9 %collective-permute-start = (bf16[280,2048]{1,0:T(8,128)(2,1)S(1)}, bf16[280,2048]{1,0:T(8,128)(2,1)S(1)}, u32[]{:S(2)}, u32[]{:S(2)}) collective-permute-start(bf16[280,2048]{1,0:T(8,128)(2,1)S(1)} %prepare.1.columns_ref), channel_id=1, source_target_pairs={{0,1},{1,0},{2,3},{3,2},{4,5},{5,4},{6,7},{7,6},{8,9},{9,8},{10,11... | collective-permute-start | bytes 3440648 | tf_op jit(solution)/shard_map/ppermute | solution.py:303
  6.7 18.2 %collective-permute-start.3 = (bf16[2,280,512]{2,1,0:T(8,128)(2,1)S(1)}, bf16[2,280,512]{2,1,0:T(8,128)(2,1)}, u32[]{:S(2)}, u32[]{:S(2)}) collective-permute-start(bf16[2,280,512]{2,1,0:T(8,128)(2,1)S(1)} %sort_pairs.3.refs_0_), channel_id=1, source_target_pairs={{0,2},{1,3},{6,4},{7,5},{8,10},{9,11},{14,12},{15,13},{16,18},{17,... | collective-permute-start | bytes 1720328 | tf_op jit(solution)/shard_map/ppermute | solution.py:300
  12.4 26.1 %collective-permute-start.2 = (bf16[2,280,512]{2,1,0:T(8,128)(2,1)S(1)}, bf16[2,280,512]{2,1,0:T(8,128)(2,1)}, u32[]{:S(2)}, u32[]{:S(2)}) collective-permute-start(bf16[2,280,512]{2,1,0:T(8,128)(2,1)S(1)} %sort_pairs.3.refs_0_), channel_id=1, source_target_pairs={{2,4},{3,5},{4,2},{5,3},{10,12},{11,13},{12,10},{13,11},{18,20},{1... | collective-permute-start | bytes 1720328 | tf_op jit(solution)/shard_map/ppermute | solution.py:300
  16.1 24.8 %collective-permute-start.1 = (bf16[2,280,512]{2,1,0:T(8,128)(2,1)}, bf16[2,280,512]{2,1,0:T(8,128)(2,1)S(1)}, u32[]{:S(2)}, u32[]{:S(2)}) collective-permute-start(bf16[2,280,512]{2,1,0:T(8,128)(2,1)} %sort_pairs.4), channel_id=1, source_target_pairs={{0,4},{1,5},{6,2},{7,3},{2,0},{3,1},{4,6},{5,7},{8,12},{9,13},{14,... | collective-permute-start | bytes 1720328 | tf_op jit(solution)/shard_map/ppermute | solution.py:300
  26.8 6.4 %collective-permute-start.7 = (bf16[256,256]{1,0:T(8,128)(2,1)S(1)}, bf16[256,256]{1,0:T(8,128)(2,1)S(1)}, u32[]{:S(2)}, u32[]{:S(2)}) collective-permute-start(bf16[256,256]{1,0:T(8,128)(2,1)S(1)} %get-tuple-element.34), channel_id=1, source_target_pairs={{0,8},{8,0},{16,24},{24,16},{1,9},{9,1},{17,25},{25,17},{2,10},{10... | collective-permute-start | bytes 393224 | tf_op jit(solution)/shard_map/ppermute | solution.py:306
  28.3 6.0 %collective-permute-start.8 = (bf16[256,256]{1,0:T(8,128)(2,1)S(1)}, bf16[256,256]{1,0:T(8,128)(2,1)S(1)}, u32[]{:S(2)}, u32[]{:S(2)}) collective-permute-start(bf16[256,256]{1,0:T(8,128)(2,1)S(1)} %get-tuple-element.35), channel_id=1, source_target_pairs={{0,16},{8,24},{16,0},{24,8},{1,17},{9,25},{17,1},{25,9},{2,18},{10... | collective-permute-start | bytes 393224 | tf_op jit(solution)/shard_map/ppermute | solution.py:306
  29.9 5.9 %collective-permute-start.9 = (bf16[256,256]{1,0:T(8,128)(2,1)S(1)}, bf16[256,256]{1,0:T(8,128)(2,1)S(1)}, u32[]{:S(2)}, u32[]{:S(2)}) collective-permute-start(bf16[256,256]{1,0:T(8,128)(2,1)S(1)} %get-tuple-element.36), channel_id=1, source_target_pairs={{0,24},{8,16},{16,8},{24,0},{1,25},{9,17},{17,9},{25,1},{2,26},{10... | collective-permute-start | bytes 393224 | tf_op jit(solution)/shard_map/ppermute | solution.py:306
  35.8 15.0 %collective-permute-start.10 = (bf16[4,256,256]{2,1,0:T(8,128)(2,1)S(1)}, bf16[4,256,256]{2,1,0:T(8,128)(2,1)S(1)}, u32[]{:S(2)}, u32[]{:S(2)}) collective-permute-start(bf16[4,256,256]{2,1,0:T(8,128)(2,1)S(1)} %stack.1), channel_id=1, source_target_pairs={{0,2},{1,3},{6,4},{7,5},{2,6},{3,7},{4,0},{5,1},{8,10},{9,11},{14,... | collective-permute-start | bytes 1572872 | tf_op jit(solution)/shard_map/ppermute | solution.py:300
  38.5 12.4 %copy-start.1 = (bf16[4,256,512]{2,1,0:T(8,128)(2,1)S(1)}, bf16[4,256,512]{2,1,0:T(8,128)(2,1)}, u32[]{:S(2)}) copy-start(bf16[4,256,512]{2,1,0:T(8,128)(2,1)} %constant.12.clone.high_ref) | copy-start | bytes 3145732
  40.9 9.9 %copy-start = (bf16[4,256,512]{2,1,0:T(8,128)(2,1)S(1)}, bf16[4,256,512]{2,1,0:T(8,128)(2,1)}, u32[]{:S(2)}) copy-start(bf16[4,256,512]{2,1,0:T(8,128)(2,1)} %constant.13.clone.low_ref) | copy-start | bytes 3145732
  41.8 5.0 %collective-permute-start.4 = (bf16[256,256]{1,0:T(8,128)(2,1)S(1)}, bf16[256,256]{1,0:T(8,128)(2,1)S(1)}, u32[]{:S(2)}, u32[]{:S(2)}) collective-permute-start(bf16[256,256]{1,0:T(8,128)(2,1)S(1)} %get-tuple-element.31), channel_id=1, source_target_pairs={{0,8},{8,0},{16,24},{24,16},{1,9},{9,1},{17,25},{25,17},{2,10},{10... | collective-permute-start | bytes 393224 | tf_op jit(solution)/shard_map/ppermute | solution.py:306
  42.3 5.0 %collective-permute-start.5 = (bf16[256,256]{1,0:T(8,128)(2,1)S(1)}, bf16[256,256]{1,0:T(8,128)(2,1)S(1)}, u32[]{:S(2)}, u32[]{:S(2)}) collective-permute-start(bf16[256,256]{1,0:T(8,128)(2,1)S(1)} %get-tuple-element.32), channel_id=1, source_target_pairs={{0,16},{8,24},{16,0},{24,8},{1,17},{9,25},{17,1},{25,9},{2,18},{10... | collective-permute-start | bytes 393224 | tf_op jit(solution)/shard_map/ppermute | solution.py:306
  43.0 5.9 %collective-permute-start.6 = (bf16[256,256]{1,0:T(8,128)(2,1)S(1)}, bf16[256,256]{1,0:T(8,128)(2,1)S(1)}, u32[]{:S(2)}, u32[]{:S(2)}) collective-permute-start(bf16[256,256]{1,0:T(8,128)(2,1)S(1)} %get-tuple-element.33), channel_id=1, source_target_pairs={{0,24},{8,16},{16,8},{24,0},{1,25},{9,17},{17,9},{25,1},{2,26},{10... | collective-permute-start | bytes 393224 | tf_op jit(solution)/shard_map/ppermute | solution.py:306
